TPU v7x, 256 devices: a whole 4x4x8 slice. The times are simulated.
256 devices in a mesh: pa: 64 (over y, z, x_hi), gz: 4 (over x_lo, core).
Axes of the slice: x: 4 (x_hi: 2, x_lo: 2; x = x_hi * 2 + x_lo), y: 4, z: 8, core: 2. Of those that a mesh axis runs over, the one named last changes fastest.
Arguments:
- volume: float32 [128, 512, 256], P('gz', 'pa'), may hold values from -5.5 to 5.5
Outputs:
- dip_inline: float32 [128, 512, 256], P('gz', 'pa')
- dip_cross: float32 [128, 512, 256], P('gz', 'pa')
- coherence: float32 [128, 512, 256], P('gz', 'pa')
All inputs are finite; a program needn't handle non-finite values.
Results may differ from a plain program's by a relative error of at most 0.000054.
Values sent between devices are 32-bit elements; how exact they have to be, the bound alone decides.
No kernel may reach another device: no remote copies, remote signals or barrier semaphores. Data moves between devices by JAX's collectives and lax.ppermute only.
A program may use at most 64 MiB of HBM per device.

v0:
```python
import functools
import math

import jax
import jax.numpy as jnp
import numpy as np
from jax import lax
from jax.experimental import pallas as pl
from jax.experimental.pallas import tpu as pltpu
from jax.sharding import PartitionSpec as P

HALF = 24
GHALF = 6
SIGMA_GRADIENT = 1.5
DECAY_LENGTH = 4.0
EPSILON = 1e-06

REACH = HALF + GHALF
DECAY = math.exp(-1.0 / DECAY_LENGTH)
CUT = math.exp(-(HALF + 1) / DECAY_LENGTH)
BF16 = jnp.bfloat16
F32 = jnp.float32


def gradient_taps():
    k = np.arange(-GHALF, GHALF + 1).astype(np.float64)
    bell = np.exp(-k * k / (2.0 * SIGMA_GRADIENT**2))
    smooth = bell / np.sqrt(np.sum(bell * bell))
    slope = k * bell / np.sqrt(np.sum((k * bell) ** 2))
    return smooth, slope


def average_scale():
    k = np.arange(-HALF, HALF + 1).astype(np.float64)
    return 1.0 / np.sum(np.exp(-np.abs(k) / DECAY_LENGTH))


SMOOTH, SLOPE = gradient_taps()


def split_constant(matrix):
    matrix = matrix.astype(np.float32)
    high = matrix.astype(BF16)
    low = (matrix - high.astype(np.float32)).astype(BF16)
    return high, low


def inline_matrix(taps, length):
    reach = (len(taps) - 1) // 2
    offset = np.arange(length)[:, None] - np.arange(length)[None, :]
    inside = np.abs(offset) <= reach
    return np.where(inside, taps[np.clip(offset + reach, 0, 2 * reach)], 0.0)


def average_matrix(length):
    offset = np.abs(np.arange(length)[:, None] - np.arange(length)[None, :])
    values = np.exp(-offset / DECAY_LENGTH) * average_scale() ** 3
    return np.where(offset <= HALF, values, 0.0)


def depth_matrix(planes, halo):
    position = np.concatenate(
        [np.arange(planes), np.arange(-halo, 0), np.arange(planes, planes + halo)]
    )
    offset = position[None, :] - np.arange(planes)[:, None]
    inside = np.abs(offset) <= GHALF
    index = np.clip(offset + GHALF, 0, 2 * GHALF)
    return np.concatenate(
        [np.where(inside, SMOOTH[index], 0.0), np.where(inside, SLOPE[index], 0.0)], axis=0
    )


def split(x):
    high = x.astype(BF16)
    low = (x - high.astype(F32)).astype(BF16)
    return high, low


def dot(a, b):
    return jnp.dot(a, b, preferred_element_type=F32)


def dot3(x, w_high, w_low):
    high, low = split(x)
    return dot(high, w_high) + (dot(high, w_low) + dot(low, w_high))


def symmetric_pair(load, centre, reach, smooth, slope):
    mid = load(centre)
    total = None if smooth is None else smooth[reach] * mid
    tilt = None
    for k in range(1, reach + 1):
        after, before = load(centre + k), load(centre - k)
        if smooth is not None:
            total = total + smooth[reach + k] * (after + before)
        if slope is not None:
            term = slope[reach + k] * (after - before)
            tilt = term if tilt is None else tilt + term
    return total, tilt


def tensor_kernel(
    rows, total_rows, planes, width, halo,
    where_ref, own, other, above, below, far, near_far, up, down,
    wz_stack, wd_high, wd_low, wg_high, wg_low, ws_high, ws_low,
    out, out_last, out_first,
    zg, zd, gx, gy, gz, pre, part, ty,
):
    device = where_ref[0]
    odd = lax.rem(device, 2)
    toward = (1 - 2 * odd) * rows
    outer = rows + 2 * HALF
    smooth = [float(v) for v in SMOOTH]
    slope = [float(v) for v in SLOPE]
    trim = 4 * rows - REACH
    pieces = [
        (own, 0, rows, 0, REACH),
        (other, 0, rows, rows, REACH + toward),
        (above, 0, rows, 2 * rows, REACH - 2 * rows),
        (above, rows, rows, 3 * rows, REACH - 2 * rows + toward),
        (below, 0, rows, 4 * rows, REACH + 2 * rows),
        (below, rows, rows, 5 * rows, REACH + 2 * rows + toward),
        (far, 0, rows - trim, 6 * rows, odd * (REACH + 4 * rows)),
        (far, rows - trim, rows, 7 * rows - trim,
         (1 - odd) * (REACH - 3 * rows) + odd * (REACH + 3 * rows)),
        (near_far, 0, rows - trim, 8 * rows - trim, (1 - odd) * (REACH + 4 * rows)),
    ]
    for ref, first, count, place, base in pieces:

        def depth_row(i, carry, ref=ref, first=first, place=place, base=base):
            x = jnp.concatenate([ref[first + i], up[place + i], down[place + i]], axis=0)
            high, low = split(x)
            stacked = dot(wz_stack[...], high)
            result = stacked[: 2 * planes] + (
                stacked[2 * planes :] + dot(wz_stack[0 : 2 * planes, :], low)
            )
            zg[base + i] = result[:planes]
            zd[base + i] = result[planes:]
            return carry

        lax.fori_loop(0, count, depth_row, 0, unroll=2)

    group = 8
    for start in range(0, outer, group):

        def cross_row(r, carry, start=start):
            centre = start + r + GHALF
            position = device * rows + (start + r - HALF)
            inside = jnp.logical_and(position >= 0, position < total_rows).astype(F32)
            for z in range(0, planes, 8):
                both = symmetric_pair(
                    lambda j, z=z: zg[j, z : z + 8, :], centre, GHALF, smooth, slope
                )
                third, _ = symmetric_pair(
                    lambda j, z=z: zd[j, z : z + 8, :], centre, GHALF, smooth, None
                )
                at = pl.multiple_of(r * planes + z, 8)
                pre[0, pl.ds(at, 8), :] = both[0] * inside
                pre[1, pl.ds(at, 8), :] = both[1] * inside
                pre[2, pl.ds(at, 8), :] = third * inside
            return carry

        lax.fori_loop(0, group, cross_row, 0)
        shape = (group, planes, width)
        gx[start : start + group] = dot3(pre[0], wd_high[...], wd_low[...]).reshape(shape)
        gy[start : start + group] = dot3(pre[1], wg_high[...], wg_low[...]).reshape(shape)
        gz[start : start + group] = dot3(pre[2], wg_high[...], wg_low[...]).reshape(shape)

    def products(j, at, lanes):
        x, y, z = (ref[j, pl.ds(at, 8), lanes] for ref in (gx, gy, gz))
        return [x * x, y * y, z * z, x * y, x * z, y * z]

    for lane in range(0, width, 128):
        lanes = slice(lane, lane + 128)

        def average_rows(t, carry, lane=lane, lanes=lanes):
            at = pl.multiple_of(t * 8, 8)
            state = products(0, at, lanes)
            for j in range(1, HALF + 1):
                state = [DECAY * s + v for s, v in zip(state, products(j, at, lanes))]
            for f in range(6):
                part[f, 0] = state[f]
            for i in range(1, rows):
                new, old = products(HALF + i, at, lanes), products(i - 1, at, lanes)
                state = [DECAY * s + (v - CUT * w) for s, v, w in zip(state, new, old)]
                for f in range(6):
                    part[f, i] = state[f]
            state = [DECAY * v for v in products(outer - 1, at, lanes)]
            for j in range(outer - 2, HALF + rows - 1, -1):
                state = [DECAY * (s + v) for s, v in zip(state, products(j, at, lanes))]
            for i in range(rows - 1, -1, -1):
                for f in range(6):
                    ty[lane // 128, f, pl.ds(t * 8 * rows + i, 8, stride=rows), :] = part[f, i] + state[f]
                if i:
                    near, far_row = products(HALF + i, at, lanes), products(2 * HALF + i, at, lanes)
                    state = [
                        DECAY * (s + v) - CUT * w for s, v, w in zip(state, near, far_row)
                    ]
            return carry

        lax.fori_loop(0, planes // 8, average_rows, 0)

    for f in range(6):
        held = jnp.concatenate([ty[h, f] for h in range(width // 128)], axis=1)
        field = dot3(held, ws_high[...], ws_low[...]).reshape(planes, rows, width)
        out[:, f] = field
        out_last[:, f] = field[planes - HALF :]
        out_first[:, f] = field[:HALF]


def attribute_kernel(planes, rows, width, own, above, below, inline, cross, coherent, part):
    for lane in range(0, width, 128):
        lanes = slice(lane, lane + 128)

        def plane(z):
            if z < 0:
                return [above[HALF + z, f, :, lanes] for f in range(6)]
            if z >= planes:
                return [below[z - planes, f, :, lanes] for f in range(6)]
            return [own[z, f, :, lanes] for f in range(6)]

        state = plane(-HALF)
        for z in range(-HALF + 1, 1):
            state = [DECAY * s + v for s, v in zip(state, plane(z))]
        for f in range(6):
            part[0, f] = state[f]
        for z in range(1, planes):
            new, old = plane(z), plane(z - HALF - 1)
            state = [DECAY * s + (v - CUT * w) for s, v, w in zip(state, new, old)]
            for f in range(6):
                part[z, f] = state[f]
        state = [DECAY * v for v in plane(planes + HALF - 1)]
        for z in range(planes + HALF - 2, planes - 1, -1):
            state = [DECAY * (s + v) for s, v in zip(state, plane(z))]
        for z in range(planes - 1, -1, -1):
            xx, yy, zz, xy, xz, yz = [part[z, f] + state[f] for f in range(6)]
            scale = -1.0 / (zz + EPSILON)
            inline[z, :, lanes] = xz * scale
            cross[z, :, lanes] = yz * scale
            trace = xx + yy + zz
            minors = xx * yy + xx * zz + yy * zz - xy * xy - xz * xz - yz * yz
            coherent[z, :, lanes] = 1.0 - 3.0 * minors / (trace * trace + EPSILON)
            if z:
                near, far_plane = plane(z), plane(z + HALF)
                state = [DECAY * (s + v) - CUT * w for s, v, w in zip(state, near, far_plane)]


def send(x, axis, target):
    devices = lax.axis_size(axis)
    pairs = [(i, target(i)) for i in range(devices) if 0 <= target(i) < devices]
    return lax.ppermute(x, axis, pairs)


def local(volume):
    planes, rows, width = volume.shape
    groups = lax.axis_size("pa")
    device = lax.axis_index("pa")
    even = lax.rem(device, 2) == 0
    trim = 4 * rows - REACH
    halo = 8
    own = volume.transpose(1, 0, 2)
    other = send(own, "pa", lambda i: i ^ 1)
    pair = jnp.concatenate([own, other], axis=0)
    above = send(pair, "pa", lambda i: i + 2)
    below = send(pair, "pa", lambda i: i - 2)
    onward = jnp.where(
        even,
        above[trim:],
        jnp.concatenate([below[: rows - trim], below[rows:]], axis=0),
    )
    back = jnp.where(even, below[: rows - trim], above[trim:rows])
    far = send(onward, "pa", lambda i: i + 2 if i % 2 == 0 else i - 2)
    near_far = send(back, "pa", lambda i: i - 2 if i % 2 == 0 else i + 2)
    held = [pair, above, below, far, near_far]
    up = send(jnp.concatenate([x[:, planes - halo :] for x in held], axis=0), "gz", lambda i: i + 1)
    down = send(jnp.concatenate([x[:, :halo] for x in held], axis=0), "gz", lambda i: i - 1)

    wz_high, wz_low = split_constant(depth_matrix(planes, halo))
    weights = [jnp.asarray(np.concatenate([wz_high, wz_low], axis=0))]
    for matrix in (
        inline_matrix(SLOPE, width), inline_matrix(SMOOTH, width), average_matrix(width)
    ):
        weights += [jnp.asarray(w) for w in split_constant(matrix)]

    outer = rows + 2 * HALF
    whole = pl.BlockSpec(memory_space=pltpu.VMEM)
    tensors, last, first = pl.pallas_call(
        functools.partial(tensor_kernel, rows, rows * groups, planes, width, halo),
        out_shape=[
            jax.ShapeDtypeStruct((planes, 6, rows, width), F32),
            jax.ShapeDtypeStruct((HALF, 6, rows, width), F32),
            jax.ShapeDtypeStruct((HALF, 6, rows, width), F32),
        ],
        in_specs=[pl.BlockSpec(memory_space=pltpu.SMEM)] + [whole] * (8 + len(weights)),
        out_specs=[whole] * 3,
        scratch_shapes=[
            pltpu.VMEM((rows + 2 * REACH, planes, width), F32),
            pltpu.VMEM((rows + 2 * REACH, planes, width), F32),
            pltpu.VMEM((outer, planes, width), F32),
            pltpu.VMEM((outer, planes, width), F32),
            pltpu.VMEM((outer, planes, width), F32),
            pltpu.VMEM((3, 8 * planes, width), F32),
            pltpu.VMEM((6, rows, 8, 128), F32),
            pltpu.VMEM((width // 128, 6, planes * rows, 128), F32),
        ],
        compiler_params=pltpu.CompilerParams(vmem_limit_bytes=40 * 2**20),
        name="tensor",
    )(device.reshape(1), own, other, above, below, far, near_far, up, down, *weights)

    from_above = send(last, "gz", lambda i: i + 1)
    from_below = send(first, "gz", lambda i: i - 1)
    shape = jax.ShapeDtypeStruct((planes, rows, width), F32)
    return tuple(
        pl.pallas_call(
            functools.partial(attribute_kernel, planes, rows, width),
            out_shape=[shape] * 3,
            in_specs=[whole] * 3,
            out_specs=[whole] * 3,
            scratch_shapes=[pltpu.VMEM((planes, 6, 8, 128), F32)],
            compiler_params=pltpu.CompilerParams(vmem_limit_bytes=32 * 2**20),
            name="attributes",
        )(tensors, from_above, from_below)
    )


def solution(mesh):
    placed = P("gz", "pa", None)
    return jax.shard_map(
        local,
        mesh=mesh,
        in_specs=(placed,),
        out_specs=(placed, placed, placed),
        check_vma=False,
    )
```

profile of v0, /device:TPU:25, one launch (start us, length us, event | category | flops | bytes accessed | tf_op | source)
XLA Modules:
  0.0 104.6 jit_solution(5651191962185399677)
XLA Ops:
  0.6 1.0 copy.13
  1.7 2.8 %collective-permute-start = (f32[8,32,256]{2,1,0:T(8,128)S(1)}, f32[8,32,256]{2,1,0:T(8,128)S(1)}, u32[]{:S(2)}, u32[]{:S(2)}) collective-permute-start(f32[8,32,256]{2,1,0:T(8,128)S(1)} %bitcast.4), channel_id=1, source_target_pairs={{0,4},{4,0},{8,12},{12,8},{16,20},{20,16},{24,28},{28,24},{32,36},... | collective-permute-start | bytes 786440 | tf_op jit(solution)/shard_map/ppermute | solution.py:251
  4.5 5.9 %collective-permute-done.other = f32[8,32,256]{2,1,0:T(8,128)S(1)} collective-permute-done((f32[8,32,256]{2,1,0:T(8,128)S(1)}, f32[8,32,256]{2,1,0:T(8,128)S(1)}, u32[]{:S(2)}, u32[]{:S(2)}) %collective-permute-start) | collective-permute-done | bytes 262176 | tf_op jit(solution)/shard_map/ppermute | solution.py:251
  10.5 7.7 %collective-permute-start.2 = (f32[16,32,256]{2,1,0:T(8,128)S(1)}, f32[16,32,256]{2,1,0:T(8,128)S(1)}, u32[]{:S(2)}, u32[]{:S(2)}) collective-permute-start(f32[16,32,256]{2,1,0:T(8,128)S(1)} %pad_maximum_fusion), channel_id=1, source_target_pairs={{8,0},{12,4},{16,8},{20,12},{24,16},{28,20},{32,24},{36,28},{40,32... | collective-permute-start | bytes 1572872 | tf_op jit(solution)/shard_map/ppermute | solution.py:251
  18.1 1.9 %collective-permute-start.1 = (f32[16,32,256]{2,1,0:T(8,128)S(1)}, f32[16,32,256]{2,1,0:T(8,128)S(1)}, u32[]{:S(2)}, u32[]{:S(2)}) collective-permute-start(f32[16,32,256]{2,1,0:T(8,128)S(1)} %pad_maximum_fusion), channel_id=1, source_target_pairs={{0,8},{4,12},{8,16},{12,20},{16,24},{20,28},{24,32},{28,36},{32,40... | collective-permute-start | bytes 1572872 | tf_op jit(solution)/shard_map/ppermute | solution.py:251
  20.1 7.7 %collective-permute-done.2.below = f32[16,32,256]{2,1,0:T(8,128)S(1)} collective-permute-done((f32[16,32,256]{2,1,0:T(8,128)S(1)}, f32[16,32,256]{2,1,0:T(8,128)S(1)}, u32[]{:S(2)}, u32[]{:S(2)}) %collective-permute-start.2) | collective-permute-done | bytes 524320 | tf_op jit(solution)/shard_map/ppermute | solution.py:251
  27.8 5.9 %collective-permute-done.1.above = f32[16,32,256]{2,1,0:T(8,128)S(1)} collective-permute-done((f32[16,32,256]{2,1,0:T(8,128)S(1)}, f32[16,32,256]{2,1,0:T(8,128)S(1)}, u32[]{:S(2)}, u32[]{:S(2)}) %collective-permute-start.1) | collective-permute-done | bytes 524320 | tf_op jit(solution)/shard_map/ppermute | solution.py:251
  33.8 1.9 %collective-permute-start.4 = (f32[6,32,256]{2,1,0:T(8,128)S(1)}, f32[6,32,256]{2,1,0:T(8,128)S(1)}, u32[]{:S(2)}, u32[]{:S(2)}) collective-permute-start(f32[6,32,256]{2,1,0:T(8,128)S(1)} %get-tuple-element.15), channel_id=1, source_target_pairs={{4,12},{8,0},{12,20},{16,8},{20,28},{24,16},{28,36},{32,24},{36,44... | collective-permute-start | bytes 589832 | tf_op jit(solution)/shard_map/ppermute | solution.py:251
  35.7 0.1 slice_select_fusion
  35.8 0.0 copy-start
  35.8 0.0 copy-start.1
  35.8 0.0 copy-start.2
  35.8 0.0 copy-start.3
  35.9 0.0 copy-start.4
  35.9 0.0 copy-start.5
  35.9 0.0 copy-start.6
  35.9 3.5 %collective-permute-start.3 = (f32[14,32,256]{2,1,0:T(8,128)S(1)}, f32[14,32,256]{2,1,0:T(8,128)S(1)}, u32[]{:S(2)}, u32[]{:S(2)}) collective-permute-start(f32[14,32,256]{2,1,0:T(8,128)S(1)} %slice_select_fusion), channel_id=1, source_target_pairs={{0,8},{8,16},{12,4},{16,24},{20,12},{24,32},{28,20},{32,40},{36,28... | collective-permute-start | bytes 1376264 | tf_op jit(solution)/shard_map/ppermute | solution.py:251
  39.4 9.8 %collective-permute-done.3.far = f32[14,32,256]{2,1,0:T(8,128)S(1)} collective-permute-done((f32[14,32,256]{2,1,0:T(8,128)S(1)}, f32[14,32,256]{2,1,0:T(8,128)S(1)}, u32[]{:S(2)}, u32[]{:S(2)}) %collective-permute-start.3) | collective-permute-done | bytes 458784 | tf_op jit(solution)/shard_map/ppermute | solution.py:251
  49.3 0.0 collective-permute-done.4.near_far
  49.3 5.6 %collective-permute-start.6 = (f32[68,8,256]{2,1,0:T(8,128)S(1)}, f32[68,8,256]{2,1,0:T(8,128)S(1)}, u32[]{:S(2)}, u32[]{:S(2)}) collective-permute-start(f32[68,8,256]{2,1,0:T(8,128)S(1)} %get-tuple-element.19), channel_id=1, source_target_pairs={{1,0},{2,1},{3,2},{5,4},{6,5},{7,6},{9,8},{10,9},{11,10},{13,12},{... | collective-permute-start | bytes 1671176 | tf_op jit(solution)/shard_map/ppermute | solution.py:251
  54.9 3.0 %collective-permute-start.5 = (f32[68,8,256]{2,1,0:T(8,128)S(1)}, f32[68,8,256]{2,1,0:T(8,128)S(1)}, u32[]{:S(2)}, u32[]{:S(2)}) collective-permute-start(f32[68,8,256]{2,1,0:T(8,128)S(1)} %get-tuple-element.20), channel_id=1, source_target_pairs={{0,1},{1,2},{2,3},{4,5},{5,6},{6,7},{8,9},{9,10},{10,11},{12,13},{... | collective-permute-start | bytes 1671176 | tf_op jit(solution)/shard_map/ppermute | solution.py:251
  58.0 5.3 %collective-permute-done.6.down = f32[68,8,256]{2,1,0:T(8,128)S(1)} collective-permute-done((f32[68,8,256]{2,1,0:T(8,128)S(1)}, f32[68,8,256]{2,1,0:T(8,128)S(1)}, u32[]{:S(2)}, u32[]{:S(2)}) %collective-permute-start.6) | collective-permute-done | bytes 557088 | tf_op jit(solution)/shard_map/ppermute | solution.py:251
  63.2 1.2 %collective-permute-done.5.up = f32[68,8,256]{2,1,0:T(8,128)S(1)} collective-permute-done((f32[68,8,256]{2,1,0:T(8,128)S(1)}, f32[68,8,256]{2,1,0:T(8,128)S(1)}, u32[]{:S(2)}, u32[]{:S(2)}) %collective-permute-start.5) | collective-permute-done | bytes 557088 | tf_op jit(solution)/shard_map/ppermute | solution.py:251
  64.4 0.0 copy-done
  64.4 0.0 copy-done.1
  64.4 0.0 copy-done.2
  64.4 0.0 copy-done.3
  64.4 0.0 copy-done.4
  64.4 0.0 copy-done.5
  64.4 0.0 copy-done.6
  64.4 16.5 %tensor.1 = (f32[32,6,8,256]{3,2,1,0:T(8,128)S(1)}, f32[24,6,8,256]{3,2,1,0:T(8,128)S(1)}, f32[24,6,8,256]{3,2,1,0:T(8,128)S(1)}) custom-call(s32[1]{0:T(128)} %bitcast.where_ref, f32[8,32,256]{2,1,0:T(8,128)S(1)} %bitcast.7, f32[8,32,256]{2,1,0:T(8,128)S(1)} %collective-permute-done.other, f32[16,32,256]{2,1,0:T(8,128)S(1)} %collective-permute-done.1.above, ...), custom_call_target="tpu_custom_call" | custom-call | tf_op jit(solution)/shard_map/tensor/pallas_call | solution.py:287
  81.0 4.4 %collective-permute-start.7 = (f32[24,6,8,256]{3,2,1,0:T(8,128)S(1)}, f32[24,6,8,256]{3,2,1,0:T(8,128)S(1)}, u32[]{:S(2)}, u32[]{:S(2)}) collective-permute-start(f32[24,6,8,256]{3,2,1,0:T(8,128)S(1)} %get-tuple-element.7), channel_id=1, source_target_pairs={{0,1},{1,2},{2,3},{4,5},{5,6},{6,7},{8,9},{9,10},{10,11},{12,13},{... | collective-permute-start | bytes 3538952 | tf_op jit(solution)/shard_map/ppermute | solution.py:251
  85.4 1.9 %collective-permute-start.8 = (f32[24,6,8,256]{3,2,1,0:T(8,128)S(1)}, f32[24,6,8,256]{3,2,1,0:T(8,128)S(1)}, u32[]{:S(2)}, u32[]{:S(2)}) collective-permute-start(f32[24,6,8,256]{3,2,1,0:T(8,128)S(1)} %get-tuple-element.8), channel_id=1, source_target_pairs={{1,0},{2,1},{3,2},{5,4},{6,5},{7,6},{9,8},{10,9},{11,10},{13,12},{... | collective-permute-start | bytes 3538952 | tf_op jit(solution)/shard_map/ppermute | solution.py:251
  87.3 11.2 %collective-permute-done.7.above = f32[24,6,8,256]{3,2,1,0:T(8,128)S(1)} collective-permute-done((f32[24,6,8,256]{3,2,1,0:T(8,128)S(1)}, f32[24,6,8,256]{3,2,1,0:T(8,128)S(1)}, u32[]{:S(2)}, u32[]{:S(2)}) %collective-permute-start.7) | collective-permute-done | bytes 1179680 | tf_op jit(solution)/shard_map/ppermute | solution.py:251
  98.5 4.4 %collective-permute-done.8.below = f32[24,6,8,256]{3,2,1,0:T(8,128)S(1)} collective-permute-done((f32[24,6,8,256]{3,2,1,0:T(8,128)S(1)}, f32[24,6,8,256]{3,2,1,0:T(8,128)S(1)}, u32[]{:S(2)}, u32[]{:S(2)}) %collective-permute-start.8) | collective-permute-done | bytes 1179680 | tf_op jit(solution)/shard_map/ppermute | solution.py:251
  102.9 1.7 %attributes.1 = (f32[32,8,256]{2,1,0:T(8,128)}, f32[32,8,256]{2,1,0:T(8,128)}, f32[32,8,256]{2,1,0:T(8,128)}) custom-call(f32[32,6,8,256]{3,2,1,0:T(8,128)S(1)} %get-tuple-element.6.own, f32[24,6,8,256]{3,2,1,0:T(8,128)S(1)} %collective-permute-done.7.above, f32[24,6,8,256]{3,2,1,0:T(8,128)S(1)} %collective-permute-done.8.below), custom_call_target="tpu_custom_call" | custom-call | tf_op jit(solution)/shard_map/attributes/pallas_call | solution.py:314
  (8 shorter events, 0.2 us)
Async XLA Ops:
  1.7 8.8 %collective-permute-start = (f32[8,32,256]{2,1,0:T(8,128)S(1)}, f32[8,32,256]{2,1,0:T(8,128)S(1)}, u32[]{:S(2)}, u32[]{:S(2)}) collective-permute-start(f32[8,32,256]{2,1,0:T(8,128)S(1)} %bitcast.4), channel_id=1, source_target_pairs={{0,4},{4,0},{8,12},{12,8},{16,20},{20,16},{24,28},{28,24},{32,36},... | collective-permute-start | bytes 786440 | tf_op jit(solution)/shard_map/ppermute | solution.py:251
  10.5 17.3 %collective-permute-start.2 = (f32[16,32,256]{2,1,0:T(8,128)S(1)}, f32[16,32,256]{2,1,0:T(8,128)S(1)}, u32[]{:S(2)}, u32[]{:S(2)}) collective-permute-start(f32[16,32,256]{2,1,0:T(8,128)S(1)} %pad_maximum_fusion), channel_id=1, source_target_pairs={{8,0},{12,4},{16,8},{20,12},{24,16},{28,20},{32,24},{36,28},{40,32... | collective-permute-start | bytes 1572872 | tf_op jit(solution)/shard_map/ppermute | solution.py:251
  18.1 15.6 %collective-permute-start.1 = (f32[16,32,256]{2,1,0:T(8,128)S(1)}, f32[16,32,256]{2,1,0:T(8,128)S(1)}, u32[]{:S(2)}, u32[]{:S(2)}) collective-permute-start(f32[16,32,256]{2,1,0:T(8,128)S(1)} %pad_maximum_fusion), channel_id=1, source_target_pairs={{0,8},{4,12},{8,16},{12,20},{16,24},{20,28},{24,32},{28,36},{32,40... | collective-permute-start | bytes 1572872 | tf_op jit(solution)/shard_map/ppermute | solution.py:251
  33.8 15.5 %collective-permute-start.4 = (f32[6,32,256]{2,1,0:T(8,128)S(1)}, f32[6,32,256]{2,1,0:T(8,128)S(1)}, u32[]{:S(2)}, u32[]{:S(2)}) collective-permute-start(f32[6,32,256]{2,1,0:T(8,128)S(1)} %get-tuple-element.15), channel_id=1, source_target_pairs={{4,12},{8,0},{12,20},{16,8},{20,28},{24,16},{28,36},{32,24},{36,44... | collective-permute-start | bytes 589832 | tf_op jit(solution)/shard_map/ppermute | solution.py:251
  35.8 28.6 %copy-start = (bf16[256,256]{1,0:T(8,128)(2,1)S(1)}, bf16[256,256]{1,0:T(8,128)(2,1)}, u32[]{:S(2)}) copy-start(bf16[256,256]{1,0:T(8,128)(2,1)} %constant.32.clone.ws_low) | copy-start | bytes 393220
  35.8 28.6 %copy-start.1 = (bf16[256,256]{1,0:T(8,128)(2,1)S(1)}, bf16[256,256]{1,0:T(8,128)(2,1)}, u32[]{:S(2)}) copy-start(bf16[256,256]{1,0:T(8,128)(2,1)} %constant.31.clone.ws_high) | copy-start | bytes 393220
  35.8 28.6 %copy-start.2 = (bf16[256,256]{1,0:T(8,128)(2,1)S(1)}, bf16[256,256]{1,0:T(8,128)(2,1)}, u32[]{:S(2)}) copy-start(bf16[256,256]{1,0:T(8,128)(2,1)} %constant.30.clone.wg_low) | copy-start | bytes 393220
  35.8 28.6 %copy-start.3 = (bf16[256,256]{1,0:T(8,128)(2,1)S(1)}, bf16[256,256]{1,0:T(8,128)(2,1)}, u32[]{:S(2)}) copy-start(bf16[256,256]{1,0:T(8,128)(2,1)} %constant.29.clone.wg_high) | copy-start | bytes 393220
  35.9 28.6 %copy-start.4 = (bf16[256,256]{1,0:T(8,128)(2,1)S(1)}, bf16[256,256]{1,0:T(8,128)(2,1)}, u32[]{:S(2)}) copy-start(bf16[256,256]{1,0:T(8,128)(2,1)} %constant.28.clone.wd_low) | copy-start | bytes 393220
  35.9 28.6 %copy-start.5 = (bf16[256,256]{1,0:T(8,128)(2,1)S(1)}, bf16[256,256]{1,0:T(8,128)(2,1)}, u32[]{:S(2)}) copy-start(bf16[256,256]{1,0:T(8,128)(2,1)} %constant.27.clone.wd_high) | copy-start | bytes 393220
  35.9 28.6 %copy-start.6 = (bf16[128,48]{1,0:T(8,128)(2,1)S(1)}, bf16[128,48]{1,0:T(8,128)(2,1)}, u32[]{:S(2)}) copy-start(bf16[128,48]{1,0:T(8,128)(2,1)} %constant.26.clone.wz_stack) | copy-start | bytes 36868
  35.9 13.4 %collective-permute-start.3 = (f32[14,32,256]{2,1,0:T(8,128)S(1)}, f32[14,32,256]{2,1,0:T(8,128)S(1)}, u32[]{:S(2)}, u32[]{:S(2)}) collective-permute-start(f32[14,32,256]{2,1,0:T(8,128)S(1)} %slice_select_fusion), channel_id=1, source_target_pairs={{0,8},{8,16},{12,4},{16,24},{20,12},{24,32},{28,20},{32,40},{36,28... | collective-permute-start | bytes 1376264 | tf_op jit(solution)/shard_map/ppermute | solution.py:251
  49.3 13.9 %collective-permute-start.6 = (f32[68,8,256]{2,1,0:T(8,128)S(1)}, f32[68,8,256]{2,1,0:T(8,128)S(1)}, u32[]{:S(2)}, u32[]{:S(2)}) collective-permute-start(f32[68,8,256]{2,1,0:T(8,128)S(1)} %get-tuple-element.19), channel_id=1, source_target_pairs={{1,0},{2,1},{3,2},{5,4},{6,5},{7,6},{9,8},{10,9},{11,10},{13,12},{... | collective-permute-start | bytes 1671176 | tf_op jit(solution)/shard_map/ppermute | solution.py:251
  54.9 9.5 %collective-permute-start.5 = (f32[68,8,256]{2,1,0:T(8,128)S(1)}, f32[68,8,256]{2,1,0:T(8,128)S(1)}, u32[]{:S(2)}, u32[]{:S(2)}) collective-permute-start(f32[68,8,256]{2,1,0:T(8,128)S(1)} %get-tuple-element.20), channel_id=1, source_target_pairs={{0,1},{1,2},{2,3},{4,5},{5,6},{6,7},{8,9},{9,10},{10,11},{12,13},{... | collective-permute-start | bytes 1671176 | tf_op jit(solution)/shard_map/ppermute | solution.py:251
  81.0 17.5 %collective-permute-start.7 = (f32[24,6,8,256]{3,2,1,0:T(8,128)S(1)}, f32[24,6,8,256]{3,2,1,0:T(8,128)S(1)}, u32[]{:S(2)}, u32[]{:S(2)}) collective-permute-start(f32[24,6,8,256]{3,2,1,0:T(8,128)S(1)} %get-tuple-element.7), channel_id=1, source_target_pairs={{0,1},{1,2},{2,3},{4,5},{5,6},{6,7},{8,9},{9,10},{10,11},{12,13},{... | collective-permute-start | bytes 3538952 | tf_op jit(solution)/shard_map/ppermute | solution.py:251
  85.4 17.5 %collective-permute-start.8 = (f32[24,6,8,256]{3,2,1,0:T(8,128)S(1)}, f32[24,6,8,256]{3,2,1,0:T(8,128)S(1)}, u32[]{:S(2)}, u32[]{:S(2)}) collective-permute-start(f32[24,6,8,256]{3,2,1,0:T(8,128)S(1)} %get-tuple-element.8), channel_id=1, source_target_pairs={{1,0},{2,1},{3,2},{5,4},{6,5},{7,6},{9,8},{10,9},{11,10},{13,12},{... | collective-permute-start | bytes 3538952 | tf_op jit(solution)/shard_map/ppermute | solution.py:251
where the time goes:
time: 105 us
  waiting for transfers between devices  51.5 us (49%)
  starting transfers between devices  32.7 us (31%)
  Pallas kernels  18.2 us (17%)
  local copies, waits for them, and re-layouts  1.17 us (1%)
    ppermute x9, waiting for transfers between devices, send(): return lax.ppermute(x, axis, pairs)  51.5 us
    ppermute x9, starting transfers between devices, send(): return lax.ppermute(x, axis, pairs)  32.7 us
    pallas_call x1, Pallas kernels, local(): pl.pallas_call(functools.partial(tensor_kernel, rows, rows * groups, plan...  16.5 us
  transfers between devices with their start and end apart: 9, of which 8 were waited for; matrix products, arithmetic and copies ran while one was open for 0% of the time, Pallas kernels for 0%

commit v1 on v0

--- a/solution.py
+++ b/solution.py
@@ -100,12 +100,16 @@
 
 
 def tensor_kernel(
-    rows, total_rows, planes, width, halo,
-    where_ref, own, other, above, below, far, near_far, up, down,
-    wz_stack, wd_high, wd_low, wg_high, wg_low, ws_high, ws_low,
-    out, out_last, out_first,
-    zg, zd, gx, gy, gz, pre, part, ty,
+    rows, total_rows, tiles, width, halos, *refs
 ):
+    where_ref, own, other, above, below, above_other, below_other, above_far, below_far, last_far = refs[:10]
+    if halos:
+        up, down = refs[10:12]
+        refs = refs[2:]
+    wz_stack, wd_high, wd_low, wg_high, wg_low, ws_high, ws_low = refs[10:17]
+    outs = refs[17 : 17 + (2 if halos else 1)]
+    zg, zd, gx, gy, gz, pre, part, ty = refs[-8:]
+    planes = 8 * tiles
     device = where_ref[0]
     odd = lax.rem(device, 2)
     toward = (1 - 2 * odd) * rows
@@ -117,18 +121,19 @@
         (own, 0, rows, 0, REACH),
         (other, 0, rows, rows, REACH + toward),
         (above, 0, rows, 2 * rows, REACH - 2 * rows),
-        (above, rows, rows, 3 * rows, REACH - 2 * rows + toward),
-        (below, 0, rows, 4 * rows, REACH + 2 * rows),
-        (below, rows, rows, 5 * rows, REACH + 2 * rows + toward),
-        (far, 0, rows - trim, 6 * rows, odd * (REACH + 4 * rows)),
-        (far, rows - trim, rows, 7 * rows - trim,
-         (1 - odd) * (REACH - 3 * rows) + odd * (REACH + 3 * rows)),
-        (near_far, 0, rows - trim, 8 * rows - trim, (1 - odd) * (REACH + 4 * rows)),
+        (below, 0, rows, 3 * rows, REACH + 2 * rows),
+        (above_other, 0, rows, 4 * rows, REACH - 2 * rows + toward),
+        (below_other, 0, rows, 5 * rows, REACH + 2 * rows + toward),
+        (above_far, trim, rows - trim, 6 * rows, 0),
+        (below_far, 0, rows - trim, 7 * rows - trim, REACH + 4 * rows),
+        (last_far, 0, rows, 8 * rows - 2 * trim, REACH - 3 * rows * (1 - 2 * odd)),
     ]
     for ref, first, count, place, base in pieces:
 
         def depth_row(i, carry, ref=ref, first=first, place=place, base=base):
-            x = jnp.concatenate([ref[first + i], up[place + i], down[place + i]], axis=0)
+            x = ref[first + i]
+            if halos:
+                x = jnp.concatenate([x, up[place + i], down[place + i]], axis=0)
             high, low = split(x)
             stacked = dot(wz_stack[...], high)
             result = stacked[: 2 * planes] + (
@@ -203,21 +208,20 @@
     for f in range(6):
         held = jnp.concatenate([ty[h, f] for h in range(width // 128)], axis=1)
         field = dot3(held, ws_high[...], ws_low[...]).reshape(planes, rows, width)
-        out[:, f] = field
-        out_last[:, f] = field[planes - HALF :]
-        out_first[:, f] = field[:HALF]
-
-
-def attribute_kernel(planes, rows, width, own, above, below, inline, cross, coherent, part):
+        step = planes // len(outs)
+        for n, out in enumerate(outs):
+            out[:, f] = field[n * step : (n + 1) * step]
+
+
+def attribute_kernel(planes, width, pieces, *refs):
+    inline, cross, coherent, part = refs[-4:]
     for lane in range(0, width, 128):
         lanes = slice(lane, lane + 128)
 
         def plane(z):
-            if z < 0:
-                return [above[HALF + z, f, :, lanes] for f in range(6)]
-            if z >= planes:
-                return [below[z - planes, f, :, lanes] for f in range(6)]
-            return [own[z, f, :, lanes] for f in range(6)]
+            for ref, start in zip(refs, pieces):
+                if start <= z < start + ref.shape[0]:
+                    return [ref[z - start, f, :, lanes] for f in range(6)]
 
         state = plane(-HALF)
         for z in range(-HALF + 1, 1):
@@ -259,67 +263,80 @@
     trim = 4 * rows - REACH
     halo = 8
     own = volume.transpose(1, 0, 2)
+    above = send(own, "pa", lambda i: i + 2)
+    below = send(own, "pa", lambda i: i - 2)
     other = send(own, "pa", lambda i: i ^ 1)
-    pair = jnp.concatenate([own, other], axis=0)
-    above = send(pair, "pa", lambda i: i + 2)
-    below = send(pair, "pa", lambda i: i - 2)
-    onward = jnp.where(
-        even,
-        above[trim:],
-        jnp.concatenate([below[: rows - trim], below[rows:]], axis=0),
-    )
-    back = jnp.where(even, below[: rows - trim], above[trim:rows])
-    far = send(onward, "pa", lambda i: i + 2 if i % 2 == 0 else i - 2)
-    near_far = send(back, "pa", lambda i: i - 2 if i % 2 == 0 else i + 2)
-    held = [pair, above, below, far, near_far]
+    above_far = send(above, "pa", lambda i: i + 2)
+    below_far = send(below, "pa", lambda i: i - 2)
+    above_other = send(other, "pa", lambda i: i + 2)
+    below_other = send(other, "pa", lambda i: i - 2)
+    last_far = send(jnp.where(even, below_far, above_far), "pa", lambda i: i ^ 1)
+    pieces = [own, other, above, below, above_other, below_other, above_far, below_far, last_far]
+    held = pieces[:6] + [above_far[trim:], below_far[: rows - trim], last_far]
     up = send(jnp.concatenate([x[:, planes - halo :] for x in held], axis=0), "gz", lambda i: i + 1)
     down = send(jnp.concatenate([x[:, :halo] for x in held], axis=0), "gz", lambda i: i - 1)
 
-    wz_high, wz_low = split_constant(depth_matrix(planes, halo))
-    weights = [jnp.asarray(np.concatenate([wz_high, wz_low], axis=0))]
+    weights = []
     for matrix in (
         inline_matrix(SLOPE, width), inline_matrix(SMOOTH, width), average_matrix(width)
     ):
         weights += [jnp.asarray(w) for w in split_constant(matrix)]
-
-    outer = rows + 2 * HALF
+    matrix = depth_matrix(planes, halo)
+    index = np.arange(planes)
+    inner = np.logical_and(index >= halo, index < planes - halo)
+
+    def tensors(chosen, halos, name):
+        used = int(np.sum(chosen))
+        columns = matrix.shape[1] if halos else planes
+        part = matrix[np.concatenate([chosen, chosen])][:, :columns]
+        stack = jnp.asarray(np.concatenate(split_constant(part), axis=0))
+        outer = rows + 2 * HALF
+        outs = 2 if halos else 1
+        operands = pieces + (list(halos) if halos else []) + [stack] + weights
+        return pl.pallas_call(
+            functools.partial(
+                tensor_kernel, rows, rows * groups, used // 8, width, bool(halos)
+            ),
+            out_shape=[jax.ShapeDtypeStruct((used // outs, 6, rows, width), F32)] * outs,
+            in_specs=[pl.BlockSpec(memory_space=pltpu.SMEM)] + [whole] * len(operands),
+            out_specs=[whole] * outs,
+            scratch_shapes=[
+                pltpu.VMEM((rows + 2 * REACH, used, width), F32),
+                pltpu.VMEM((rows + 2 * REACH, used, width), F32),
+                pltpu.VMEM((outer, used, width), F32),
+                pltpu.VMEM((outer, used, width), F32),
+                pltpu.VMEM((outer, used, width), F32),
+                pltpu.VMEM((3, 8 * used, width), F32),
+                pltpu.VMEM((6, rows, 8, 128), F32),
+                pltpu.VMEM((width // 128, 6, used * rows, 128), F32),
+            ],
+            compiler_params=pltpu.CompilerParams(vmem_limit_bytes=28 * 2**20),
+            cost_estimate=pl.CostEstimate(
+                flops=8 * 10**9, bytes_accessed=4 * 2**20, transcendentals=0
+            ),
+            name=name,
+        )(device.reshape(1), *operands)
+
     whole = pl.BlockSpec(memory_space=pltpu.VMEM)
-    tensors, last, first = pl.pallas_call(
-        functools.partial(tensor_kernel, rows, rows * groups, planes, width, halo),
-        out_shape=[
-            jax.ShapeDtypeStruct((planes, 6, rows, width), F32),
-            jax.ShapeDtypeStruct((HALF, 6, rows, width), F32),
-            jax.ShapeDtypeStruct((HALF, 6, rows, width), F32),
-        ],
-        in_specs=[pl.BlockSpec(memory_space=pltpu.SMEM)] + [whole] * (8 + len(weights)),
-        out_specs=[whole] * 3,
-        scratch_shapes=[
-            pltpu.VMEM((rows + 2 * REACH, planes, width), F32),
-            pltpu.VMEM((rows + 2 * REACH, planes, width), F32),
-            pltpu.VMEM((outer, planes, width), F32),
-            pltpu.VMEM((outer, planes, width), F32),
-            pltpu.VMEM((outer, planes, width), F32),
-            pltpu.VMEM((3, 8 * planes, width), F32),
-            pltpu.VMEM((6, rows, 8, 128), F32),
-            pltpu.VMEM((width // 128, 6, planes * rows, 128), F32),
-        ],
-        compiler_params=pltpu.CompilerParams(vmem_limit_bytes=40 * 2**20),
-        name="tensor",
-    )(device.reshape(1), own, other, above, below, far, near_far, up, down, *weights)
-
-    from_above = send(last, "gz", lambda i: i + 1)
-    from_below = send(first, "gz", lambda i: i - 1)
+    (middle,) = tensors(inner, None, "tensor_middle")
+    middle_above = send(middle, "gz", lambda i: i + 1)
+    middle_below = send(middle, "gz", lambda i: i - 1)
+    first, last = tensors(~inner, (up, down), "tensor_ends")
+    last_above = send(last, "gz", lambda i: i + 1)
+    first_below = send(first, "gz", lambda i: i - 1)
+    arrays = [middle_above, last_above, first, middle, last, first_below, middle_below]
+    starts = [-HALF, -halo, 0, halo, planes - halo, planes, planes + halo]
     shape = jax.ShapeDtypeStruct((planes, rows, width), F32)
     return tuple(
         pl.pallas_call(
-            functools.partial(attribute_kernel, planes, rows, width),
+            functools.partial(attribute_kernel, planes, width, starts),
             out_shape=[shape] * 3,
-            in_specs=[whole] * 3,
+            in_specs=[whole] * len(arrays),
             out_specs=[whole] * 3,
             scratch_shapes=[pltpu.VMEM((planes, 6, 8, 128), F32)],
-            compiler_params=pltpu.CompilerParams(vmem_limit_bytes=32 * 2**20),
+            compiler_params=pltpu.CompilerParams(vmem_limit_bytes=28 * 2**20),
             name="attributes",
-        )(tensors, from_above, from_below)
+        )(*arrays)
     )
 
 

time: 105 us -> 89.6 us (0.85)
  waiting for transfers between devices: 51.5 us -> 15.2 us
  starting transfers between devices: 32.7 us -> 46.9 us
  Pallas kernels: 18.2 us -> 24.8 us
    ppermute x9 -> x14, waiting for transfers between devices: 51.5 us -> 15.2 us  [send(): return lax.ppermute(x, axis, pairs)]
    ppermute x9 -> x14, starting transfers between devices: 32.7 us -> 46.9 us  [send(): return lax.ppermute(x, axis, pairs)]
    pallas_call x2 -> x3, Pallas kernels: 18.2 us -> 24.8 us  [the longest x2 23.1 us: tensors(): pl.pallas_call(functools.partial(tensor_kernel, rows, rows * groups, used...]
  transfers between devices with their start and end apart: 9 -> 14, of which waited for: 8 -> 5; matrix products, arithmetic and copies ran while one was open for 0% -> 0% of each run, Pallas kernels for 0% -> 26%
where the time goes in v1:
time: 89.6 us; the launch traced here: 89.2 us
  starting transfers between devices  46.9 us (52%)
  Pallas kernels  24.8 us (28%)
  waiting for transfers between devices  15.2 us (17%)
  local copies, waits for them, and re-layouts  1.19 us (1%)
  between operations  0.99 us (1%)
    ppermute x14, starting transfers between devices, send(): return lax.ppermute(x, axis, pairs)  46.9 us
    pallas_call x2, Pallas kernels, tensors(): pl.pallas_call(functools.partial(tensor_kernel, rows, rows * groups, used...  23.1 us
    ppermute x14, waiting for transfers between devices, send(): return lax.ppermute(x, axis, pairs)  15.2 us
  transfers between devices with their start and end apart: 14, of which 5 were waited for; matrix products, arithmetic and copies ran while one was open for 0% of the time, Pallas kernels for 26%

profile of v1, /device:TPU:25, one launch (start us, length us, event | category | flops | bytes accessed | tf_op | source)
XLA Modules:
  0.0 89.2 jit_solution(7389104487347176757)
XLA Ops:
  0.6 1.0 %copy.14 = f32[32,8,256]{2,0,1:T(8,128)S(1)} copy(f32[32,8,256]{2,1,0:T(8,128)} %param.9) | data formatting | bytes 524288 | tf_op args[0]
  1.7 2.8 %collective-permute-start = (f32[8,32,256]{2,1,0:T(8,128)S(1)}, f32[8,32,256]{2,1,0:T(8,128)S(1)}, u32[]{:S(2)}, u32[]{:S(2)}) collective-permute-start(f32[8,32,256]{2,1,0:T(8,128)S(1)} %bitcast.4), channel_id=1, source_target_pairs={{0,4},{4,0},{8,12},{12,8},{16,20},{20,16},{24,28},{28,24},{32,36},... | collective-permute-start | bytes 786440 | tf_op jit(solution)/shard_map/ppermute | solution.py:255
  4.5 3.5 %collective-permute-start.1 = (f32[8,32,256]{2,1,0:T(8,128)S(1)}, f32[8,32,256]{2,1,0:T(8,128)S(1)}, u32[]{:S(2)}, u32[]{:S(2)}) collective-permute-start(f32[8,32,256]{2,1,0:T(8,128)S(1)} %bitcast.5), channel_id=1, source_target_pairs={{0,8},{4,12},{8,16},{12,20},{16,24},{20,28},{24,32},{28,36},{32,40... | collective-permute-start | bytes 786440 | tf_op jit(solution)/shard_map/ppermute | solution.py:255
  8.0 6.0 %collective-permute-start.2 = (f32[8,32,256]{2,1,0:T(8,128)S(1)}, f32[8,32,256]{2,1,0:T(8,128)S(1)}, u32[]{:S(2)}, u32[]{:S(2)}) collective-permute-start(f32[8,32,256]{2,1,0:T(8,128)S(1)} %bitcast.6), channel_id=1, source_target_pairs={{8,0},{12,4},{16,8},{20,12},{24,16},{28,20},{32,24},{36,28},{40,32... | collective-permute-start | bytes 786440 | tf_op jit(solution)/shard_map/ppermute | solution.py:255
  14.1 0.0 collective-permute-done.refs_2_
  14.1 1.9 %collective-permute-start.3 = (f32[8,32,256]{2,1,0:T(8,128)S(1)}, f32[8,32,256]{2,1,0:T(8,128)S(1)}, u32[]{:S(2)}, u32[]{:S(2)}) collective-permute-start(f32[8,32,256]{2,1,0:T(8,128)S(1)} %collective-permute-done.refs_2_), channel_id=1, source_target_pairs={{0,8},{4,12},{8,16},{12,20},{16,24},{20,28},{24,32},{28,36},{32,40... | collective-permute-start | bytes 786440 | tf_op jit(solution)/shard_map/ppermute | solution.py:255
  16.1 5.5 %collective-permute-start.4 = (f32[8,32,256]{2,1,0:T(8,128)S(1)}, f32[8,32,256]{2,1,0:T(8,128)S(1)}, u32[]{:S(2)}, u32[]{:S(2)}) collective-permute-start(f32[8,32,256]{2,1,0:T(8,128)S(1)} %collective-permute-done.refs_2_), channel_id=1, source_target_pairs={{8,0},{12,4},{16,8},{20,12},{24,16},{28,20},{32,24},{36,28},{40,32... | collective-permute-start | bytes 786440 | tf_op jit(solution)/shard_map/ppermute | solution.py:255
  21.5 0.0 collective-permute-done.1.refs_3_
  21.5 1.9 %collective-permute-start.5 = (f32[8,32,256]{2,1,0:T(8,128)S(1)}, f32[8,32,256]{2,1,0:T(8,128)S(1)}, u32[]{:S(2)}, u32[]{:S(2)}) collective-permute-start(f32[8,32,256]{2,1,0:T(8,128)S(1)} %collective-permute-done.1.refs_3_), channel_id=1, source_target_pairs={{0,8},{4,12},{8,16},{12,20},{16,24},{20,28},{24,32},{28,36},{32,40... | collective-permute-start | bytes 786440 | tf_op jit(solution)/shard_map/ppermute | solution.py:255
  23.5 0.0 collective-permute-done.2.refs_4_
  23.5 5.5 %collective-permute-start.6 = (f32[8,32,256]{2,1,0:T(8,128)S(1)}, f32[8,32,256]{2,1,0:T(8,128)S(1)}, u32[]{:S(2)}, u32[]{:S(2)}) collective-permute-start(f32[8,32,256]{2,1,0:T(8,128)S(1)} %collective-permute-done.2.refs_4_), channel_id=1, source_target_pairs={{8,0},{12,4},{16,8},{20,12},{24,16},{28,20},{32,24},{36,28},{40,32... | collective-permute-start | bytes 786440 | tf_op jit(solution)/shard_map/ppermute | solution.py:255
  29.0 2.5 %collective-permute-done.5.refs_7_ = f32[8,32,256]{2,1,0:T(8,128)S(1)} collective-permute-done((f32[8,32,256]{2,1,0:T(8,128)S(1)}, f32[8,32,256]{2,1,0:T(8,128)S(1)}, u32[]{:S(2)}, u32[]{:S(2)}) %collective-permute-start.5) | collective-permute-done | bytes 262176 | tf_op jit(solution)/shard_map/ppermute | solution.py:255
  31.5 0.7 collective-permute-done.6.refs_8_
  32.3 1.3 %collective-permute-start.7 = (f32[8,32,256]{2,1,0:T(8,128)S(1)}, f32[8,32,256]{2,1,0:T(8,128)S(1)}, u32[]{:S(2)}, u32[]{:S(2)}) collective-permute-start(f32[8,32,256]{2,1,0:T(8,128)S(1)} %broadcast_select_fusion), channel_id=1, source_target_pairs={{0,4},{4,0},{8,12},{12,8},{16,20},{20,16},{24,28},{28,24},{32,36},... | collective-permute-start | bytes 786440 | tf_op jit(solution)/shard_map/ppermute | solution.py:255
  33.6 0.0 collective-permute-done.3.refs_5_
  33.6 0.0 collective-permute-done.4.refs_6_
  33.6 0.0 copy-start.5
  33.7 0.0 copy-start.7
  33.7 0.0 copy-start.3
  33.7 0.0 copy-start.4
  33.7 0.0 copy-start.2
  33.8 5.3 %collective-permute-done.7.refs_9_ = f32[8,32,256]{2,1,0:T(8,128)S(1)} collective-permute-done((f32[8,32,256]{2,1,0:T(8,128)S(1)}, f32[8,32,256]{2,1,0:T(8,128)S(1)}, u32[]{:S(2)}, u32[]{:S(2)}) %collective-permute-start.7) | collective-permute-done | bytes 262176 | tf_op jit(solution)/shard_map/ppermute | solution.py:255
  39.1 0.0 copy-start
  39.1 0.0 copy-start.1
  39.1 6.4 %collective-permute-start.10 = (f32[68,8,256]{2,1,0:T(8,128)S(1)}, f32[68,8,256]{2,1,0:T(8,128)S(1)}, u32[]{:S(2)}, u32[]{:S(2)}) collective-permute-start(f32[68,8,256]{2,1,0:T(8,128)S(1)} %get-tuple-element.7), channel_id=1, source_target_pairs={{1,0},{2,1},{3,2},{5,4},{6,5},{7,6},{9,8},{10,9},{11,10},{13,12},{... | collective-permute-start | bytes 1671176 | tf_op jit(solution)/shard_map/ppermute | solution.py:255
  45.5 2.1 %collective-permute-start.9 = (f32[68,8,256]{2,1,0:T(8,128)S(1)}, f32[68,8,256]{2,1,0:T(8,128)S(1)}, u32[]{:S(2)}, u32[]{:S(2)}) collective-permute-start(f32[68,8,256]{2,1,0:T(8,128)S(1)} %get-tuple-element.8), channel_id=1, source_target_pairs={{0,1},{1,2},{2,3},{4,5},{5,6},{6,7},{8,9},{9,10},{10,11},{12,13},{... | collective-permute-start | bytes 1671176 | tf_op jit(solution)/shard_map/ppermute | solution.py:255
  47.7 0.0 copy-done.5
  47.7 0.0 copy-done.7
  47.7 0.0 copy-done.3
  47.7 0.0 copy-done.4
  47.7 0.0 copy-done.2
  47.7 0.0 copy-done
  47.7 0.0 copy-done.1
  47.7 0.0 copy-start.6
  47.7 11.5 %tensor_middle.1.refs_3_ = f32[16,6,8,256]{3,2,1,0:T(8,128)S(1)} custom-call(s32[1]{0:T(128)} %bitcast.refs_0_, f32[8,32,256]{2,1,0:T(8,128)S(1)} %bitcast.8, f32[8,32,256]{2,1,0:T(8,128)S(1)} %collective-permute-done.refs_2_, f32[8,32,256]{2,1,0:T(8,128)S(1)} %collective-permute-done.1.refs_3_, f32[8,32,256]{2,1,0:T(8,128)S(1)} %collective-permute-done.2.refs_4_, ...), custom_call_target="tpu_custom_call" | custom-call | flops 8000000000 | bytes 4194304 | tf_op jit(solution)/shard_map/tensor_middle/pallas_call | solution.py:296
  59.2 2.2 %collective-permute-start.13 = (f32[16,6,8,256]{3,2,1,0:T(8,128)S(1)}, f32[16,6,8,256]{3,2,1,0:T(8,128)S(1)}, u32[]{:S(2)}, u32[]{:S(2)}) collective-permute-start(f32[16,6,8,256]{3,2,1,0:T(8,128)S(1)} %tensor_middle.1.refs_3_), channel_id=1, source_target_pairs={{1,0},{2,1},{3,2},{5,4},{6,5},{7,6},{9,8},{10,9},{11,10},{13,12},{... | collective-permute-start | bytes 2359304 | tf_op jit(solution)/shard_map/ppermute | solution.py:255
  61.5 3.3 %collective-permute-start.8 = (f32[16,6,8,256]{3,2,1,0:T(8,128)S(1)}, f32[16,6,8,256]{3,2,1,0:T(8,128)S(1)}, u32[]{:S(2)}, u32[]{:S(2)}) collective-permute-start(f32[16,6,8,256]{3,2,1,0:T(8,128)S(1)} %tensor_middle.1.refs_3_), channel_id=1, source_target_pairs={{0,1},{1,2},{2,3},{4,5},{5,6},{6,7},{8,9},{9,10},{10,11},{12,13},{... | collective-permute-start | bytes 2359304 | tf_op jit(solution)/shard_map/ppermute | solution.py:255
  64.8 0.0 collective-permute-done.10.refs_11_
  64.8 0.0 collective-permute-done.9.refs_10_
  64.8 0.0 copy-done.6
  64.8 11.6 %tensor_ends.1 = (f32[8,6,8,256]{3,2,1,0:T(8,128)S(1)}, f32[8,6,8,256]{3,2,1,0:T(8,128)S(1)}) custom-call(s32[1]{0:T(128)} %bitcast.refs_0_, f32[8,32,256]{2,1,0:T(8,128)S(1)} %bitcast.9, f32[8,32,256]{2,1,0:T(8,128)S(1)} %collective-permute-done.refs_2_, f32[8,32,256]{2,1,0:T(8,128)S(1)} %collective-permute-done.1.refs_3_, ...), custom_call_target="tpu_custom_call" | custom-call | flops 8000000000 | bytes 4194304 | tf_op jit(solution)/shard_map/tensor_ends/pallas_call | solution.py:296
  76.4 1.9 %collective-permute-start.11 = (f32[8,6,8,256]{3,2,1,0:T(8,128)S(1)}, f32[8,6,8,256]{3,2,1,0:T(8,128)S(1)}, u32[]{:S(2)}, u32[]{:S(2)}) collective-permute-start(f32[8,6,8,256]{3,2,1,0:T(8,128)S(1)} %get-tuple-element.5.refs_4_), channel_id=1, source_target_pairs={{0,1},{1,2},{2,3},{4,5},{5,6},{6,7},{8,9},{9,10},{10,11},{12,13},{... | collective-permute-start | bytes 1179656 | tf_op jit(solution)/shard_map/ppermute | solution.py:255
  78.4 2.4 %collective-permute-start.12 = (f32[8,6,8,256]{3,2,1,0:T(8,128)S(1)}, f32[8,6,8,256]{3,2,1,0:T(8,128)S(1)}, u32[]{:S(2)}, u32[]{:S(2)}) collective-permute-start(f32[8,6,8,256]{3,2,1,0:T(8,128)S(1)} %get-tuple-element.6.refs_2_), channel_id=1, source_target_pairs={{1,0},{2,1},{3,2},{5,4},{6,5},{7,6},{9,8},{10,9},{11,10},{13,12},{... | collective-permute-start | bytes 1179656 | tf_op jit(solution)/shard_map/ppermute | solution.py:255
  80.8 0.0 collective-permute-done.13.refs_6_
  80.8 0.0 collective-permute-done.8.refs_0_
  80.8 2.2 %collective-permute-done.11.refs_1_ = f32[8,6,8,256]{3,2,1,0:T(8,128)S(1)} collective-permute-done((f32[8,6,8,256]{3,2,1,0:T(8,128)S(1)}, f32[8,6,8,256]{3,2,1,0:T(8,128)S(1)}, u32[]{:S(2)}, u32[]{:S(2)}) %collective-permute-start.11) | collective-permute-done | bytes 393248 | tf_op jit(solution)/shard_map/ppermute | solution.py:255
  83.1 4.4 %collective-permute-done.12.refs_5_ = f32[8,6,8,256]{3,2,1,0:T(8,128)S(1)} collective-permute-done((f32[8,6,8,256]{3,2,1,0:T(8,128)S(1)}, f32[8,6,8,256]{3,2,1,0:T(8,128)S(1)}, u32[]{:S(2)}, u32[]{:S(2)}) %collective-permute-start.12) | collective-permute-done | bytes 393248 | tf_op jit(solution)/shard_map/ppermute | solution.py:255
  87.4 1.7 %attributes.1 = (f32[32,8,256]{2,1,0:T(8,128)}, f32[32,8,256]{2,1,0:T(8,128)}, f32[32,8,256]{2,1,0:T(8,128)}) custom-call(f32[16,6,8,256]{3,2,1,0:T(8,128)S(1)} %collective-permute-done.8.refs_0_, f32[8,6,8,256]{3,2,1,0:T(8,128)S(1)} %collective-permute-done.11.refs_1_, f32[8,6,8,256]{3,2,1,0:T(8,128)S(1)} %get-tuple-element.6.refs_2_, ...), custom_call_target="tpu_custom_call" | custom-call | tf_op jit(solution)/shard_map/attributes/pallas_call | solution.py:331
  (10 shorter events, 0.1 us)
Async XLA Ops:
  1.7 12.4 %collective-permute-start = (f32[8,32,256]{2,1,0:T(8,128)S(1)}, f32[8,32,256]{2,1,0:T(8,128)S(1)}, u32[]{:S(2)}, u32[]{:S(2)}) collective-permute-start(f32[8,32,256]{2,1,0:T(8,128)S(1)} %bitcast.4), channel_id=1, source_target_pairs={{0,4},{4,0},{8,12},{12,8},{16,20},{20,16},{24,28},{28,24},{32,36},... | collective-permute-start | bytes 786440 | tf_op jit(solution)/shard_map/ppermute | solution.py:255
  4.5 17.0 %collective-permute-start.1 = (f32[8,32,256]{2,1,0:T(8,128)S(1)}, f32[8,32,256]{2,1,0:T(8,128)S(1)}, u32[]{:S(2)}, u32[]{:S(2)}) collective-permute-start(f32[8,32,256]{2,1,0:T(8,128)S(1)} %bitcast.5), channel_id=1, source_target_pairs={{0,8},{4,12},{8,16},{12,20},{16,24},{20,28},{24,32},{28,36},{32,40... | collective-permute-start | bytes 786440 | tf_op jit(solution)/shard_map/ppermute | solution.py:255
  8.0 15.4 %collective-permute-start.2 = (f32[8,32,256]{2,1,0:T(8,128)S(1)}, f32[8,32,256]{2,1,0:T(8,128)S(1)}, u32[]{:S(2)}, u32[]{:S(2)}) collective-permute-start(f32[8,32,256]{2,1,0:T(8,128)S(1)} %bitcast.6), channel_id=1, source_target_pairs={{8,0},{12,4},{16,8},{20,12},{24,16},{28,20},{32,24},{36,28},{40,32... | collective-permute-start | bytes 786440 | tf_op jit(solution)/shard_map/ppermute | solution.py:255
  14.1 19.5 %collective-permute-start.3 = (f32[8,32,256]{2,1,0:T(8,128)S(1)}, f32[8,32,256]{2,1,0:T(8,128)S(1)}, u32[]{:S(2)}, u32[]{:S(2)}) collective-permute-start(f32[8,32,256]{2,1,0:T(8,128)S(1)} %collective-permute-done.refs_2_), channel_id=1, source_target_pairs={{0,8},{4,12},{8,16},{12,20},{16,24},{20,28},{24,32},{28,36},{32,40... | collective-permute-start | bytes 786440 | tf_op jit(solution)/shard_map/ppermute | solution.py:255
  16.1 17.6 %collective-permute-start.4 = (f32[8,32,256]{2,1,0:T(8,128)S(1)}, f32[8,32,256]{2,1,0:T(8,128)S(1)}, u32[]{:S(2)}, u32[]{:S(2)}) collective-permute-start(f32[8,32,256]{2,1,0:T(8,128)S(1)} %collective-permute-done.refs_2_), channel_id=1, source_target_pairs={{8,0},{12,4},{16,8},{20,12},{24,16},{28,20},{32,24},{36,28},{40,32... | collective-permute-start | bytes 786440 | tf_op jit(solution)/shard_map/ppermute | solution.py:255
  21.5 10.0 %collective-permute-start.5 = (f32[8,32,256]{2,1,0:T(8,128)S(1)}, f32[8,32,256]{2,1,0:T(8,128)S(1)}, u32[]{:S(2)}, u32[]{:S(2)}) collective-permute-start(f32[8,32,256]{2,1,0:T(8,128)S(1)} %collective-permute-done.1.refs_3_), channel_id=1, source_target_pairs={{0,8},{4,12},{8,16},{12,20},{16,24},{20,28},{24,32},{28,36},{32,40... | collective-permute-start | bytes 786440 | tf_op jit(solution)/shard_map/ppermute | solution.py:255
  23.5 8.8 %collective-permute-start.6 = (f32[8,32,256]{2,1,0:T(8,128)S(1)}, f32[8,32,256]{2,1,0:T(8,128)S(1)}, u32[]{:S(2)}, u32[]{:S(2)}) collective-permute-start(f32[8,32,256]{2,1,0:T(8,128)S(1)} %collective-permute-done.2.refs_4_), channel_id=1, source_target_pairs={{8,0},{12,4},{16,8},{20,12},{24,16},{28,20},{32,24},{36,28},{40,32... | collective-permute-start | bytes 786440 | tf_op jit(solution)/shard_map/ppermute | solution.py:255
  32.3 6.8 %collective-permute-start.7 = (f32[8,32,256]{2,1,0:T(8,128)S(1)}, f32[8,32,256]{2,1,0:T(8,128)S(1)}, u32[]{:S(2)}, u32[]{:S(2)}) collective-permute-start(f32[8,32,256]{2,1,0:T(8,128)S(1)} %broadcast_select_fusion), channel_id=1, source_target_pairs={{0,4},{4,0},{8,12},{12,8},{16,20},{20,16},{24,28},{28,24},{32,36},... | collective-permute-start | bytes 786440 | tf_op jit(solution)/shard_map/ppermute | solution.py:255
  33.6 14.0 %copy-start.5 = (bf16[256,256]{1,0:T(8,128)(2,1)S(1)}, bf16[256,256]{1,0:T(8,128)(2,1)}, u32[]{:S(2)}) copy-start(bf16[256,256]{1,0:T(8,128)(2,1)} %constant.33.clone.refs_16_.refs_18_) | copy-start | bytes 393220
  33.7 14.0 %copy-start.7 = (bf16[64,32]{1,0:T(8,128)(2,1)S(1)}, bf16[64,32]{1,0:T(8,128)(2,1)}, u32[]{:S(2)}) copy-start(bf16[64,32]{1,0:T(8,128)(2,1)} %constant.34.clone.refs_10_) | copy-start | bytes 12292
  33.7 14.0 %copy-start.3 = (bf16[256,256]{1,0:T(8,128)(2,1)S(1)}, bf16[256,256]{1,0:T(8,128)(2,1)}, u32[]{:S(2)}) copy-start(bf16[256,256]{1,0:T(8,128)(2,1)} %constant.31.clone.refs_14_.refs_16_) | copy-start | bytes 393220
  33.7 14.0 %copy-start.4 = (bf16[256,256]{1,0:T(8,128)(2,1)S(1)}, bf16[256,256]{1,0:T(8,128)(2,1)}, u32[]{:S(2)}) copy-start(bf16[256,256]{1,0:T(8,128)(2,1)} %constant.32.clone.refs_15_.refs_17_) | copy-start | bytes 393220
  33.7 14.0 %copy-start.2 = (bf16[256,256]{1,0:T(8,128)(2,1)S(1)}, bf16[256,256]{1,0:T(8,128)(2,1)}, u32[]{:S(2)}) copy-start(bf16[256,256]{1,0:T(8,128)(2,1)} %constant.30.clone.refs_13_.refs_15_) | copy-start | bytes 393220
  39.1 8.6 %copy-start = (bf16[256,256]{1,0:T(8,128)(2,1)S(1)}, bf16[256,256]{1,0:T(8,128)(2,1)}, u32[]{:S(2)}) copy-start(bf16[256,256]{1,0:T(8,128)(2,1)} %constant.28.clone.refs_11_.refs_13_) | copy-start | bytes 393220
  39.1 8.6 %copy-start.1 = (bf16[256,256]{1,0:T(8,128)(2,1)S(1)}, bf16[256,256]{1,0:T(8,128)(2,1)}, u32[]{:S(2)}) copy-start(bf16[256,256]{1,0:T(8,128)(2,1)} %constant.29.clone.refs_12_.refs_14_) | copy-start | bytes 393220
  39.1 25.7 %collective-permute-start.10 = (f32[68,8,256]{2,1,0:T(8,128)S(1)}, f32[68,8,256]{2,1,0:T(8,128)S(1)}, u32[]{:S(2)}, u32[]{:S(2)}) collective-permute-start(f32[68,8,256]{2,1,0:T(8,128)S(1)} %get-tuple-element.7), channel_id=1, source_target_pairs={{1,0},{2,1},{3,2},{5,4},{6,5},{7,6},{9,8},{10,9},{11,10},{13,12},{... | collective-permute-start | bytes 1671176 | tf_op jit(solution)/shard_map/ppermute | solution.py:255
  45.5 19.3 %collective-permute-start.9 = (f32[68,8,256]{2,1,0:T(8,128)S(1)}, f32[68,8,256]{2,1,0:T(8,128)S(1)}, u32[]{:S(2)}, u32[]{:S(2)}) collective-permute-start(f32[68,8,256]{2,1,0:T(8,128)S(1)} %get-tuple-element.8), channel_id=1, source_target_pairs={{0,1},{1,2},{2,3},{4,5},{5,6},{6,7},{8,9},{9,10},{10,11},{12,13},{... | collective-permute-start | bytes 1671176 | tf_op jit(solution)/shard_map/ppermute | solution.py:255
  47.7 17.1 %copy-start.6 = (bf16[64,48]{1,0:T(8,128)(2,1)S(1)}, bf16[64,48]{1,0:T(8,128)(2,1)}, u32[]{:S(2)}) copy-start(bf16[64,48]{1,0:T(8,128)(2,1)} %constant.35.clone.refs_12_) | copy-start | bytes 18436
  59.2 21.6 %collective-permute-start.13 = (f32[16,6,8,256]{3,2,1,0:T(8,128)S(1)}, f32[16,6,8,256]{3,2,1,0:T(8,128)S(1)}, u32[]{:S(2)}, u32[]{:S(2)}) collective-permute-start(f32[16,6,8,256]{3,2,1,0:T(8,128)S(1)} %tensor_middle.1.refs_3_), channel_id=1, source_target_pairs={{1,0},{2,1},{3,2},{5,4},{6,5},{7,6},{9,8},{10,9},{11,10},{13,12},{... | collective-permute-start | bytes 2359304 | tf_op jit(solution)/shard_map/ppermute | solution.py:255
  61.5 19.3 %collective-permute-start.8 = (f32[16,6,8,256]{3,2,1,0:T(8,128)S(1)}, f32[16,6,8,256]{3,2,1,0:T(8,128)S(1)}, u32[]{:S(2)}, u32[]{:S(2)}) collective-permute-start(f32[16,6,8,256]{3,2,1,0:T(8,128)S(1)} %tensor_middle.1.refs_3_), channel_id=1, source_target_pairs={{0,1},{1,2},{2,3},{4,5},{5,6},{6,7},{8,9},{9,10},{10,11},{12,13},{... | collective-permute-start | bytes 2359304 | tf_op jit(solution)/shard_map/ppermute | solution.py:255
  76.4 6.6 %collective-permute-start.11 = (f32[8,6,8,256]{3,2,1,0:T(8,128)S(1)}, f32[8,6,8,256]{3,2,1,0:T(8,128)S(1)}, u32[]{:S(2)}, u32[]{:S(2)}) collective-permute-start(f32[8,6,8,256]{3,2,1,0:T(8,128)S(1)} %get-tuple-element.5.refs_4_), channel_id=1, source_target_pairs={{0,1},{1,2},{2,3},{4,5},{5,6},{6,7},{8,9},{9,10},{10,11},{12,13},{... | collective-permute-start | bytes 1179656 | tf_op jit(solution)/shard_map/ppermute | solution.py:255
  78.4 9.1 %collective-permute-start.12 = (f32[8,6,8,256]{3,2,1,0:T(8,128)S(1)}, f32[8,6,8,256]{3,2,1,0:T(8,128)S(1)}, u32[]{:S(2)}, u32[]{:S(2)}) collective-permute-start(f32[8,6,8,256]{3,2,1,0:T(8,128)S(1)} %get-tuple-element.6.refs_2_), channel_id=1, source_target_pairs={{1,0},{2,1},{3,2},{5,4},{6,5},{7,6},{9,8},{10,9},{11,10},{13,12},{... | collective-permute-start | bytes 1179656 | tf_op jit(solution)/shard_map/ppermute | solution.py:255

commit v2 on v1

--- a/solution.py
+++ b/solution.py
@@ -58,15 +58,19 @@
     return np.where(offset <= HALF, values, 0.0)
 
 
-def depth_matrix(planes, halo):
-    position = np.concatenate(
-        [np.arange(planes), np.arange(-halo, 0), np.arange(planes, planes + halo)]
-    )
-    offset = position[None, :] - np.arange(planes)[:, None]
-    inside = np.abs(offset) <= GHALF
-    index = np.clip(offset + GHALF, 0, 2 * GHALF)
+def tile_matrix(rows, planes):
+    def band(taps, outputs, inputs, lead):
+        offset = np.arange(inputs)[None, :] - np.arange(outputs)[:, None] - lead
+        inside = np.abs(offset) <= GHALF
+        return np.where(inside, taps[np.clip(offset + GHALF, 0, 2 * GHALF)], 0.0)
+
+    def pair(cross, depth):
+        cross = band(cross, rows, rows + 2 * GHALF, GHALF)
+        depth = band(depth, planes, 3 * planes, planes)
+        return np.kron(cross, depth)
+
     return np.concatenate(
-        [np.where(inside, SMOOTH[index], 0.0), np.where(inside, SLOPE[index], 0.0)], axis=0
+        [pair(SMOOTH, SMOOTH), pair(SLOPE, SMOOTH), pair(SMOOTH, SLOPE)], axis=0
     )
 
 
@@ -85,101 +89,74 @@
     return dot(high, w_high) + (dot(high, w_low) + dot(low, w_high))
 
 
-def symmetric_pair(load, centre, reach, smooth, slope):
-    mid = load(centre)
-    total = None if smooth is None else smooth[reach] * mid
-    tilt = None
-    for k in range(1, reach + 1):
-        after, before = load(centre + k), load(centre - k)
-        if smooth is not None:
-            total = total + smooth[reach + k] * (after + before)
-        if slope is not None:
-            term = slope[reach + k] * (after - before)
-            tilt = term if tilt is None else tilt + term
-    return total, tilt
-
-
-def tensor_kernel(
-    rows, total_rows, tiles, width, halos, *refs
-):
-    where_ref, own, other, above, below, above_other, below_other, above_far, below_far, last_far = refs[:10]
+def tensor_kernel(rows, total_rows, tiles, width, halos, *refs):
+    where_ref = refs[0]
+    blocks, refs = refs[1:10], refs[10:]
     if halos:
-        up, down = refs[10:12]
+        up, down = refs[:2]
         refs = refs[2:]
-    wz_stack, wd_high, wd_low, wg_high, wg_low, ws_high, ws_low = refs[10:17]
-    outs = refs[17 : 17 + (2 if halos else 1)]
-    zg, zd, gx, gy, gz, pre, part, ty = refs[-8:]
-    planes = 8 * tiles
+    taps, wd_high, wd_low, wg_high, wg_low, ws_high, ws_low = refs[:7]
+    outs = refs[7 : 7 + (2 if halos else 1)]
+    raw_high, raw_low, pre_high, pre_low, grads, part, ty = refs[-7:]
+    count = len(tiles)
+    planes = 8 * count
     device = where_ref[0]
-    odd = lax.rem(device, 2)
-    toward = (1 - 2 * odd) * rows
+    side = 1 - 2 * lax.rem(device, 2)
     outer = rows + 2 * HALF
-    smooth = [float(v) for v in SMOOTH]
-    slope = [float(v) for v in SLOPE]
     trim = 4 * rows - REACH
-    pieces = [
-        (own, 0, rows, 0, REACH),
-        (other, 0, rows, rows, REACH + toward),
-        (above, 0, rows, 2 * rows, REACH - 2 * rows),
-        (below, 0, rows, 3 * rows, REACH + 2 * rows),
-        (above_other, 0, rows, 4 * rows, REACH - 2 * rows + toward),
-        (below_other, 0, rows, 5 * rows, REACH + 2 * rows + toward),
-        (above_far, trim, rows - trim, 6 * rows, 0),
-        (below_far, 0, rows - trim, 7 * rows - trim, REACH + 4 * rows),
-        (last_far, 0, rows, 8 * rows - 2 * trim, REACH - 3 * rows * (1 - 2 * odd)),
-    ]
-    for ref, first, count, place, base in pieces:
-
-        def depth_row(i, carry, ref=ref, first=first, place=place, base=base):
-            x = ref[first + i]
-            if halos:
-                x = jnp.concatenate([x, up[place + i], down[place + i]], axis=0)
-            high, low = split(x)
-            stacked = dot(wz_stack[...], high)
-            result = stacked[: 2 * planes] + (
-                stacked[2 * planes :] + dot(wz_stack[0 : 2 * planes, :], low)
-            )
-            zg[base + i] = result[:planes]
-            zd[base + i] = result[planes:]
-            return carry
-
-        lax.fori_loop(0, count, depth_row, 0, unroll=2)
+    places = [0, side, -2, 2, side - 2, side + 2, -4, 4, -3 * side]
+    starts = [n * rows for n in range(6)]
+    starts += [6 * rows - trim, 7 * rows - trim, 8 * rows - 2 * trim]
+    span = 3 * 8
+    for n, plane in enumerate(tiles):
+        for block, place, start in zip(blocks, places, starts):
+            low_plane, high_plane = plane - 8, plane + 16
+            if low_plane < 0:
+                x = jnp.concatenate([up[start : start + rows], block[:, :high_plane]], axis=1)
+            elif high_plane > block.shape[1]:
+                x = jnp.concatenate([block[:, low_plane:], down[start : start + rows]], axis=1)
+            else:
+                x = block[:, low_plane:high_plane]
+            high, low = split(x.reshape(rows * span, width))
+            at = pl.ds(pl.multiple_of((place + 4) * (rows * span), 16), rows * span)
+            raw_high[n, at, :] = high
+            raw_low[n, at, :] = low
 
     group = 8
-    for start in range(0, outer, group):
-
-        def cross_row(r, carry, start=start):
-            centre = start + r + GHALF
-            position = device * rows + (start + r - HALF)
-            inside = jnp.logical_and(position >= 0, position < total_rows).astype(F32)
-            for z in range(0, planes, 8):
-                both = symmetric_pair(
-                    lambda j, z=z: zg[j, z : z + 8, :], centre, GHALF, smooth, slope
-                )
-                third, _ = symmetric_pair(
-                    lambda j, z=z: zd[j, z : z + 8, :], centre, GHALF, smooth, None
-                )
-                at = pl.multiple_of(r * planes + z, 8)
-                pre[0, pl.ds(at, 8), :] = both[0] * inside
-                pre[1, pl.ds(at, 8), :] = both[1] * inside
-                pre[2, pl.ds(at, 8), :] = third * inside
-            return carry
-
-        lax.fori_loop(0, group, cross_row, 0)
-        shape = (group, planes, width)
-        gx[start : start + group] = dot3(pre[0], wd_high[...], wd_low[...]).reshape(shape)
-        gy[start : start + group] = dot3(pre[1], wg_high[...], wg_low[...]).reshape(shape)
-        gz[start : start + group] = dot3(pre[2], wg_high[...], wg_low[...]).reshape(shape)
+    size = group * 8
+    reach = (group + 2 * GHALF) * span
+    for n in range(count):
+        for start in range(0, outer, group):
+            at = (start + trim) * span
+            high, low = raw_high[n, at : at + reach, :], raw_low[n, at : at + reach, :]
+            both = dot(taps[...], high)
+            result = both[: 3 * size] + (both[3 * size :] + dot(taps[: 3 * size, :], low))
+            first = device * rows + (start - HALF)
+            row = first + lax.broadcasted_iota(jnp.int32, (size, width), 0) // 8
+            inside = jnp.logical_and(row >= 0, row < total_rows).astype(F32)
+            to = n * outer * 8 + start * 8
+            for f in range(3):
+                high, low = split(result[f * size : (f + 1) * size] * inside)
+                pre_high[f, to : to + size, :] = high
+                pre_low[f, to : to + size, :] = low
+    for f, (w_high, w_low) in enumerate(
+        ((wd_high, wd_low), (wg_high, wg_low), (wg_high, wg_low))
+    ):
+        for n in range(count):
+            at = slice(n * outer * 8, (n + 1) * outer * 8)
+            high, low = pre_high[f, at, :], pre_low[f, at, :]
+            result = dot(high, w_high[...]) + (dot(high, w_low[...]) + dot(low, w_high[...]))
+            grads[f, at, :] = result
 
     def products(j, at, lanes):
-        x, y, z = (ref[j, pl.ds(at, 8), lanes] for ref in (gx, gy, gz))
+        x, y, z = (grads[f, pl.ds(at + 8 * j, 8), lanes] for f in range(3))
         return [x * x, y * y, z * z, x * y, x * z, y * z]
 
     for lane in range(0, width, 128):
         lanes = slice(lane, lane + 128)
 
         def average_rows(t, carry, lane=lane, lanes=lanes):
-            at = pl.multiple_of(t * 8, 8)
+            at = pl.multiple_of(t * (outer * 8), 8)
             state = products(0, at, lanes)
             for j in range(1, HALF + 1):
                 state = [DECAY * s + v for s, v in zip(state, products(j, at, lanes))]
@@ -203,7 +180,7 @@
                     ]
             return carry
 
-        lax.fori_loop(0, planes // 8, average_rows, 0)
+        lax.fori_loop(0, count, average_rows, 0)
 
     for f in range(6):
         held = jnp.concatenate([ty[h, f] for h in range(width // 128)], axis=1)
@@ -281,32 +258,27 @@
         inline_matrix(SLOPE, width), inline_matrix(SMOOTH, width), average_matrix(width)
     ):
         weights += [jnp.asarray(w) for w in split_constant(matrix)]
-    matrix = depth_matrix(planes, halo)
-    index = np.arange(planes)
-    inner = np.logical_and(index >= halo, index < planes - halo)
-
-    def tensors(chosen, halos, name):
-        used = int(np.sum(chosen))
-        columns = matrix.shape[1] if halos else planes
-        part = matrix[np.concatenate([chosen, chosen])][:, :columns]
-        stack = jnp.asarray(np.concatenate(split_constant(part), axis=0))
-        outer = rows + 2 * HALF
+    matrix = np.concatenate(split_constant(tile_matrix(8, 8)), axis=0)
+    weights = [jnp.asarray(matrix)] + weights
+    outer = rows + 2 * HALF
+
+    def tensors(tiles, halos, name):
+        used = 8 * len(tiles)
         outs = 2 if halos else 1
-        operands = pieces + (list(halos) if halos else []) + [stack] + weights
+        operands = pieces + (list(halos) if halos else []) + weights
         return pl.pallas_call(
             functools.partial(
-                tensor_kernel, rows, rows * groups, used // 8, width, bool(halos)
+                tensor_kernel, rows, rows * groups, tiles, width, bool(halos)
             ),
             out_shape=[jax.ShapeDtypeStruct((used // outs, 6, rows, width), F32)] * outs,
             in_specs=[pl.BlockSpec(memory_space=pltpu.SMEM)] + [whole] * len(operands),
             out_specs=[whole] * outs,
             scratch_shapes=[
-                pltpu.VMEM((rows + 2 * REACH, used, width), F32),
-                pltpu.VMEM((rows + 2 * REACH, used, width), F32),
-                pltpu.VMEM((outer, used, width), F32),
-                pltpu.VMEM((outer, used, width), F32),
-                pltpu.VMEM((outer, used, width), F32),
-                pltpu.VMEM((3, 8 * used, width), F32),
+                pltpu.VMEM((len(tiles), 9 * rows * 24, width), BF16),
+                pltpu.VMEM((len(tiles), 9 * rows * 24, width), BF16),
+                pltpu.VMEM((3, outer * used, width), BF16),
+                pltpu.VMEM((3, outer * used, width), BF16),
+                pltpu.VMEM((3, outer * used, width), F32),
                 pltpu.VMEM((6, rows, 8, 128), F32),
                 pltpu.VMEM((width // 128, 6, used * rows, 128), F32),
             ],
@@ -318,10 +290,10 @@
         )(device.reshape(1), *operands)
 
     whole = pl.BlockSpec(memory_space=pltpu.VMEM)
-    (middle,) = tensors(inner, None, "tensor_middle")
+    (middle,) = tensors([8, 16], None, "tensor_middle")
     middle_above = send(middle, "gz", lambda i: i + 1)
     middle_below = send(middle, "gz", lambda i: i - 1)
-    first, last = tensors(~inner, (up, down), "tensor_ends")
+    first, last = tensors([0, 24], (up, down), "tensor_ends")
     last_above = send(last, "gz", lambda i: i + 1)
     first_below = send(first, "gz", lambda i: i - 1)
     arrays = [middle_above, last_above, first, middle, last, first_below, middle_below]

time: 89.6 us -> 76.4 us (0.85)
  Pallas kernels: 24.8 us -> 11.6 us
    pallas_call x2, Pallas kernels: 23.1 us -> 9.92 us  [tensors(): pl.pallas_call(functools.partial(tensor_kernel, rows, rows * groups, tile...]
  transfers between devices with their start and end apart: 14 -> 14, of which waited for: 5 -> 5; matrix products, arithmetic and copies ran while one was open for 0% -> 0% of each run, Pallas kernels for 26% -> 13%
where the time goes in v2:
time: 76.4 us; the launch traced here: 76 us
  starting transfers between devices  46.9 us (61%)
  waiting for transfers between devices  15.3 us (20%)
  Pallas kernels  11.6 us (15%)
  local copies, waits for them, and re-layouts  1.17 us (2%)
  between operations  0.96 us (1%)
    ppermute x14, starting transfers between devices, send(): return lax.ppermute(x, axis, pairs)  46.9 us
    ppermute x14, waiting for transfers between devices, send(): return lax.ppermute(x, axis, pairs)  15.3 us
    pallas_call x2, Pallas kernels, tensors(): pl.pallas_call(functools.partial(tensor_kernel, rows, rows * groups, tile...  9.92 us
    pallas_call x1, Pallas kernels, local(): pl.pallas_call(functools.partial(attribute_kernel, planes, width, starts)...  1.71 us
  transfers between devices with their start and end apart: 14, of which 5 were waited for; matrix products, arithmetic and copies ran while one was open for 0% of the time, Pallas kernels for 13%

profile of v2, /device:TPU:25, one launch (start us, length us, event | category | flops | bytes accessed | tf_op | source)
XLA Modules:
  0.0 76.0 jit_solution(16719294355413837630)
XLA Ops:
  0.6 1.0 %copy.13 = f32[32,8,256]{2,0,1:T(8,128)S(1)} copy(f32[32,8,256]{2,1,0:T(8,128)} %param.8) | data formatting | bytes 524288 | tf_op args[0]
  1.7 2.8 %collective-permute-start = (f32[8,32,256]{2,1,0:T(8,128)S(1)}, f32[8,32,256]{2,1,0:T(8,128)S(1)}, u32[]{:S(2)}, u32[]{:S(2)}) collective-permute-start(f32[8,32,256]{2,1,0:T(8,128)S(1)} %bitcast.4), channel_id=1, source_target_pairs={{0,4},{4,0},{8,12},{12,8},{16,20},{20,16},{24,28},{28,24},{32,36},... | collective-permute-start | bytes 786440 | tf_op jit(solution)/shard_map/ppermute | solution.py:232
  4.5 3.5 %collective-permute-start.1 = (f32[8,32,256]{2,1,0:T(8,128)S(1)}, f32[8,32,256]{2,1,0:T(8,128)S(1)}, u32[]{:S(2)}, u32[]{:S(2)}) collective-permute-start(f32[8,32,256]{2,1,0:T(8,128)S(1)} %bitcast.5), channel_id=1, source_target_pairs={{0,8},{4,12},{8,16},{12,20},{16,24},{20,28},{24,32},{28,36},{32,40... | collective-permute-start | bytes 786440 | tf_op jit(solution)/shard_map/ppermute | solution.py:232
  8.0 6.0 %collective-permute-start.2 = (f32[8,32,256]{2,1,0:T(8,128)S(1)}, f32[8,32,256]{2,1,0:T(8,128)S(1)}, u32[]{:S(2)}, u32[]{:S(2)}) collective-permute-start(f32[8,32,256]{2,1,0:T(8,128)S(1)} %bitcast.6), channel_id=1, source_target_pairs={{8,0},{12,4},{16,8},{20,12},{24,16},{28,20},{32,24},{36,28},{40,32... | collective-permute-start | bytes 786440 | tf_op jit(solution)/shard_map/ppermute | solution.py:232
  14.1 0.0 collective-permute-done.refs_2_
  14.1 1.9 %collective-permute-start.3 = (f32[8,32,256]{2,1,0:T(8,128)S(1)}, f32[8,32,256]{2,1,0:T(8,128)S(1)}, u32[]{:S(2)}, u32[]{:S(2)}) collective-permute-start(f32[8,32,256]{2,1,0:T(8,128)S(1)} %collective-permute-done.refs_2_), channel_id=1, source_target_pairs={{0,8},{4,12},{8,16},{12,20},{16,24},{20,28},{24,32},{28,36},{32,40... | collective-permute-start | bytes 786440 | tf_op jit(solution)/shard_map/ppermute | solution.py:232
  16.1 5.5 %collective-permute-start.4 = (f32[8,32,256]{2,1,0:T(8,128)S(1)}, f32[8,32,256]{2,1,0:T(8,128)S(1)}, u32[]{:S(2)}, u32[]{:S(2)}) collective-permute-start(f32[8,32,256]{2,1,0:T(8,128)S(1)} %collective-permute-done.refs_2_), channel_id=1, source_target_pairs={{8,0},{12,4},{16,8},{20,12},{24,16},{28,20},{32,24},{36,28},{40,32... | collective-permute-start | bytes 786440 | tf_op jit(solution)/shard_map/ppermute | solution.py:232
  21.5 0.0 collective-permute-done.1.refs_3_
  21.5 1.9 %collective-permute-start.5 = (f32[8,32,256]{2,1,0:T(8,128)S(1)}, f32[8,32,256]{2,1,0:T(8,128)S(1)}, u32[]{:S(2)}, u32[]{:S(2)}) collective-permute-start(f32[8,32,256]{2,1,0:T(8,128)S(1)} %collective-permute-done.1.refs_3_), channel_id=1, source_target_pairs={{0,8},{4,12},{8,16},{12,20},{16,24},{20,28},{24,32},{28,36},{32,40... | collective-permute-start | bytes 786440 | tf_op jit(solution)/shard_map/ppermute | solution.py:232
  23.5 0.0 collective-permute-done.2.refs_4_
  23.5 5.5 %collective-permute-start.6 = (f32[8,32,256]{2,1,0:T(8,128)S(1)}, f32[8,32,256]{2,1,0:T(8,128)S(1)}, u32[]{:S(2)}, u32[]{:S(2)}) collective-permute-start(f32[8,32,256]{2,1,0:T(8,128)S(1)} %collective-permute-done.2.refs_4_), channel_id=1, source_target_pairs={{8,0},{12,4},{16,8},{20,12},{24,16},{28,20},{32,24},{36,28},{40,32... | collective-permute-start | bytes 786440 | tf_op jit(solution)/shard_map/ppermute | solution.py:232
  29.0 2.5 %collective-permute-done.5.refs_7_ = f32[8,32,256]{2,1,0:T(8,128)S(1)} collective-permute-done((f32[8,32,256]{2,1,0:T(8,128)S(1)}, f32[8,32,256]{2,1,0:T(8,128)S(1)}, u32[]{:S(2)}, u32[]{:S(2)}) %collective-permute-start.5) | collective-permute-done | bytes 262176 | tf_op jit(solution)/shard_map/ppermute | solution.py:232
  31.5 0.7 collective-permute-done.6.refs_8_
  32.3 1.3 %collective-permute-start.7 = (f32[8,32,256]{2,1,0:T(8,128)S(1)}, f32[8,32,256]{2,1,0:T(8,128)S(1)}, u32[]{:S(2)}, u32[]{:S(2)}) collective-permute-start(f32[8,32,256]{2,1,0:T(8,128)S(1)} %broadcast_select_fusion), channel_id=1, source_target_pairs={{0,4},{4,0},{8,12},{12,8},{16,20},{20,16},{24,28},{28,24},{32,36},... | collective-permute-start | bytes 786440 | tf_op jit(solution)/shard_map/ppermute | solution.py:232
  33.6 0.0 collective-permute-done.3.refs_5_
  33.6 0.0 copy-start.5
  33.6 0.0 copy-start.6
  33.6 0.0 collective-permute-done.4.refs_6_
  33.6 0.0 copy-start.3
  33.7 0.0 copy-start.4
  33.7 0.0 copy-start
  33.7 5.4 %collective-permute-done.7.refs_9_ = f32[8,32,256]{2,1,0:T(8,128)S(1)} collective-permute-done((f32[8,32,256]{2,1,0:T(8,128)S(1)}, f32[8,32,256]{2,1,0:T(8,128)S(1)}, u32[]{:S(2)}, u32[]{:S(2)}) %collective-permute-start.7) | collective-permute-done | bytes 262176 | tf_op jit(solution)/shard_map/ppermute | solution.py:232
  39.1 0.0 copy-start.1
  39.1 0.0 copy-start.2
  39.1 6.4 %collective-permute-start.10 = (f32[68,8,256]{2,1,0:T(8,128)S(1)}, f32[68,8,256]{2,1,0:T(8,128)S(1)}, u32[]{:S(2)}, u32[]{:S(2)}) collective-permute-start(f32[68,8,256]{2,1,0:T(8,128)S(1)} %get-tuple-element.7), channel_id=1, source_target_pairs={{1,0},{2,1},{3,2},{5,4},{6,5},{7,6},{9,8},{10,9},{11,10},{13,12},{... | collective-permute-start | bytes 1671176 | tf_op jit(solution)/shard_map/ppermute | solution.py:232
  45.5 2.1 %collective-permute-start.9 = (f32[68,8,256]{2,1,0:T(8,128)S(1)}, f32[68,8,256]{2,1,0:T(8,128)S(1)}, u32[]{:S(2)}, u32[]{:S(2)}) collective-permute-start(f32[68,8,256]{2,1,0:T(8,128)S(1)} %get-tuple-element.8), channel_id=1, source_target_pairs={{0,1},{1,2},{2,3},{4,5},{5,6},{6,7},{8,9},{9,10},{10,11},{12,13},{... | collective-permute-start | bytes 1671176 | tf_op jit(solution)/shard_map/ppermute | solution.py:232
  47.7 0.0 copy-done.5
  47.7 0.0 copy-done.6
  47.7 0.0 copy-done.3
  47.7 0.0 copy-done.4
  47.7 0.0 copy-done
  47.7 0.0 copy-done.1
  47.7 0.0 copy-done.2
  47.7 5.0 %tensor_middle.1.refs_3_ = f32[16,6,8,256]{3,2,1,0:T(8,128)S(1)} custom-call(s32[1]{0:T(128)} %bitcast.refs_0_, f32[8,32,256]{2,1,0:T(8,128)S(1)} %bitcast.8, f32[8,32,256]{2,1,0:T(8,128)S(1)} %collective-permute-done.refs_2_, f32[8,32,256]{2,1,0:T(8,128)S(1)} %collective-permute-done.1.refs_3_, f32[8,32,256]{2,1,0:T(8,128)S(1)} %collective-permute-done.2.refs_4_, ...), custom_call_target="tpu_custom_call" | custom-call | flops 8000000000 | bytes 4194304 | tf_op jit(solution)/shard_map/tensor_middle/pallas_call | solution.py:269
  52.7 2.2 %collective-permute-start.13 = (f32[16,6,8,256]{3,2,1,0:T(8,128)S(1)}, f32[16,6,8,256]{3,2,1,0:T(8,128)S(1)}, u32[]{:S(2)}, u32[]{:S(2)}) collective-permute-start(f32[16,6,8,256]{3,2,1,0:T(8,128)S(1)} %tensor_middle.1.refs_3_), channel_id=1, source_target_pairs={{1,0},{2,1},{3,2},{5,4},{6,5},{7,6},{9,8},{10,9},{11,10},{13,12},{... | collective-permute-start | bytes 2359304 | tf_op jit(solution)/shard_map/ppermute | solution.py:232
  54.9 3.3 %collective-permute-start.8 = (f32[16,6,8,256]{3,2,1,0:T(8,128)S(1)}, f32[16,6,8,256]{3,2,1,0:T(8,128)S(1)}, u32[]{:S(2)}, u32[]{:S(2)}) collective-permute-start(f32[16,6,8,256]{3,2,1,0:T(8,128)S(1)} %tensor_middle.1.refs_3_), channel_id=1, source_target_pairs={{0,1},{1,2},{2,3},{4,5},{5,6},{6,7},{8,9},{9,10},{10,11},{12,13},{... | collective-permute-start | bytes 2359304 | tf_op jit(solution)/shard_map/ppermute | solution.py:232
  58.3 0.0 collective-permute-done.10.refs_11_
  58.3 0.0 collective-permute-done.9.refs_10_
  58.3 5.0 %tensor_ends.1 = (f32[8,6,8,256]{3,2,1,0:T(8,128)S(1)}, f32[8,6,8,256]{3,2,1,0:T(8,128)S(1)}) custom-call(s32[1]{0:T(128)} %bitcast.refs_0_, f32[8,32,256]{2,1,0:T(8,128)S(1)} %bitcast.9, f32[8,32,256]{2,1,0:T(8,128)S(1)} %collective-permute-done.refs_2_, f32[8,32,256]{2,1,0:T(8,128)S(1)} %collective-permute-done.1.refs_3_, ...), custom_call_target="tpu_custom_call" | custom-call | flops 8000000000 | bytes 4194304 | tf_op jit(solution)/shard_map/tensor_ends/pallas_call | solution.py:269
  63.3 1.9 %collective-permute-start.11 = (f32[8,6,8,256]{3,2,1,0:T(8,128)S(1)}, f32[8,6,8,256]{3,2,1,0:T(8,128)S(1)}, u32[]{:S(2)}, u32[]{:S(2)}) collective-permute-start(f32[8,6,8,256]{3,2,1,0:T(8,128)S(1)} %get-tuple-element.5.refs_4_), channel_id=1, source_target_pairs={{0,1},{1,2},{2,3},{4,5},{5,6},{6,7},{8,9},{9,10},{10,11},{12,13},{... | collective-permute-start | bytes 1179656 | tf_op jit(solution)/shard_map/ppermute | solution.py:232
  65.2 2.4 %collective-permute-start.12 = (f32[8,6,8,256]{3,2,1,0:T(8,128)S(1)}, f32[8,6,8,256]{3,2,1,0:T(8,128)S(1)}, u32[]{:S(2)}, u32[]{:S(2)}) collective-permute-start(f32[8,6,8,256]{3,2,1,0:T(8,128)S(1)} %get-tuple-element.6.refs_2_), channel_id=1, source_target_pairs={{1,0},{2,1},{3,2},{5,4},{6,5},{7,6},{9,8},{10,9},{11,10},{13,12},{... | collective-permute-start | bytes 1179656 | tf_op jit(solution)/shard_map/ppermute | solution.py:232
  67.6 0.0 collective-permute-done.13.refs_6_
  67.6 0.0 collective-permute-done.8.refs_0_
  67.6 3.8 %collective-permute-done.11.refs_1_ = f32[8,6,8,256]{3,2,1,0:T(8,128)S(1)} collective-permute-done((f32[8,6,8,256]{3,2,1,0:T(8,128)S(1)}, f32[8,6,8,256]{3,2,1,0:T(8,128)S(1)}, u32[]{:S(2)}, u32[]{:S(2)}) %collective-permute-start.11) | collective-permute-done | bytes 393248 | tf_op jit(solution)/shard_map/ppermute | solution.py:232
  71.4 2.9 %collective-permute-done.12.refs_5_ = f32[8,6,8,256]{3,2,1,0:T(8,128)S(1)} collective-permute-done((f32[8,6,8,256]{3,2,1,0:T(8,128)S(1)}, f32[8,6,8,256]{3,2,1,0:T(8,128)S(1)}, u32[]{:S(2)}, u32[]{:S(2)}) %collective-permute-start.12) | collective-permute-done | bytes 393248 | tf_op jit(solution)/shard_map/ppermute | solution.py:232
  74.3 1.7 %attributes.1 = (f32[32,8,256]{2,1,0:T(8,128)}, f32[32,8,256]{2,1,0:T(8,128)}, f32[32,8,256]{2,1,0:T(8,128)}) custom-call(f32[16,6,8,256]{3,2,1,0:T(8,128)S(1)} %collective-permute-done.8.refs_0_, f32[8,6,8,256]{3,2,1,0:T(8,128)S(1)} %collective-permute-done.11.refs_1_, f32[8,6,8,256]{3,2,1,0:T(8,128)S(1)} %get-tuple-element.6.refs_2_, ...), custom_call_target="tpu_custom_call" | custom-call | tf_op jit(solution)/shard_map/attributes/pallas_call | solution.py:303
  (10 shorter events, 0.1 us)
Async XLA Ops:
  1.7 12.4 %collective-permute-start = (f32[8,32,256]{2,1,0:T(8,128)S(1)}, f32[8,32,256]{2,1,0:T(8,128)S(1)}, u32[]{:S(2)}, u32[]{:S(2)}) collective-permute-start(f32[8,32,256]{2,1,0:T(8,128)S(1)} %bitcast.4), channel_id=1, source_target_pairs={{0,4},{4,0},{8,12},{12,8},{16,20},{20,16},{24,28},{28,24},{32,36},... | collective-permute-start | bytes 786440 | tf_op jit(solution)/shard_map/ppermute | solution.py:232
  4.5 17.0 %collective-permute-start.1 = (f32[8,32,256]{2,1,0:T(8,128)S(1)}, f32[8,32,256]{2,1,0:T(8,128)S(1)}, u32[]{:S(2)}, u32[]{:S(2)}) collective-permute-start(f32[8,32,256]{2,1,0:T(8,128)S(1)} %bitcast.5), channel_id=1, source_target_pairs={{0,8},{4,12},{8,16},{12,20},{16,24},{20,28},{24,32},{28,36},{32,40... | collective-permute-start | bytes 786440 | tf_op jit(solution)/shard_map/ppermute | solution.py:232
  8.0 15.4 %collective-permute-start.2 = (f32[8,32,256]{2,1,0:T(8,128)S(1)}, f32[8,32,256]{2,1,0:T(8,128)S(1)}, u32[]{:S(2)}, u32[]{:S(2)}) collective-permute-start(f32[8,32,256]{2,1,0:T(8,128)S(1)} %bitcast.6), channel_id=1, source_target_pairs={{8,0},{12,4},{16,8},{20,12},{24,16},{28,20},{32,24},{36,28},{40,32... | collective-permute-start | bytes 786440 | tf_op jit(solution)/shard_map/ppermute | solution.py:232
  14.1 19.5 %collective-permute-start.3 = (f32[8,32,256]{2,1,0:T(8,128)S(1)}, f32[8,32,256]{2,1,0:T(8,128)S(1)}, u32[]{:S(2)}, u32[]{:S(2)}) collective-permute-start(f32[8,32,256]{2,1,0:T(8,128)S(1)} %collective-permute-done.refs_2_), channel_id=1, source_target_pairs={{0,8},{4,12},{8,16},{12,20},{16,24},{20,28},{24,32},{28,36},{32,40... | collective-permute-start | bytes 786440 | tf_op jit(solution)/shard_map/ppermute | solution.py:232
  16.1 17.6 %collective-permute-start.4 = (f32[8,32,256]{2,1,0:T(8,128)S(1)}, f32[8,32,256]{2,1,0:T(8,128)S(1)}, u32[]{:S(2)}, u32[]{:S(2)}) collective-permute-start(f32[8,32,256]{2,1,0:T(8,128)S(1)} %collective-permute-done.refs_2_), channel_id=1, source_target_pairs={{8,0},{12,4},{16,8},{20,12},{24,16},{28,20},{32,24},{36,28},{40,32... | collective-permute-start | bytes 786440 | tf_op jit(solution)/shard_map/ppermute | solution.py:232
  21.5 10.0 %collective-permute-start.5 = (f32[8,32,256]{2,1,0:T(8,128)S(1)}, f32[8,32,256]{2,1,0:T(8,128)S(1)}, u32[]{:S(2)}, u32[]{:S(2)}) collective-permute-start(f32[8,32,256]{2,1,0:T(8,128)S(1)} %collective-permute-done.1.refs_3_), channel_id=1, source_target_pairs={{0,8},{4,12},{8,16},{12,20},{16,24},{20,28},{24,32},{28,36},{32,40... | collective-permute-start | bytes 786440 | tf_op jit(solution)/shard_map/ppermute | solution.py:232
  23.5 8.8 %collective-permute-start.6 = (f32[8,32,256]{2,1,0:T(8,128)S(1)}, f32[8,32,256]{2,1,0:T(8,128)S(1)}, u32[]{:S(2)}, u32[]{:S(2)}) collective-permute-start(f32[8,32,256]{2,1,0:T(8,128)S(1)} %collective-permute-done.2.refs_4_), channel_id=1, source_target_pairs={{8,0},{12,4},{16,8},{20,12},{24,16},{28,20},{32,24},{36,28},{40,32... | collective-permute-start | bytes 786440 | tf_op jit(solution)/shard_map/ppermute | solution.py:232
  32.3 6.8 %collective-permute-start.7 = (f32[8,32,256]{2,1,0:T(8,128)S(1)}, f32[8,32,256]{2,1,0:T(8,128)S(1)}, u32[]{:S(2)}, u32[]{:S(2)}) collective-permute-start(f32[8,32,256]{2,1,0:T(8,128)S(1)} %broadcast_select_fusion), channel_id=1, source_target_pairs={{0,4},{4,0},{8,12},{12,8},{16,20},{20,16},{24,28},{28,24},{32,36},... | collective-permute-start | bytes 786440 | tf_op jit(solution)/shard_map/ppermute | solution.py:232
  33.6 14.0 %copy-start.5 = (bf16[256,256]{1,0:T(8,128)(2,1)S(1)}, bf16[256,256]{1,0:T(8,128)(2,1)}, u32[]{:S(2)}) copy-start(bf16[256,256]{1,0:T(8,128)(2,1)} %constant.30.clone.refs_15_.refs_17_) | copy-start | bytes 393220
  33.6 14.0 %copy-start.6 = (bf16[256,256]{1,0:T(8,128)(2,1)S(1)}, bf16[256,256]{1,0:T(8,128)(2,1)}, u32[]{:S(2)}) copy-start(bf16[256,256]{1,0:T(8,128)(2,1)} %constant.31.clone.refs_16_.refs_18_) | copy-start | bytes 393220
  33.6 14.0 %copy-start.3 = (bf16[256,256]{1,0:T(8,128)(2,1)S(1)}, bf16[256,256]{1,0:T(8,128)(2,1)}, u32[]{:S(2)}) copy-start(bf16[256,256]{1,0:T(8,128)(2,1)} %constant.28.clone.refs_13_.refs_15_) | copy-start | bytes 393220
  33.7 14.0 %copy-start.4 = (bf16[256,256]{1,0:T(8,128)(2,1)S(1)}, bf16[256,256]{1,0:T(8,128)(2,1)}, u32[]{:S(2)}) copy-start(bf16[256,256]{1,0:T(8,128)(2,1)} %constant.29.clone.refs_14_.refs_16_) | copy-start | bytes 393220
  33.7 14.0 %copy-start = (bf16[384,480]{1,0:T(8,128)(2,1)S(1)}, bf16[384,480]{1,0:T(8,128)(2,1)}, u32[]{:S(2)}) copy-start(bf16[384,480]{1,0:T(8,128)(2,1)} %constant.32.clone.refs_10_.refs_12_) | copy-start | bytes 1105924
  39.1 8.6 %copy-start.1 = (bf16[256,256]{1,0:T(8,128)(2,1)S(1)}, bf16[256,256]{1,0:T(8,128)(2,1)}, u32[]{:S(2)}) copy-start(bf16[256,256]{1,0:T(8,128)(2,1)} %constant.26.clone.refs_11_.refs_13_) | copy-start | bytes 393220
  39.1 8.6 %copy-start.2 = (bf16[256,256]{1,0:T(8,128)(2,1)S(1)}, bf16[256,256]{1,0:T(8,128)(2,1)}, u32[]{:S(2)}) copy-start(bf16[256,256]{1,0:T(8,128)(2,1)} %constant.27.clone.refs_12_.refs_14_) | copy-start | bytes 393220
  39.1 19.1 %collective-permute-start.10 = (f32[68,8,256]{2,1,0:T(8,128)S(1)}, f32[68,8,256]{2,1,0:T(8,128)S(1)}, u32[]{:S(2)}, u32[]{:S(2)}) collective-permute-start(f32[68,8,256]{2,1,0:T(8,128)S(1)} %get-tuple-element.7), channel_id=1, source_target_pairs={{1,0},{2,1},{3,2},{5,4},{6,5},{7,6},{9,8},{10,9},{11,10},{13,12},{... | collective-permute-start | bytes 1671176 | tf_op jit(solution)/shard_map/ppermute | solution.py:232
  45.5 12.8 %collective-permute-start.9 = (f32[68,8,256]{2,1,0:T(8,128)S(1)}, f32[68,8,256]{2,1,0:T(8,128)S(1)}, u32[]{:S(2)}, u32[]{:S(2)}) collective-permute-start(f32[68,8,256]{2,1,0:T(8,128)S(1)} %get-tuple-element.8), channel_id=1, source_target_pairs={{0,1},{1,2},{2,3},{4,5},{5,6},{6,7},{8,9},{9,10},{10,11},{12,13},{... | collective-permute-start | bytes 1671176 | tf_op jit(solution)/shard_map/ppermute | solution.py:232
  52.7 14.9 %collective-permute-start.13 = (f32[16,6,8,256]{3,2,1,0:T(8,128)S(1)}, f32[16,6,8,256]{3,2,1,0:T(8,128)S(1)}, u32[]{:S(2)}, u32[]{:S(2)}) collective-permute-start(f32[16,6,8,256]{3,2,1,0:T(8,128)S(1)} %tensor_middle.1.refs_3_), channel_id=1, source_target_pairs={{1,0},{2,1},{3,2},{5,4},{6,5},{7,6},{9,8},{10,9},{11,10},{13,12},{... | collective-permute-start | bytes 2359304 | tf_op jit(solution)/shard_map/ppermute | solution.py:232
  54.9 12.7 %collective-permute-start.8 = (f32[16,6,8,256]{3,2,1,0:T(8,128)S(1)}, f32[16,6,8,256]{3,2,1,0:T(8,128)S(1)}, u32[]{:S(2)}, u32[]{:S(2)}) collective-permute-start(f32[16,6,8,256]{3,2,1,0:T(8,128)S(1)} %tensor_middle.1.refs_3_), channel_id=1, source_target_pairs={{0,1},{1,2},{2,3},{4,5},{5,6},{6,7},{8,9},{9,10},{10,11},{12,13},{... | collective-permute-start | bytes 2359304 | tf_op jit(solution)/shard_map/ppermute | solution.py:232
  63.3 8.1 %collective-permute-start.11 = (f32[8,6,8,256]{3,2,1,0:T(8,128)S(1)}, f32[8,6,8,256]{3,2,1,0:T(8,128)S(1)}, u32[]{:S(2)}, u32[]{:S(2)}) collective-permute-start(f32[8,6,8,256]{3,2,1,0:T(8,128)S(1)} %get-tuple-element.5.refs_4_), channel_id=1, source_target_pairs={{0,1},{1,2},{2,3},{4,5},{5,6},{6,7},{8,9},{9,10},{10,11},{12,13},{... | collective-permute-start | bytes 1179656 | tf_op jit(solution)/shard_map/ppermute | solution.py:232
  65.2 9.1 %collective-permute-start.12 = (f32[8,6,8,256]{3,2,1,0:T(8,128)S(1)}, f32[8,6,8,256]{3,2,1,0:T(8,128)S(1)}, u32[]{:S(2)}, u32[]{:S(2)}) collective-permute-start(f32[8,6,8,256]{3,2,1,0:T(8,128)S(1)} %get-tuple-element.6.refs_2_), channel_id=1, source_target_pairs={{1,0},{2,1},{3,2},{5,4},{6,5},{7,6},{9,8},{10,9},{11,10},{13,12},{... | collective-permute-start | bytes 1179656 | tf_op jit(solution)/shard_map/ppermute | solution.py:232

commit v3 on v2

--- a/solution.py
+++ b/solution.py
@@ -90,37 +90,45 @@
 
 
 def tensor_kernel(rows, total_rows, tiles, width, halos, *refs):
-    where_ref = refs[0]
-    blocks, refs = refs[1:10], refs[10:]
+    blocks, refs = refs[:9], refs[9:]
     if halos:
-        up, down = refs[:2]
-        refs = refs[2:]
+        swaps, last_halo = refs[:2], refs[2]
+        refs = refs[3:]
     taps, wd_high, wd_low, wg_high, wg_low, ws_high, ws_low = refs[:7]
-    outs = refs[7 : 7 + (2 if halos else 1)]
+    outs = refs[7 : 7 + (4 if halos else 1)]
     raw_high, raw_low, pre_high, pre_low, grads, part, ty = refs[-7:]
     count = len(tiles)
     planes = 8 * count
-    device = where_ref[0]
+    device = lax.axis_index("pa")
     side = 1 - 2 * lax.rem(device, 2)
+    even_depth = lax.rem(lax.axis_index("gz"), 2) == 0
     outer = rows + 2 * HALF
     trim = 4 * rows - REACH
-    places = [0, side, -2, 2, side - 2, side + 2, -4, 4, -3 * side]
-    starts = [n * rows for n in range(6)]
-    starts += [6 * rows - trim, 7 * rows - trim, 8 * rows - 2 * trim]
+    places = [0, -2, 2, side, -4, 4, side - 2, side + 2, -3 * side]
     span = 3 * 8
-    for n, plane in enumerate(tiles):
-        for block, place, start in zip(blocks, places, starts):
-            low_plane, high_plane = plane - 8, plane + 16
-            if low_plane < 0:
-                x = jnp.concatenate([up[start : start + rows], block[:, :high_plane]], axis=1)
-            elif high_plane > block.shape[1]:
-                x = jnp.concatenate([block[:, low_plane:], down[start : start + rows]], axis=1)
-            else:
-                x = block[:, low_plane:high_plane]
-            high, low = split(x.reshape(rows * span, width))
-            at = pl.ds(pl.multiple_of((place + 4) * (rows * span), 16), rows * span)
-            raw_high[n, at, :] = high
-            raw_low[n, at, :] = low
+
+    def stage(n, place, x):
+        high, low = split(x.reshape(rows * span, width))
+        at = pl.ds(pl.multiple_of((place + 4) * (rows * span), 16), rows * span)
+        raw_high[n, at, :] = high
+        raw_low[n, at, :] = low
+
+    def stage_ends(up, down):
+        for i, (block, place) in enumerate(zip(blocks, places)):
+            at = slice(i * rows, (i + 1) * rows)
+            last = i == len(blocks) - 1
+            above = last_halo[:, :8] if last else up[at]
+            below = last_halo[:, 8:] if last else down[at]
+            stage(0, place, jnp.concatenate([above, block[:, :16]], axis=1))
+            stage(1, place, jnp.concatenate([block[:, -16:], below], axis=1))
+
+    if halos:
+        pl.when(even_depth)(lambda: stage_ends(swaps[1], swaps[0]))
+        pl.when(jnp.logical_not(even_depth))(lambda: stage_ends(swaps[0], swaps[1]))
+    else:
+        for n, plane in enumerate(tiles):
+            for block, place in zip(blocks, places):
+                stage(n, place, block[:, plane - 8 : plane + 16])
 
     group = 8
     size = group * 8
@@ -185,13 +193,35 @@
     for f in range(6):
         held = jnp.concatenate([ty[h, f] for h in range(width // 128)], axis=1)
         field = dot3(held, ws_high[...], ws_low[...]).reshape(planes, rows, width)
-        step = planes // len(outs)
-        for n, out in enumerate(outs):
-            out[:, f] = field[n * step : (n + 1) * step]
+        if not halos:
+            outs[0][:, f] = field
+            continue
+        first, last = field[:8], field[8:]
+        outs[0][:, f] = first
+        outs[1][:, f] = last
+        outs[2][:, f] = jnp.where(even_depth, last, first)
+        outs[3][:, f] = jnp.where(even_depth, first, last)
 
 
 def attribute_kernel(planes, width, pieces, *refs):
     inline, cross, coherent, part = refs[-4:]
+    first, middle, last, ends_a, middle_a, ends_b, middle_b = refs[:7]
+    even_depth = lax.rem(lax.axis_index("gz"), 2) == 0
+    results = (inline, cross, coherent, part)
+    own = (first, middle, last)
+    pl.when(even_depth)(
+        lambda: attributes(
+            planes, width, pieces, (middle_b, ends_b, *own, ends_a, middle_a), *results
+        )
+    )
+    pl.when(jnp.logical_not(even_depth))(
+        lambda: attributes(
+            planes, width, pieces, (middle_a, ends_a, *own, ends_b, middle_b), *results
+        )
+    )
+
+
+def attributes(planes, width, pieces, refs, inline, cross, coherent, part):
     for lane in range(0, width, 128):
         lanes = slice(lane, lane + 128)
 
@@ -236,22 +266,42 @@
     planes, rows, width = volume.shape
     groups = lax.axis_size("pa")
     device = lax.axis_index("pa")
-    even = lax.rem(device, 2) == 0
-    trim = 4 * rows - REACH
+    depth = lax.rem(lax.axis_index("gz"), 2)
+    turn = lax.rem(device, 2) == lax.rem(device // 2, 2)
     halo = 8
+
+    def cross(x):
+        return send(x, "pa", lambda i: i ^ 1)
+
+    def near(x):
+        return send(x, "pa", lambda i: i ^ 2)
+
+    def away(x):
+        return send(x, "pa", lambda i: i - 2 if i % 4 < 2 else i + 2)
+
+    def depth_swaps(even_near, even_away):
+        one = send(even_near, "gz", lambda i: i ^ 1)
+        two = send(even_away, "gz", lambda i: i - 1 if i % 2 == 0 else i + 1)
+        return one, two
+
+    def ordered(one, two):
+        return jnp.where(low, two, one), jnp.where(low, one, two)
+
+    low = lax.rem(device // 2, 2) == 0
     own = volume.transpose(1, 0, 2)
-    above = send(own, "pa", lambda i: i + 2)
-    below = send(own, "pa", lambda i: i - 2)
-    other = send(own, "pa", lambda i: i ^ 1)
-    above_far = send(above, "pa", lambda i: i + 2)
-    below_far = send(below, "pa", lambda i: i - 2)
-    above_other = send(other, "pa", lambda i: i + 2)
-    below_other = send(other, "pa", lambda i: i - 2)
-    last_far = send(jnp.where(even, below_far, above_far), "pa", lambda i: i ^ 1)
-    pieces = [own, other, above, below, above_other, below_other, above_far, below_far, last_far]
-    held = pieces[:6] + [above_far[trim:], below_far[: rows - trim], last_far]
-    up = send(jnp.concatenate([x[:, planes - halo :] for x in held], axis=0), "gz", lambda i: i + 1)
-    down = send(jnp.concatenate([x[:, :halo] for x in held], axis=0), "gz", lambda i: i - 1)
+    near_own, away_own, other = near(own), away(own), cross(own)
+    near_far, away_far = near(away_own), away(near_own)
+    near_other, away_other = near(other), away(other)
+    last_far = cross(jnp.where(turn, near_far, away_far))
+    pieces = [own, *ordered(near_own, away_own), other, *ordered(near_far, away_far)]
+    pieces += ordered(near_other, away_other)
+    last_planes = jnp.concatenate([x[:, planes - halo :] for x in pieces], axis=0)
+    first_planes = jnp.concatenate([x[:, :halo] for x in pieces], axis=0)
+    even = depth == 0
+    swaps = depth_swaps(
+        jnp.where(even, last_planes, first_planes), jnp.where(even, first_planes, last_planes)
+    )
+    pieces.append(last_far)
 
     weights = []
     for matrix in (
@@ -264,14 +314,15 @@
 
     def tensors(tiles, halos, name):
         used = 8 * len(tiles)
-        outs = 2 if halos else 1
+        outs = 4 if halos else 1
+        count = 8 if halos else used
         operands = pieces + (list(halos) if halos else []) + weights
         return pl.pallas_call(
             functools.partial(
                 tensor_kernel, rows, rows * groups, tiles, width, bool(halos)
             ),
-            out_shape=[jax.ShapeDtypeStruct((used // outs, 6, rows, width), F32)] * outs,
-            in_specs=[pl.BlockSpec(memory_space=pltpu.SMEM)] + [whole] * len(operands),
+            out_shape=[jax.ShapeDtypeStruct((count, 6, rows, width), F32)] * outs,
+            in_specs=[whole] * len(operands),
             out_specs=[whole] * outs,
             scratch_shapes=[
                 pltpu.VMEM((len(tiles), 9 * rows * 24, width), BF16),
@@ -287,16 +338,27 @@
                 flops=8 * 10**9, bytes_accessed=4 * 2**20, transcendentals=0
             ),
             name=name,
-        )(device.reshape(1), *operands)
+        )(*operands)
 
     whole = pl.BlockSpec(memory_space=pltpu.VMEM)
     (middle,) = tensors([8, 16], None, "tensor_middle")
-    middle_above = send(middle, "gz", lambda i: i + 1)
-    middle_below = send(middle, "gz", lambda i: i - 1)
-    first, last = tensors([0, 24], (up, down), "tensor_ends")
-    last_above = send(last, "gz", lambda i: i + 1)
-    first_below = send(first, "gz", lambda i: i - 1)
-    arrays = [middle_above, last_above, first, middle, last, first_below, middle_below]
+    middle, *swaps = lax.optimization_barrier((middle, *swaps))
+    at, beyond = 4 * rows, 5 * rows
+    kept = lax.rem(device, 2) == 0
+    chosen = [jnp.where(kept, x[beyond : beyond + rows], x[at:beyond]) for x in swaps]
+    last_halo = cross(
+        jnp.concatenate(
+            [
+                jnp.where(even, chosen[1], chosen[0]),
+                jnp.where(even, chosen[0], chosen[1]),
+            ],
+            axis=1,
+        )
+    )
+    middle_swaps = depth_swaps(middle, middle)
+    first, last, even_near, even_away = tensors([0, 24], (*swaps, last_halo), "tensor_ends")
+    end_swaps = depth_swaps(even_near, even_away)
+    arrays = [first, middle, last, end_swaps[0], middle_swaps[0], end_swaps[1], middle_swaps[1]]
     starts = [-HALF, -halo, 0, halo, planes - halo, planes, planes + halo]
     shape = jax.ShapeDtypeStruct((planes, rows, width), F32)
     return tuple(

time: 76.4 us -> 70.2 us (0.919)
  starting transfers between devices: 46.9 us -> 39 us
  waiting for transfers between devices: 15.3 us -> 16.5 us
    ppermute x14 -> x15, starting transfers between devices: 46.9 us -> 39 us  [send(): return lax.ppermute(x, axis, pairs)]
    ppermute x14 -> x15, waiting for transfers between devices: 15.3 us -> 16.5 us  [send(): return lax.ppermute(x, axis, pairs)]
  transfers between devices with their start and end apart: 14 -> 15, of which waited for: 5 -> 7; matrix products, arithmetic and copies ran while one was open for 0% -> 0% of each run, Pallas kernels for 13% -> 15%
where the time goes in v3:
time: 70.2 us; the launch traced here: 69.9 us
  starting transfers between devices  39 us (56%)
  waiting for transfers between devices  16.5 us (24%)
  Pallas kernels  12.1 us (17%)
  local copies, waits for them, and re-layouts  1.18 us (2%)
  between operations  0.96 us (1%)
    ppermute x15, starting transfers between devices, send(): return lax.ppermute(x, axis, pairs)  39 us
    ppermute x15, waiting for transfers between devices, send(): return lax.ppermute(x, axis, pairs)  16.5 us
    pallas_call x2, Pallas kernels, tensors(): pl.pallas_call(functools.partial(tensor_kernel, rows, rows * groups, tile...  10.3 us
    pallas_call x1, Pallas kernels, local(): pl.pallas_call(functools.partial(attribute_kernel, planes, width, starts)...  1.76 us
  transfers between devices with their start and end apart: 15, of which 7 were waited for; matrix products, arithmetic and copies ran while one was open for 0% of the time, Pallas kernels for 15%

profile of v3, /device:TPU:25, one launch (start us, length us, event | category | flops | bytes accessed | tf_op | source)
XLA Modules:
  0.0 69.9 jit_solution(8853003729726023225)
XLA Ops:
  0.6 1.0 %copy.13 = f32[32,8,256]{2,0,1:T(8,128)S(1)} copy(f32[32,8,256]{2,1,0:T(8,128)} %param.8) | data formatting | bytes 524288 | tf_op args[0]
  1.7 1.7 %collective-permute-start.1 = (f32[8,32,256]{2,1,0:T(8,128)S(1)}, f32[8,32,256]{2,1,0:T(8,128)S(1)}, u32[]{:S(2)}, u32[]{:S(2)}) collective-permute-start(f32[8,32,256]{2,1,0:T(8,128)S(1)} %bitcast.3), channel_id=1, source_target_pairs={{0,8},{4,12},{8,0},{12,4},{16,24},{20,28},{24,16},{28,20},{32,40},... | collective-permute-start | bytes 786440 | tf_op jit(solution)/shard_map/ppermute | solution.py:262
  3.4 6.7 %collective-permute-start = (f32[8,32,256]{2,1,0:T(8,128)S(1)}, f32[8,32,256]{2,1,0:T(8,128)S(1)}, u32[]{:S(2)}, u32[]{:S(2)}) collective-permute-start(f32[8,32,256]{2,1,0:T(8,128)S(1)} %bitcast.4), channel_id=1, source_target_pairs={{8,16},{12,20},{16,8},{20,12},{24,32},{28,36},{32,24},{36,28},{40,... | collective-permute-start | bytes 786440 | tf_op jit(solution)/shard_map/ppermute | solution.py:262
  10.1 2.8 %collective-permute-start.2 = (f32[8,32,256]{2,1,0:T(8,128)S(1)}, f32[8,32,256]{2,1,0:T(8,128)S(1)}, u32[]{:S(2)}, u32[]{:S(2)}) collective-permute-start(f32[8,32,256]{2,1,0:T(8,128)S(1)} %bitcast.5), channel_id=1, source_target_pairs={{0,4},{4,0},{8,12},{12,8},{16,20},{20,16},{24,28},{28,24},{32,36},... | collective-permute-start | bytes 786440 | tf_op jit(solution)/shard_map/ppermute | solution.py:262
  13.0 0.0 collective-permute-done.1
  13.0 2.8 %collective-permute-done = f32[8,32,256]{2,1,0:T(8,128)S(1)} collective-permute-done((f32[8,32,256]{2,1,0:T(8,128)S(1)}, f32[8,32,256]{2,1,0:T(8,128)S(1)}, u32[]{:S(2)}, u32[]{:S(2)}) %collective-permute-start) | collective-permute-done | bytes 262176 | tf_op jit(solution)/shard_map/ppermute | solution.py:262
  15.9 5.2 %collective-permute-start.3 = (f32[8,32,256]{2,1,0:T(8,128)S(1)}, f32[8,32,256]{2,1,0:T(8,128)S(1)}, u32[]{:S(2)}, u32[]{:S(2)}) collective-permute-start(f32[8,32,256]{2,1,0:T(8,128)S(1)} %collective-permute-done.1), channel_id=1, source_target_pairs={{8,16},{12,20},{16,8},{20,12},{24,32},{28,36},{32,24},{36,28},{40,... | collective-permute-start | bytes 786440 | tf_op jit(solution)/shard_map/ppermute | solution.py:262
  21.1 0.1 collective-permute-start.4
  21.2 0.0 collective-permute-done.2.refs_3_
  21.2 1.5 %collective-permute-start.6 = (f32[8,32,256]{2,1,0:T(8,128)S(1)}, f32[8,32,256]{2,1,0:T(8,128)S(1)}, u32[]{:S(2)}, u32[]{:S(2)}) collective-permute-start(f32[8,32,256]{2,1,0:T(8,128)S(1)} %collective-permute-done.2.refs_3_), channel_id=1, source_target_pairs={{0,8},{4,12},{8,0},{12,4},{16,24},{20,28},{24,16},{28,20},{32,40},... | collective-permute-start | bytes 786440 | tf_op jit(solution)/shard_map/ppermute | solution.py:262
  22.7 2.2 %collective-permute-start.5 = (f32[8,32,256]{2,1,0:T(8,128)S(1)}, f32[8,32,256]{2,1,0:T(8,128)S(1)}, u32[]{:S(2)}, u32[]{:S(2)}) collective-permute-start(f32[8,32,256]{2,1,0:T(8,128)S(1)} %collective-permute-done.2.refs_3_), channel_id=1, source_target_pairs={{8,16},{12,20},{16,8},{20,12},{24,32},{28,36},{32,24},{36,28},{40,... | collective-permute-start | bytes 786440 | tf_op jit(solution)/shard_map/ppermute | solution.py:262
  25.0 1.2 %collective-permute-done.3 = f32[8,32,256]{2,1,0:T(8,128)S(1)} collective-permute-done((f32[8,32,256]{2,1,0:T(8,128)S(1)}, f32[8,32,256]{2,1,0:T(8,128)S(1)}, u32[]{:S(2)}, u32[]{:S(2)}) %collective-permute-start.3) | collective-permute-done | bytes 262176 | tf_op jit(solution)/shard_map/ppermute | solution.py:262
  26.2 0.6 collective-permute-done.4
  26.8 0.1 broadcast_select_fusion.2
  26.9 2.8 %collective-permute-start.7 = (f32[8,32,256]{2,1,0:T(8,128)S(1)}, f32[8,32,256]{2,1,0:T(8,128)S(1)}, u32[]{:S(2)}, u32[]{:S(2)}) collective-permute-start(f32[8,32,256]{2,1,0:T(8,128)S(1)} %get-tuple-element.21), channel_id=1, source_target_pairs={{0,4},{4,0},{8,12},{12,8},{16,20},{20,16},{24,28},{28,24},{32,36},... | collective-permute-start | bytes 786440 | tf_op jit(solution)/shard_map/ppermute | solution.py:262
  29.8 2.7 %collective-permute-done.6 = f32[8,32,256]{2,1,0:T(8,128)S(1)} collective-permute-done((f32[8,32,256]{2,1,0:T(8,128)S(1)}, f32[8,32,256]{2,1,0:T(8,128)S(1)}, u32[]{:S(2)}, u32[]{:S(2)}) %collective-permute-start.6) | collective-permute-done | bytes 262176 | tf_op jit(solution)/shard_map/ppermute | solution.py:262
  32.4 0.0 collective-permute-done.5
  32.5 0.0 copy-start
  32.5 0.0 copy-start.1
  32.5 0.0 copy-start.2
  32.6 0.0 copy-start.3
  32.6 0.0 copy-start.4
  32.6 0.0 copy-start.5
  32.6 0.0 copy-start.6
  32.6 0.1 broadcast_select_fusion
  32.7 6.5 %collective-permute-start.9 = (f32[64,8,256]{2,1,0:T(8,128)S(1)}, f32[64,8,256]{2,1,0:T(8,128)S(1)}, u32[]{:S(2)}, u32[]{:S(2)}) collective-permute-start(f32[64,8,256]{2,1,0:T(8,128)S(1)} %get-tuple-element.19), channel_id=1, source_target_pairs={{1,2},{2,1},{5,6},{6,5},{9,10},{10,9},{13,14},{14,13},{17,18},{18,... | collective-permute-start | bytes 1572872 | tf_op jit(solution)/shard_map/ppermute | solution.py:262
  39.2 0.1 collective-permute-start.8
  39.3 0.0 collective-permute-done.7.refs_8_
  39.3 0.0 copy-done
  39.3 0.0 copy-done.1
  39.3 0.0 copy-done.2
  39.3 0.0 copy-done.3
  39.4 0.0 copy-done.4
  39.4 5.0 %tensor_middle.1.refs_1_ = f32[16,6,8,256]{3,2,1,0:T(8,128)S(1)} custom-call(f32[8,32,256]{2,1,0:T(8,128)S(1)} %bitcast.7, f32[8,32,256]{2,1,0:T(8,128)S(1)} %get-tuple-element.27.refs_1_, f32[8,32,256]{2,1,0:T(8,128)S(1)} %get-tuple-element.26.refs_2_, f32[8,32,256]{2,1,0:T(8,128)S(1)} %collective-permute-done.2.refs_3_, ...), custom_call_target="tpu_custom_call" | custom-call | flops 8000000000 | bytes 4194304 | tf_op jit(solution)/shard_map/tensor_middle/pallas_call | solution.py:320
  44.4 1.7 %collective-permute-done.9.refs_10_ = f32[64,8,256]{2,1,0:T(8,128)S(1)} collective-permute-done((f32[64,8,256]{2,1,0:T(8,128)S(1)}, f32[64,8,256]{2,1,0:T(8,128)S(1)}, u32[]{:S(2)}, u32[]{:S(2)}) %collective-permute-start.9) | collective-permute-done | bytes 524320 | tf_op jit(solution)/shard_map/ppermute | solution.py:262
  46.1 0.0 collective-permute-done.8.refs_9_
  46.1 2.5 %collective-permute-start.10 = (f32[8,16,256]{2,1,0:T(8,128)S(1)}, f32[8,16,256]{2,1,0:T(8,128)S(1)}, u32[]{:S(2)}, u32[]{:S(2)}) collective-permute-start(f32[8,16,256]{2,1,0:T(8,128)S(1)} %pad_maximum_fusion), channel_id=1, source_target_pairs={{0,4},{4,0},{8,12},{12,8},{16,20},{20,16},{24,28},{28,24},{32,36},... | collective-permute-start | bytes 393224 | tf_op jit(solution)/shard_map/ppermute | solution.py:262
  48.6 3.3 %collective-permute-start.14 = (f32[16,6,8,256]{3,2,1,0:T(8,128)S(1)}, f32[16,6,8,256]{3,2,1,0:T(8,128)S(1)}, u32[]{:S(2)}, u32[]{:S(2)}) collective-permute-start(f32[16,6,8,256]{3,2,1,0:T(8,128)S(1)} %tensor_middle.1.refs_1_), channel_id=1, source_target_pairs={{1,2},{2,1},{5,6},{6,5},{9,10},{10,9},{13,14},{14,13},{17,18},{18,... | collective-permute-start | bytes 2359304 | tf_op jit(solution)/shard_map/ppermute | solution.py:262
  52.0 0.1 collective-permute-start.12
  52.1 1.1 %collective-permute-done.10.refs_11_ = f32[8,16,256]{2,1,0:T(8,128)S(1)} collective-permute-done((f32[8,16,256]{2,1,0:T(8,128)S(1)}, f32[8,16,256]{2,1,0:T(8,128)S(1)}, u32[]{:S(2)}, u32[]{:S(2)}) %collective-permute-start.10) | collective-permute-done | bytes 131104 | tf_op jit(solution)/shard_map/ppermute | solution.py:262
  53.1 5.3 %tensor_ends.1 = (f32[8,6,8,256]{3,2,1,0:T(8,128)S(1)}, f32[8,6,8,256]{3,2,1,0:T(8,128)S(1)}, f32[8,6,8,256]{3,2,1,0:T(8,128)S(1)}, f32[8,6,8,256]{3,2,1,0:T(8,128)S(1)}) custom-call(f32[8,32,256]{2,1,0:T(8,128)S(1)} %bitcast.8, f32[8,32,256]{2,1,0:T(8,128)S(1)} %get-tuple-element.27.refs_1_, f32[8,32,256]{2,1,0:T(8,128)S(1)} %get-tuple-element.26.refs_2_, ...), custom_call_target="tpu_custom_call" | custom-call | flops 8000000000 | bytes 4194304 | tf_op jit(solution)/shard_map/tensor_ends/pallas_call | solution.py:320
  58.5 0.6 collective-permute-start.11
  59.1 2.7 %collective-permute-start.13 = (f32[8,6,8,256]{3,2,1,0:T(8,128)S(1)}, f32[8,6,8,256]{3,2,1,0:T(8,128)S(1)}, u32[]{:S(2)}, u32[]{:S(2)}) collective-permute-start(f32[8,6,8,256]{3,2,1,0:T(8,128)S(1)} %get-tuple-element.16), channel_id=1, source_target_pairs={{1,2},{2,1},{5,6},{6,5},{9,10},{10,9},{13,14},{14,13},{17,18},{18,... | collective-permute-start | bytes 1179656 | tf_op jit(solution)/shard_map/ppermute | solution.py:262
  61.8 0.0 collective-permute-done.11.refs_3_
  61.8 6.4 %collective-permute-done.13.refs_5_ = f32[8,6,8,256]{3,2,1,0:T(8,128)S(1)} collective-permute-done((f32[8,6,8,256]{3,2,1,0:T(8,128)S(1)}, f32[8,6,8,256]{3,2,1,0:T(8,128)S(1)}, u32[]{:S(2)}, u32[]{:S(2)}) %collective-permute-start.13) | collective-permute-done | bytes 393248 | tf_op jit(solution)/shard_map/ppermute | solution.py:262
  68.1 0.0 collective-permute-done.14.refs_6_
  68.1 0.0 collective-permute-done.12.refs_4_
  68.1 1.8 %attributes.1 = (f32[32,8,256]{2,1,0:T(8,128)}, f32[32,8,256]{2,1,0:T(8,128)}, f32[32,8,256]{2,1,0:T(8,128)}) custom-call(f32[8,6,8,256]{3,2,1,0:T(8,128)S(1)} %get-tuple-element.12.refs_0_, f32[16,6,8,256]{3,2,1,0:T(8,128)S(1)} %tensor_middle.1.refs_1_, f32[8,6,8,256]{3,2,1,0:T(8,128)S(1)} %get-tuple-element.14.refs_2_, ...), custom_call_target="tpu_custom_call" | custom-call | tf_op jit(solution)/shard_map/attributes/pallas_call | solution.py:365
  (14 shorter events, 0.2 us)
Async XLA Ops:
  1.7 11.3 %collective-permute-start.1 = (f32[8,32,256]{2,1,0:T(8,128)S(1)}, f32[8,32,256]{2,1,0:T(8,128)S(1)}, u32[]{:S(2)}, u32[]{:S(2)}) collective-permute-start(f32[8,32,256]{2,1,0:T(8,128)S(1)} %bitcast.3), channel_id=1, source_target_pairs={{0,8},{4,12},{8,0},{12,4},{16,24},{20,28},{24,16},{28,20},{32,40},... | collective-permute-start | bytes 786440 | tf_op jit(solution)/shard_map/ppermute | solution.py:262
  3.4 12.4 %collective-permute-start = (f32[8,32,256]{2,1,0:T(8,128)S(1)}, f32[8,32,256]{2,1,0:T(8,128)S(1)}, u32[]{:S(2)}, u32[]{:S(2)}) collective-permute-start(f32[8,32,256]{2,1,0:T(8,128)S(1)} %bitcast.4), channel_id=1, source_target_pairs={{8,16},{12,20},{16,8},{20,12},{24,32},{28,36},{32,24},{36,28},{40,... | collective-permute-start | bytes 786440 | tf_op jit(solution)/shard_map/ppermute | solution.py:262
  10.1 11.1 %collective-permute-start.2 = (f32[8,32,256]{2,1,0:T(8,128)S(1)}, f32[8,32,256]{2,1,0:T(8,128)S(1)}, u32[]{:S(2)}, u32[]{:S(2)}) collective-permute-start(f32[8,32,256]{2,1,0:T(8,128)S(1)} %bitcast.5), channel_id=1, source_target_pairs={{0,4},{4,0},{8,12},{12,8},{16,20},{20,16},{24,28},{28,24},{32,36},... | collective-permute-start | bytes 786440 | tf_op jit(solution)/shard_map/ppermute | solution.py:262
  15.9 10.3 %collective-permute-start.3 = (f32[8,32,256]{2,1,0:T(8,128)S(1)}, f32[8,32,256]{2,1,0:T(8,128)S(1)}, u32[]{:S(2)}, u32[]{:S(2)}) collective-permute-start(f32[8,32,256]{2,1,0:T(8,128)S(1)} %collective-permute-done.1), channel_id=1, source_target_pairs={{8,16},{12,20},{16,8},{20,12},{24,32},{28,36},{32,24},{36,28},{40,... | collective-permute-start | bytes 786440 | tf_op jit(solution)/shard_map/ppermute | solution.py:262
  21.1 5.7 %collective-permute-start.4 = (f32[8,32,256]{2,1,0:T(8,128)S(1)}, f32[8,32,256]{2,1,0:T(8,128)S(1)}, u32[]{:S(2)}, u32[]{:S(2)}) collective-permute-start(f32[8,32,256]{2,1,0:T(8,128)S(1)} %collective-permute-done), channel_id=1, source_target_pairs={{0,8},{4,12},{8,0},{12,4},{16,24},{20,28},{24,16},{28,20},{32,40},... | collective-permute-start | bytes 786440 | tf_op jit(solution)/shard_map/ppermute | solution.py:262
  21.2 11.2 %collective-permute-start.6 = (f32[8,32,256]{2,1,0:T(8,128)S(1)}, f32[8,32,256]{2,1,0:T(8,128)S(1)}, u32[]{:S(2)}, u32[]{:S(2)}) collective-permute-start(f32[8,32,256]{2,1,0:T(8,128)S(1)} %collective-permute-done.2.refs_3_), channel_id=1, source_target_pairs={{0,8},{4,12},{8,0},{12,4},{16,24},{20,28},{24,16},{28,20},{32,40},... | collective-permute-start | bytes 786440 | tf_op jit(solution)/shard_map/ppermute | solution.py:262
  22.7 9.7 %collective-permute-start.5 = (f32[8,32,256]{2,1,0:T(8,128)S(1)}, f32[8,32,256]{2,1,0:T(8,128)S(1)}, u32[]{:S(2)}, u32[]{:S(2)}) collective-permute-start(f32[8,32,256]{2,1,0:T(8,128)S(1)} %collective-permute-done.2.refs_3_), channel_id=1, source_target_pairs={{8,16},{12,20},{16,8},{20,12},{24,32},{28,36},{32,24},{36,28},{40,... | collective-permute-start | bytes 786440 | tf_op jit(solution)/shard_map/ppermute | solution.py:262
  26.9 12.4 %collective-permute-start.7 = (f32[8,32,256]{2,1,0:T(8,128)S(1)}, f32[8,32,256]{2,1,0:T(8,128)S(1)}, u32[]{:S(2)}, u32[]{:S(2)}) collective-permute-start(f32[8,32,256]{2,1,0:T(8,128)S(1)} %get-tuple-element.21), channel_id=1, source_target_pairs={{0,4},{4,0},{8,12},{12,8},{16,20},{20,16},{24,28},{28,24},{32,36},... | collective-permute-start | bytes 786440 | tf_op jit(solution)/shard_map/ppermute | solution.py:262
  32.5 6.8 %copy-start = (bf16[384,480]{1,0:T(8,128)(2,1)S(1)}, bf16[384,480]{1,0:T(8,128)(2,1)}, u32[]{:S(2)}) copy-start(bf16[384,480]{1,0:T(8,128)(2,1)} %constant.50.clone.refs_9_.refs_12_) | copy-start | bytes 1105924
  32.5 6.8 %copy-start.1 = (bf16[256,256]{1,0:T(8,128)(2,1)S(1)}, bf16[256,256]{1,0:T(8,128)(2,1)}, u32[]{:S(2)}) copy-start(bf16[256,256]{1,0:T(8,128)(2,1)} %constant.49.clone.refs_15_.refs_18_) | copy-start | bytes 393220
  32.5 6.8 %copy-start.2 = (bf16[256,256]{1,0:T(8,128)(2,1)S(1)}, bf16[256,256]{1,0:T(8,128)(2,1)}, u32[]{:S(2)}) copy-start(bf16[256,256]{1,0:T(8,128)(2,1)} %constant.48.clone.refs_14_.refs_17_) | copy-start | bytes 393220
  32.6 6.8 %copy-start.3 = (bf16[256,256]{1,0:T(8,128)(2,1)S(1)}, bf16[256,256]{1,0:T(8,128)(2,1)}, u32[]{:S(2)}) copy-start(bf16[256,256]{1,0:T(8,128)(2,1)} %constant.47.clone.refs_13_.refs_16_) | copy-start | bytes 393220
  32.6 6.8 %copy-start.4 = (bf16[256,256]{1,0:T(8,128)(2,1)S(1)}, bf16[256,256]{1,0:T(8,128)(2,1)}, u32[]{:S(2)}) copy-start(bf16[256,256]{1,0:T(8,128)(2,1)} %constant.46.clone.refs_12_.refs_15_) | copy-start | bytes 393220
  32.6 6.8 %copy-start.5 = (bf16[256,256]{1,0:T(8,128)(2,1)S(1)}, bf16[256,256]{1,0:T(8,128)(2,1)}, u32[]{:S(2)}) copy-start(bf16[256,256]{1,0:T(8,128)(2,1)} %constant.45.clone.refs_11_.refs_14_) | copy-start | bytes 393220
  32.6 6.8 %copy-start.6 = (bf16[256,256]{1,0:T(8,128)(2,1)S(1)}, bf16[256,256]{1,0:T(8,128)(2,1)}, u32[]{:S(2)}) copy-start(bf16[256,256]{1,0:T(8,128)(2,1)} %constant.44.clone.refs_10_.refs_13_) | copy-start | bytes 393220
  32.7 13.4 %collective-permute-start.9 = (f32[64,8,256]{2,1,0:T(8,128)S(1)}, f32[64,8,256]{2,1,0:T(8,128)S(1)}, u32[]{:S(2)}, u32[]{:S(2)}) collective-permute-start(f32[64,8,256]{2,1,0:T(8,128)S(1)} %get-tuple-element.19), channel_id=1, source_target_pairs={{1,2},{2,1},{5,6},{6,5},{9,10},{10,9},{13,14},{14,13},{17,18},{18,... | collective-permute-start | bytes 1572872 | tf_op jit(solution)/shard_map/ppermute | solution.py:262
  39.2 6.9 %collective-permute-start.8 = (f32[64,8,256]{2,1,0:T(8,128)S(1)}, f32[64,8,256]{2,1,0:T(8,128)S(1)}, u32[]{:S(2)}, u32[]{:S(2)}) collective-permute-start(f32[64,8,256]{2,1,0:T(8,128)S(1)} %get-tuple-element.20), channel_id=1, source_target_pairs={{0,1},{1,0},{2,3},{3,2},{4,5},{5,4},{6,7},{7,6},{8,9},{9,8},{10,11... | collective-permute-start | bytes 1572872 | tf_op jit(solution)/shard_map/ppermute | solution.py:262
  46.1 7.0 %collective-permute-start.10 = (f32[8,16,256]{2,1,0:T(8,128)S(1)}, f32[8,16,256]{2,1,0:T(8,128)S(1)}, u32[]{:S(2)}, u32[]{:S(2)}) collective-permute-start(f32[8,16,256]{2,1,0:T(8,128)S(1)} %pad_maximum_fusion), channel_id=1, source_target_pairs={{0,4},{4,0},{8,12},{12,8},{16,20},{20,16},{24,28},{28,24},{32,36},... | collective-permute-start | bytes 393224 | tf_op jit(solution)/shard_map/ppermute | solution.py:262
  48.6 19.5 %collective-permute-start.14 = (f32[16,6,8,256]{3,2,1,0:T(8,128)S(1)}, f32[16,6,8,256]{3,2,1,0:T(8,128)S(1)}, u32[]{:S(2)}, u32[]{:S(2)}) collective-permute-start(f32[16,6,8,256]{3,2,1,0:T(8,128)S(1)} %tensor_middle.1.refs_1_), channel_id=1, source_target_pairs={{1,2},{2,1},{5,6},{6,5},{9,10},{10,9},{13,14},{14,13},{17,18},{18,... | collective-permute-start | bytes 2359304 | tf_op jit(solution)/shard_map/ppermute | solution.py:262
  52.0 16.2 %collective-permute-start.12 = (f32[16,6,8,256]{3,2,1,0:T(8,128)S(1)}, f32[16,6,8,256]{3,2,1,0:T(8,128)S(1)}, u32[]{:S(2)}, u32[]{:S(2)}) collective-permute-start(f32[16,6,8,256]{3,2,1,0:T(8,128)S(1)} %tensor_middle.1.refs_1_), channel_id=1, source_target_pairs={{0,1},{1,0},{2,3},{3,2},{4,5},{5,4},{6,7},{7,6},{8,9},{9,8},{10,11... | collective-permute-start | bytes 2359304 | tf_op jit(solution)/shard_map/ppermute | solution.py:262
  58.5 3.3 %collective-permute-start.11 = (f32[8,6,8,256]{3,2,1,0:T(8,128)S(1)}, f32[8,6,8,256]{3,2,1,0:T(8,128)S(1)}, u32[]{:S(2)}, u32[]{:S(2)}) collective-permute-start(f32[8,6,8,256]{3,2,1,0:T(8,128)S(1)} %get-tuple-element.15), channel_id=1, source_target_pairs={{0,1},{1,0},{2,3},{3,2},{4,5},{5,4},{6,7},{7,6},{8,9},{9,8},{10,11... | collective-permute-start | bytes 1179656 | tf_op jit(solution)/shard_map/ppermute | solution.py:262
  59.1 9.1 %collective-permute-start.13 = (f32[8,6,8,256]{3,2,1,0:T(8,128)S(1)}, f32[8,6,8,256]{3,2,1,0:T(8,128)S(1)}, u32[]{:S(2)}, u32[]{:S(2)}) collective-permute-start(f32[8,6,8,256]{3,2,1,0:T(8,128)S(1)} %get-tuple-element.16), channel_id=1, source_target_pairs={{1,2},{2,1},{5,6},{6,5},{9,10},{10,9},{13,14},{14,13},{17,18},{18,... | collective-permute-start | bytes 1179656 | tf_op jit(solution)/shard_map/ppermute | solution.py:262

commit v4 on v3

--- a/solution.py
+++ b/solution.py
@@ -92,10 +92,9 @@
 def tensor_kernel(rows, total_rows, tiles, width, halos, *refs):
     blocks, refs = refs[:9], refs[9:]
     if halos:
-        swaps, last_halo = refs[:2], refs[2]
-        refs = refs[3:]
+        halo, refs = refs[0], refs[1:]
     taps, wd_high, wd_low, wg_high, wg_low, ws_high, ws_low = refs[:7]
-    outs = refs[7 : 7 + (4 if halos else 1)]
+    out = refs[7]
     raw_high, raw_low, pre_high, pre_low, grads, part, ty = refs[-7:]
     count = len(tiles)
     planes = 8 * count
@@ -113,18 +112,16 @@
         raw_high[n, at, :] = high
         raw_low[n, at, :] = low
 
-    def stage_ends(up, down):
+    def stage_end(first):
         for i, (block, place) in enumerate(zip(blocks, places)):
-            at = slice(i * rows, (i + 1) * rows)
-            last = i == len(blocks) - 1
-            above = last_halo[:, :8] if last else up[at]
-            below = last_halo[:, 8:] if last else down[at]
-            stage(0, place, jnp.concatenate([above, block[:, :16]], axis=1))
-            stage(1, place, jnp.concatenate([block[:, -16:], below], axis=1))
+            beyond = halo[i * rows : (i + 1) * rows]
+            parts = [beyond, block[:, :16]] if first else [block[:, -16:], beyond]
+            stage(0, place, jnp.concatenate(parts, axis=1))
 
     if halos:
-        pl.when(even_depth)(lambda: stage_ends(swaps[1], swaps[0]))
-        pl.when(jnp.logical_not(even_depth))(lambda: stage_ends(swaps[0], swaps[1]))
+        upper = even_depth if halos == "away" else jnp.logical_not(even_depth)
+        pl.when(upper)(lambda: stage_end(True))
+        pl.when(jnp.logical_not(upper))(lambda: stage_end(False))
     else:
         for n, plane in enumerate(tiles):
             for block, place in zip(blocks, places):
@@ -193,30 +190,24 @@
     for f in range(6):
         held = jnp.concatenate([ty[h, f] for h in range(width // 128)], axis=1)
         field = dot3(held, ws_high[...], ws_low[...]).reshape(planes, rows, width)
-        if not halos:
-            outs[0][:, f] = field
-            continue
-        first, last = field[:8], field[8:]
-        outs[0][:, f] = first
-        outs[1][:, f] = last
-        outs[2][:, f] = jnp.where(even_depth, last, first)
-        outs[3][:, f] = jnp.where(even_depth, first, last)
+        out[:, f] = field
 
 
 def attribute_kernel(planes, width, pieces, *refs):
     inline, cross, coherent, part = refs[-4:]
-    first, middle, last, ends_a, middle_a, ends_b, middle_b = refs[:7]
+    middle, end_near, end_away, ends_a, middle_a, ends_b, middle_b = refs[:7]
     even_depth = lax.rem(lax.axis_index("gz"), 2) == 0
     results = (inline, cross, coherent, part)
-    own = (first, middle, last)
     pl.when(even_depth)(
         lambda: attributes(
-            planes, width, pieces, (middle_b, ends_b, *own, ends_a, middle_a), *results
+            planes, width, pieces,
+            (middle_b, ends_b, end_away, middle, end_near, ends_a, middle_a), *results
         )
     )
     pl.when(jnp.logical_not(even_depth))(
         lambda: attributes(
-            planes, width, pieces, (middle_a, ends_a, *own, ends_b, middle_b), *results
+            planes, width, pieces,
+            (middle_a, ends_a, end_near, middle, end_away, ends_b, middle_b), *results
         )
     )
 
@@ -279,10 +270,11 @@
     def away(x):
         return send(x, "pa", lambda i: i - 2 if i % 4 < 2 else i + 2)
 
-    def depth_swaps(even_near, even_away):
-        one = send(even_near, "gz", lambda i: i ^ 1)
-        two = send(even_away, "gz", lambda i: i - 1 if i % 2 == 0 else i + 1)
-        return one, two
+    def depth_near(x):
+        return send(x, "gz", lambda i: i ^ 1)
+
+    def depth_away(x):
+        return send(x, "gz", lambda i: i - 1 if i % 2 == 0 else i + 1)
 
     def ordered(one, two):
         return jnp.where(low, two, one), jnp.where(low, one, two)
@@ -294,14 +286,12 @@
     near_other, away_other = near(other), away(other)
     last_far = cross(jnp.where(turn, near_far, away_far))
     pieces = [own, *ordered(near_own, away_own), other, *ordered(near_far, away_far)]
-    pieces += ordered(near_other, away_other)
+    pieces += [*ordered(near_other, away_other), last_far]
     last_planes = jnp.concatenate([x[:, planes - halo :] for x in pieces], axis=0)
     first_planes = jnp.concatenate([x[:, :halo] for x in pieces], axis=0)
     even = depth == 0
-    swaps = depth_swaps(
-        jnp.where(even, last_planes, first_planes), jnp.where(even, first_planes, last_planes)
-    )
-    pieces.append(last_far)
+    swap_away = depth_away(jnp.where(even, first_planes, last_planes))
+    swap_near = depth_near(jnp.where(even, last_planes, first_planes))
 
     weights = []
     for matrix in (
@@ -312,18 +302,16 @@
     weights = [jnp.asarray(matrix)] + weights
     outer = rows + 2 * HALF
 
-    def tensors(tiles, halos, name):
+    def tensors(tiles, halos, kind, name):
         used = 8 * len(tiles)
-        outs = 4 if halos else 1
-        count = 8 if halos else used
-        operands = pieces + (list(halos) if halos else []) + weights
+        operands = pieces + halos + weights
         return pl.pallas_call(
             functools.partial(
-                tensor_kernel, rows, rows * groups, tiles, width, bool(halos)
+                tensor_kernel, rows, rows * groups, tiles, width, kind
             ),
-            out_shape=[jax.ShapeDtypeStruct((count, 6, rows, width), F32)] * outs,
+            out_shape=jax.ShapeDtypeStruct((used, 6, rows, width), F32),
             in_specs=[whole] * len(operands),
-            out_specs=[whole] * outs,
+            out_specs=whole,
             scratch_shapes=[
                 pltpu.VMEM((len(tiles), 9 * rows * 24, width), BF16),
                 pltpu.VMEM((len(tiles), 9 * rows * 24, width), BF16),
@@ -341,24 +329,14 @@
         )(*operands)
 
     whole = pl.BlockSpec(memory_space=pltpu.VMEM)
-    (middle,) = tensors([8, 16], None, "tensor_middle")
-    middle, *swaps = lax.optimization_barrier((middle, *swaps))
-    at, beyond = 4 * rows, 5 * rows
-    kept = lax.rem(device, 2) == 0
-    chosen = [jnp.where(kept, x[beyond : beyond + rows], x[at:beyond]) for x in swaps]
-    last_halo = cross(
-        jnp.concatenate(
-            [
-                jnp.where(even, chosen[1], chosen[0]),
-                jnp.where(even, chosen[0], chosen[1]),
-            ],
-            axis=1,
-        )
-    )
-    middle_swaps = depth_swaps(middle, middle)
-    first, last, even_near, even_away = tensors([0, 24], (*swaps, last_halo), "tensor_ends")
-    end_swaps = depth_swaps(even_near, even_away)
-    arrays = [first, middle, last, end_swaps[0], middle_swaps[0], end_swaps[1], middle_swaps[1]]
+    middle = tensors([8, 16], [], None, "tensor_middle")
+    middle_away = depth_away(middle)
+    middle_near = depth_near(middle)
+    end_away = tensors([0], [swap_away], "away", "tensor_away")
+    from_away = depth_away(end_away)
+    end_near = tensors([0], [swap_near], "near", "tensor_near")
+    from_near = depth_near(end_near)
+    arrays = [middle, end_near, end_away, from_near, middle_near, from_away, middle_away]
     starts = [-HALF, -halo, 0, halo, planes - halo, planes, planes + halo]
     shape = jax.ShapeDtypeStruct((planes, rows, width), F32)
     return tuple(

time: 70.2 us -> 67.8 us (0.966)
  starting transfers between devices: 39 us -> 36.1 us
    ppermute x15 -> x14, starting transfers between devices: 39 us -> 36.1 us  [send(): return lax.ppermute(x, axis, pairs)]
    pallas_call x2 -> x3, Pallas kernels: 10.3 us -> 10.9 us  [tensors(): pl.pallas_call(functools.partial(tensor_kernel, rows, rows * groups, tile...]
    ppermute x15 -> x14, waiting for transfers between devices: 16.5 us -> 16.4 us  [send(): return lax.ppermute(x, axis, pairs)]
  transfers between devices with their start and end apart: 15 -> 14, of which waited for: 7 -> 9; matrix products, arithmetic and copies ran while one was open for 0% -> 0% of each run, Pallas kernels for 15% -> 16%
where the time goes in v4:
time: 67.8 us; the launch traced here: 67.5 us
  starting transfers between devices  36.1 us (53%)
  waiting for transfers between devices  16.4 us (24%)
  Pallas kernels  12.6 us (19%)
  local copies, waits for them, and re-layouts  1.19 us (2%)
  between operations  0.96 us (1%)
    ppermute x14, starting transfers between devices, send(): return lax.ppermute(x, axis, pairs)  36.1 us
    ppermute x14, waiting for transfers between devices, send(): return lax.ppermute(x, axis, pairs)  16.4 us
    pallas_call x3, Pallas kernels, tensors(): pl.pallas_call(functools.partial(tensor_kernel, rows, rows * groups, tile...  10.9 us
    pallas_call x1, Pallas kernels, local(): pl.pallas_call(functools.partial(attribute_kernel, planes, width, starts)...  1.75 us
  transfers between devices with their start and end apart: 14, of which 9 were waited for; matrix products, arithmetic and copies ran while one was open for 0% of the time, Pallas kernels for 16%

profile of v4, /device:TPU:25, one launch (start us, length us, event | category | flops | bytes accessed | tf_op | source)
XLA Modules:
  0.0 67.5 jit_solution(6795616775622152602)
XLA Ops:
  0.6 1.0 %copy.13 = f32[32,8,256]{2,0,1:T(8,128)S(1)} copy(f32[32,8,256]{2,1,0:T(8,128)} %param.8) | data formatting | bytes 524288 | tf_op args[0]
  1.7 7.7 %collective-permute-start = (f32[8,32,256]{2,1,0:T(8,128)S(1)}, f32[8,32,256]{2,1,0:T(8,128)S(1)}, u32[]{:S(2)}, u32[]{:S(2)}) collective-permute-start(f32[8,32,256]{2,1,0:T(8,128)S(1)} %bitcast.3), channel_id=1, source_target_pairs={{8,16},{12,20},{16,8},{20,12},{24,32},{28,36},{32,24},{36,28},{40,... | collective-permute-start | bytes 786440 | tf_op jit(solution)/shard_map/ppermute | solution.py:253
  9.3 0.1 collective-permute-start.1
  9.4 2.8 %collective-permute-start.2 = (f32[8,32,256]{2,1,0:T(8,128)S(1)}, f32[8,32,256]{2,1,0:T(8,128)S(1)}, u32[]{:S(2)}, u32[]{:S(2)}) collective-permute-start(f32[8,32,256]{2,1,0:T(8,128)S(1)} %bitcast.5), channel_id=1, source_target_pairs={{0,4},{4,0},{8,12},{12,8},{16,20},{20,16},{24,28},{28,24},{32,36},... | collective-permute-start | bytes 786440 | tf_op jit(solution)/shard_map/ppermute | solution.py:253
  12.3 3.1 %collective-permute-done = f32[8,32,256]{2,1,0:T(8,128)S(1)} collective-permute-done((f32[8,32,256]{2,1,0:T(8,128)S(1)}, f32[8,32,256]{2,1,0:T(8,128)S(1)}, u32[]{:S(2)}, u32[]{:S(2)}) %collective-permute-start) | collective-permute-done | bytes 262176 | tf_op jit(solution)/shard_map/ppermute | solution.py:253
  15.4 0.9 %collective-permute-done.1 = f32[8,32,256]{2,1,0:T(8,128)S(1)} collective-permute-done((f32[8,32,256]{2,1,0:T(8,128)S(1)}, f32[8,32,256]{2,1,0:T(8,128)S(1)}, u32[]{:S(2)}, u32[]{:S(2)}) %collective-permute-start.1) | collective-permute-done | bytes 262176 | tf_op jit(solution)/shard_map/ppermute | solution.py:253
  16.4 4.2 %collective-permute-start.3 = (f32[8,32,256]{2,1,0:T(8,128)S(1)}, f32[8,32,256]{2,1,0:T(8,128)S(1)}, u32[]{:S(2)}, u32[]{:S(2)}) collective-permute-start(f32[8,32,256]{2,1,0:T(8,128)S(1)} %collective-permute-done.1), channel_id=1, source_target_pairs={{8,16},{12,20},{16,8},{20,12},{24,32},{28,36},{32,24},{36,28},{40,... | collective-permute-start | bytes 786440 | tf_op jit(solution)/shard_map/ppermute | solution.py:253
  20.6 0.1 collective-permute-start.4
  20.7 0.0 collective-permute-done.2.refs_3_
  20.7 3.2 %collective-permute-start.5 = (f32[8,32,256]{2,1,0:T(8,128)S(1)}, f32[8,32,256]{2,1,0:T(8,128)S(1)}, u32[]{:S(2)}, u32[]{:S(2)}) collective-permute-start(f32[8,32,256]{2,1,0:T(8,128)S(1)} %collective-permute-done.2.refs_3_), channel_id=1, source_target_pairs={{8,16},{12,20},{16,8},{20,12},{24,32},{28,36},{32,24},{36,28},{40,... | collective-permute-start | bytes 786440 | tf_op jit(solution)/shard_map/ppermute | solution.py:253
  23.9 0.3 collective-permute-start.6
  24.2 2.1 %collective-permute-done.3 = f32[8,32,256]{2,1,0:T(8,128)S(1)} collective-permute-done((f32[8,32,256]{2,1,0:T(8,128)S(1)}, f32[8,32,256]{2,1,0:T(8,128)S(1)}, u32[]{:S(2)}, u32[]{:S(2)}) %collective-permute-start.3) | collective-permute-done | bytes 262176 | tf_op jit(solution)/shard_map/ppermute | solution.py:253
  26.3 0.4 collective-permute-done.4
  26.7 0.1 broadcast_select_fusion.2
  26.7 2.8 %collective-permute-start.7 = (f32[8,32,256]{2,1,0:T(8,128)S(1)}, f32[8,32,256]{2,1,0:T(8,128)S(1)}, u32[]{:S(2)}, u32[]{:S(2)}) collective-permute-start(f32[8,32,256]{2,1,0:T(8,128)S(1)} %get-tuple-element.5), channel_id=1, source_target_pairs={{0,4},{4,0},{8,12},{12,8},{16,20},{20,16},{24,28},{28,24},{32,36},... | collective-permute-start | bytes 786440 | tf_op jit(solution)/shard_map/ppermute | solution.py:253
  29.6 3.5 %collective-permute-done.5 = f32[8,32,256]{2,1,0:T(8,128)S(1)} collective-permute-done((f32[8,32,256]{2,1,0:T(8,128)S(1)}, f32[8,32,256]{2,1,0:T(8,128)S(1)}, u32[]{:S(2)}, u32[]{:S(2)}) %collective-permute-start.5) | collective-permute-done | bytes 262176 | tf_op jit(solution)/shard_map/ppermute | solution.py:253
  33.1 0.0 collective-permute-done.6
  33.2 0.6 collective-permute-done.7.refs_8_
  33.8 0.0 copy-start
  33.9 0.0 copy-start.1
  33.9 0.0 copy-start.2
  33.9 0.0 copy-start.3
  33.9 0.0 copy-start.4
  33.9 0.0 copy-start.5
  33.9 0.0 copy-start.6
  33.9 0.1 broadcast_select_fusion
  34.0 9.1 %collective-permute-start.9 = (f32[72,8,256]{2,1,0:T(8,128)S(1)}, f32[72,8,256]{2,1,0:T(8,128)S(1)}, u32[]{:S(2)}, u32[]{:S(2)}) collective-permute-start(f32[72,8,256]{2,1,0:T(8,128)S(1)} %get-tuple-element.3), channel_id=1, source_target_pairs={{1,2},{2,1},{5,6},{6,5},{9,10},{10,9},{13,14},{14,13},{17,18},{18,... | collective-permute-start | bytes 1769480 | tf_op jit(solution)/shard_map/ppermute | solution.py:253
  43.1 0.0 copy-done
  43.1 0.0 copy-done.1
  43.1 0.0 copy-done.2
  43.1 0.0 copy-done.3
  43.1 0.0 copy-done.4
  43.1 0.0 copy-done.5
  43.2 5.0 %tensor_middle.1.refs_0_ = f32[16,6,8,256]{3,2,1,0:T(8,128)S(1)} custom-call(f32[8,32,256]{2,1,0:T(8,128)S(1)} %bitcast.7, f32[8,32,256]{2,1,0:T(8,128)S(1)} %get-tuple-element.11.refs_1_, f32[8,32,256]{2,1,0:T(8,128)S(1)} %get-tuple-element.10.refs_2_, f32[8,32,256]{2,1,0:T(8,128)S(1)} %collective-permute-done.2.refs_3_, ...), custom_call_target="tpu_custom_call" | custom-call | flops 8000000000 | bytes 4194304 | tf_op jit(solution)/shard_map/tensor_middle/pallas_call | solution.py:308
  48.2 0.1 collective-permute-start.11
  48.3 1.9 %collective-permute-start.13 = (f32[16,6,8,256]{3,2,1,0:T(8,128)S(1)}, f32[16,6,8,256]{3,2,1,0:T(8,128)S(1)}, u32[]{:S(2)}, u32[]{:S(2)}) collective-permute-start(f32[16,6,8,256]{3,2,1,0:T(8,128)S(1)} %tensor_middle.1.refs_0_), channel_id=1, source_target_pairs={{1,2},{2,1},{5,6},{6,5},{9,10},{10,9},{13,14},{14,13},{17,18},{18,... | collective-permute-start | bytes 2359304 | tf_op jit(solution)/shard_map/ppermute | solution.py:253
  50.2 0.1 collective-permute-start.8
  50.3 0.4 collective-permute-done.9.refs_9_
  50.6 2.9 %tensor_away.1.refs_2_ = f32[8,6,8,256]{3,2,1,0:T(8,128)S(1)} custom-call(f32[8,32,256]{2,1,0:T(8,128)S(1)} %bitcast.8, f32[8,32,256]{2,1,0:T(8,128)S(1)} %get-tuple-element.11.refs_1_, f32[8,32,256]{2,1,0:T(8,128)S(1)} %get-tuple-element.10.refs_2_, f32[8,32,256]{2,1,0:T(8,128)S(1)} %collective-permute-done.2.refs_3_, ...), custom_call_target="tpu_custom_call" | custom-call | flops 8000000000 | bytes 4194304 | tf_op jit(solution)/shard_map/tensor_away/pallas_call | solution.py:308
  53.5 3.6 %collective-permute-start.12 = (f32[8,6,8,256]{3,2,1,0:T(8,128)S(1)}, f32[8,6,8,256]{3,2,1,0:T(8,128)S(1)}, u32[]{:S(2)}, u32[]{:S(2)}) collective-permute-start(f32[8,6,8,256]{3,2,1,0:T(8,128)S(1)} %tensor_away.1.refs_2_), channel_id=1, source_target_pairs={{1,2},{2,1},{5,6},{6,5},{9,10},{10,9},{13,14},{14,13},{17,18},{18,... | collective-permute-start | bytes 1179656 | tf_op jit(solution)/shard_map/ppermute | solution.py:253
  57.1 0.0 collective-permute-done.8.refs_9_
  57.2 3.1 %tensor_near.1.refs_1_ = f32[8,6,8,256]{3,2,1,0:T(8,128)S(1)} custom-call(f32[8,32,256]{2,1,0:T(8,128)S(1)} %bitcast.9, f32[8,32,256]{2,1,0:T(8,128)S(1)} %get-tuple-element.11.refs_1_, f32[8,32,256]{2,1,0:T(8,128)S(1)} %get-tuple-element.10.refs_2_, f32[8,32,256]{2,1,0:T(8,128)S(1)} %collective-permute-done.2.refs_3_, ...), custom_call_target="tpu_custom_call" | custom-call | flops 8000000000 | bytes 4194304 | tf_op jit(solution)/shard_map/tensor_near/pallas_call | solution.py:308
  60.2 0.1 collective-permute-start.10
  60.3 0.0 collective-permute-done.11.refs_4_
  60.3 1.2 %collective-permute-done.13.refs_6_ = f32[16,6,8,256]{3,2,1,0:T(8,128)S(1)} collective-permute-done((f32[16,6,8,256]{3,2,1,0:T(8,128)S(1)}, f32[16,6,8,256]{3,2,1,0:T(8,128)S(1)}, u32[]{:S(2)}, u32[]{:S(2)}) %collective-permute-start.13) | collective-permute-done | bytes 786464 | tf_op jit(solution)/shard_map/ppermute | solution.py:253
  61.6 4.2 %collective-permute-done.12.refs_5_ = f32[8,6,8,256]{3,2,1,0:T(8,128)S(1)} collective-permute-done((f32[8,6,8,256]{3,2,1,0:T(8,128)S(1)}, f32[8,6,8,256]{3,2,1,0:T(8,128)S(1)}, u32[]{:S(2)}, u32[]{:S(2)}) %collective-permute-start.12) | collective-permute-done | bytes 393248 | tf_op jit(solution)/shard_map/ppermute | solution.py:253
  65.8 0.0 collective-permute-done.10.refs_3_
  65.8 1.8 %attributes.1 = (f32[32,8,256]{2,1,0:T(8,128)}, f32[32,8,256]{2,1,0:T(8,128)}, f32[32,8,256]{2,1,0:T(8,128)}) custom-call(f32[16,6,8,256]{3,2,1,0:T(8,128)S(1)} %tensor_middle.1.refs_0_, f32[8,6,8,256]{3,2,1,0:T(8,128)S(1)} %tensor_near.1.refs_1_, f32[8,6,8,256]{3,2,1,0:T(8,128)S(1)} %tensor_away.1.refs_2_, ...), custom_call_target="tpu_custom_call" | custom-call | tf_op jit(solution)/shard_map/attributes/pallas_call | solution.py:343
  (12 shorter events, 0.2 us)
Async XLA Ops:
  1.7 13.7 %collective-permute-start = (f32[8,32,256]{2,1,0:T(8,128)S(1)}, f32[8,32,256]{2,1,0:T(8,128)S(1)}, u32[]{:S(2)}, u32[]{:S(2)}) collective-permute-start(f32[8,32,256]{2,1,0:T(8,128)S(1)} %bitcast.3), channel_id=1, source_target_pairs={{8,16},{12,20},{16,8},{20,12},{24,32},{28,36},{32,24},{36,28},{40,... | collective-permute-start | bytes 786440 | tf_op jit(solution)/shard_map/ppermute | solution.py:253
  9.3 6.9 %collective-permute-start.1 = (f32[8,32,256]{2,1,0:T(8,128)S(1)}, f32[8,32,256]{2,1,0:T(8,128)S(1)}, u32[]{:S(2)}, u32[]{:S(2)}) collective-permute-start(f32[8,32,256]{2,1,0:T(8,128)S(1)} %bitcast.4), channel_id=1, source_target_pairs={{0,8},{4,12},{8,0},{12,4},{16,24},{20,28},{24,16},{28,20},{32,40},... | collective-permute-start | bytes 786440 | tf_op jit(solution)/shard_map/ppermute | solution.py:253
  9.4 11.3 %collective-permute-start.2 = (f32[8,32,256]{2,1,0:T(8,128)S(1)}, f32[8,32,256]{2,1,0:T(8,128)S(1)}, u32[]{:S(2)}, u32[]{:S(2)}) collective-permute-start(f32[8,32,256]{2,1,0:T(8,128)S(1)} %bitcast.5), channel_id=1, source_target_pairs={{0,4},{4,0},{8,12},{12,8},{16,20},{20,16},{24,28},{28,24},{32,36},... | collective-permute-start | bytes 786440 | tf_op jit(solution)/shard_map/ppermute | solution.py:253
  16.4 9.9 %collective-permute-start.3 = (f32[8,32,256]{2,1,0:T(8,128)S(1)}, f32[8,32,256]{2,1,0:T(8,128)S(1)}, u32[]{:S(2)}, u32[]{:S(2)}) collective-permute-start(f32[8,32,256]{2,1,0:T(8,128)S(1)} %collective-permute-done.1), channel_id=1, source_target_pairs={{8,16},{12,20},{16,8},{20,12},{24,32},{28,36},{32,24},{36,28},{40,... | collective-permute-start | bytes 786440 | tf_op jit(solution)/shard_map/ppermute | solution.py:253
  20.6 6.1 %collective-permute-start.4 = (f32[8,32,256]{2,1,0:T(8,128)S(1)}, f32[8,32,256]{2,1,0:T(8,128)S(1)}, u32[]{:S(2)}, u32[]{:S(2)}) collective-permute-start(f32[8,32,256]{2,1,0:T(8,128)S(1)} %collective-permute-done), channel_id=1, source_target_pairs={{0,8},{4,12},{8,0},{12,4},{16,24},{20,28},{24,16},{28,20},{32,40},... | collective-permute-start | bytes 786440 | tf_op jit(solution)/shard_map/ppermute | solution.py:253
  20.7 12.4 %collective-permute-start.5 = (f32[8,32,256]{2,1,0:T(8,128)S(1)}, f32[8,32,256]{2,1,0:T(8,128)S(1)}, u32[]{:S(2)}, u32[]{:S(2)}) collective-permute-start(f32[8,32,256]{2,1,0:T(8,128)S(1)} %collective-permute-done.2.refs_3_), channel_id=1, source_target_pairs={{8,16},{12,20},{16,8},{20,12},{24,32},{28,36},{32,24},{36,28},{40,... | collective-permute-start | bytes 786440 | tf_op jit(solution)/shard_map/ppermute | solution.py:253
  23.9 9.2 %collective-permute-start.6 = (f32[8,32,256]{2,1,0:T(8,128)S(1)}, f32[8,32,256]{2,1,0:T(8,128)S(1)}, u32[]{:S(2)}, u32[]{:S(2)}) collective-permute-start(f32[8,32,256]{2,1,0:T(8,128)S(1)} %collective-permute-done.2.refs_3_), channel_id=1, source_target_pairs={{0,8},{4,12},{8,0},{12,4},{16,24},{20,28},{24,16},{28,20},{32,40},... | collective-permute-start | bytes 786440 | tf_op jit(solution)/shard_map/ppermute | solution.py:253
  26.7 7.1 %collective-permute-start.7 = (f32[8,32,256]{2,1,0:T(8,128)S(1)}, f32[8,32,256]{2,1,0:T(8,128)S(1)}, u32[]{:S(2)}, u32[]{:S(2)}) collective-permute-start(f32[8,32,256]{2,1,0:T(8,128)S(1)} %get-tuple-element.5), channel_id=1, source_target_pairs={{0,4},{4,0},{8,12},{12,8},{16,20},{20,16},{24,28},{28,24},{32,36},... | collective-permute-start | bytes 786440 | tf_op jit(solution)/shard_map/ppermute | solution.py:253
  33.8 9.2 %copy-start = (bf16[384,480]{1,0:T(8,128)(2,1)S(1)}, bf16[384,480]{1,0:T(8,128)(2,1)}, u32[]{:S(2)}) copy-start(bf16[384,480]{1,0:T(8,128)(2,1)} %constant.50.clone.refs_9_.refs_10_) | copy-start | bytes 1105924
  33.9 9.2 %copy-start.1 = (bf16[256,256]{1,0:T(8,128)(2,1)S(1)}, bf16[256,256]{1,0:T(8,128)(2,1)}, u32[]{:S(2)}) copy-start(bf16[256,256]{1,0:T(8,128)(2,1)} %constant.44.clone.refs_10_.refs_11_) | copy-start | bytes 393220
  33.9 9.2 %copy-start.2 = (bf16[256,256]{1,0:T(8,128)(2,1)S(1)}, bf16[256,256]{1,0:T(8,128)(2,1)}, u32[]{:S(2)}) copy-start(bf16[256,256]{1,0:T(8,128)(2,1)} %constant.45.clone.refs_11_.refs_12_) | copy-start | bytes 393220
  33.9 9.2 %copy-start.3 = (bf16[256,256]{1,0:T(8,128)(2,1)S(1)}, bf16[256,256]{1,0:T(8,128)(2,1)}, u32[]{:S(2)}) copy-start(bf16[256,256]{1,0:T(8,128)(2,1)} %constant.46.clone.refs_12_.refs_13_) | copy-start | bytes 393220
  33.9 9.2 %copy-start.4 = (bf16[256,256]{1,0:T(8,128)(2,1)S(1)}, bf16[256,256]{1,0:T(8,128)(2,1)}, u32[]{:S(2)}) copy-start(bf16[256,256]{1,0:T(8,128)(2,1)} %constant.47.clone.refs_13_.refs_14_) | copy-start | bytes 393220
  33.9 9.2 %copy-start.5 = (bf16[256,256]{1,0:T(8,128)(2,1)S(1)}, bf16[256,256]{1,0:T(8,128)(2,1)}, u32[]{:S(2)}) copy-start(bf16[256,256]{1,0:T(8,128)(2,1)} %constant.48.clone.refs_14_.refs_15_) | copy-start | bytes 393220
  33.9 9.2 %copy-start.6 = (bf16[256,256]{1,0:T(8,128)(2,1)S(1)}, bf16[256,256]{1,0:T(8,128)(2,1)}, u32[]{:S(2)}) copy-start(bf16[256,256]{1,0:T(8,128)(2,1)} %constant.49.clone.refs_15_.refs_16_) | copy-start | bytes 393220
  34.0 16.6 %collective-permute-start.9 = (f32[72,8,256]{2,1,0:T(8,128)S(1)}, f32[72,8,256]{2,1,0:T(8,128)S(1)}, u32[]{:S(2)}, u32[]{:S(2)}) collective-permute-start(f32[72,8,256]{2,1,0:T(8,128)S(1)} %get-tuple-element.3), channel_id=1, source_target_pairs={{1,2},{2,1},{5,6},{6,5},{9,10},{10,9},{13,14},{14,13},{17,18},{18,... | collective-permute-start | bytes 1769480 | tf_op jit(solution)/shard_map/ppermute | solution.py:253
  48.2 12.2 %collective-permute-start.11 = (f32[16,6,8,256]{3,2,1,0:T(8,128)S(1)}, f32[16,6,8,256]{3,2,1,0:T(8,128)S(1)}, u32[]{:S(2)}, u32[]{:S(2)}) collective-permute-start(f32[16,6,8,256]{3,2,1,0:T(8,128)S(1)} %tensor_middle.1.refs_0_), channel_id=1, source_target_pairs={{0,1},{1,0},{2,3},{3,2},{4,5},{5,4},{6,7},{7,6},{8,9},{9,8},{10,11... | collective-permute-start | bytes 2359304 | tf_op jit(solution)/shard_map/ppermute | solution.py:253
  48.3 13.3 %collective-permute-start.13 = (f32[16,6,8,256]{3,2,1,0:T(8,128)S(1)}, f32[16,6,8,256]{3,2,1,0:T(8,128)S(1)}, u32[]{:S(2)}, u32[]{:S(2)}) collective-permute-start(f32[16,6,8,256]{3,2,1,0:T(8,128)S(1)} %tensor_middle.1.refs_0_), channel_id=1, source_target_pairs={{1,2},{2,1},{5,6},{6,5},{9,10},{10,9},{13,14},{14,13},{17,18},{18,... | collective-permute-start | bytes 2359304 | tf_op jit(solution)/shard_map/ppermute | solution.py:253
  50.2 7.0 %collective-permute-start.8 = (f32[72,8,256]{2,1,0:T(8,128)S(1)}, f32[72,8,256]{2,1,0:T(8,128)S(1)}, u32[]{:S(2)}, u32[]{:S(2)}) collective-permute-start(f32[72,8,256]{2,1,0:T(8,128)S(1)} %get-tuple-element.4), channel_id=1, source_target_pairs={{0,1},{1,0},{2,3},{3,2},{4,5},{5,4},{6,7},{7,6},{8,9},{9,8},{10,11... | collective-permute-start | bytes 1769480 | tf_op jit(solution)/shard_map/ppermute | solution.py:253
  53.5 12.3 %collective-permute-start.12 = (f32[8,6,8,256]{3,2,1,0:T(8,128)S(1)}, f32[8,6,8,256]{3,2,1,0:T(8,128)S(1)}, u32[]{:S(2)}, u32[]{:S(2)}) collective-permute-start(f32[8,6,8,256]{3,2,1,0:T(8,128)S(1)} %tensor_away.1.refs_2_), channel_id=1, source_target_pairs={{1,2},{2,1},{5,6},{6,5},{9,10},{10,9},{13,14},{14,13},{17,18},{18,... | collective-permute-start | bytes 1179656 | tf_op jit(solution)/shard_map/ppermute | solution.py:253
  60.2 5.6 %collective-permute-start.10 = (f32[8,6,8,256]{3,2,1,0:T(8,128)S(1)}, f32[8,6,8,256]{3,2,1,0:T(8,128)S(1)}, u32[]{:S(2)}, u32[]{:S(2)}) collective-permute-start(f32[8,6,8,256]{3,2,1,0:T(8,128)S(1)} %tensor_near.1.refs_1_), channel_id=1, source_target_pairs={{0,1},{1,0},{2,3},{3,2},{4,5},{5,4},{6,7},{7,6},{8,9},{9,8},{10,11... | collective-permute-start | bytes 1179656 | tf_op jit(solution)/shard_map/ppermute | solution.py:253

commit v5 on v4

--- a/solution.py
+++ b/solution.py
@@ -92,12 +92,13 @@
 def tensor_kernel(rows, total_rows, tiles, width, halos, *refs):
     blocks, refs = refs[:9], refs[9:]
     if halos:
-        halo, refs = refs[0], refs[1:]
+        count, upper_side = halos
+        halo, refs = refs[:count], refs[count:]
     taps, wd_high, wd_low, wg_high, wg_low, ws_high, ws_low = refs[:7]
     out = refs[7]
     raw_high, raw_low, pre_high, pre_low, grads, part, ty = refs[-7:]
-    count = len(tiles)
-    planes = 8 * count
+    tile_count = len(tiles)
+    planes = 8 * tile_count
     device = lax.axis_index("pa")
     side = 1 - 2 * lax.rem(device, 2)
     even_depth = lax.rem(lax.axis_index("gz"), 2) == 0
@@ -114,12 +115,13 @@
 
     def stage_end(first):
         for i, (block, place) in enumerate(zip(blocks, places)):
-            beyond = halo[i * rows : (i + 1) * rows]
+            part, at = (halo[0], i) if i < 4 or count == 1 else (halo[1], i - 4)
+            beyond = part[at * rows : (at + 1) * rows]
             parts = [beyond, block[:, :16]] if first else [block[:, -16:], beyond]
             stage(0, place, jnp.concatenate(parts, axis=1))
 
     if halos:
-        upper = even_depth if halos == "away" else jnp.logical_not(even_depth)
+        upper = even_depth if upper_side == "away" else jnp.logical_not(even_depth)
         pl.when(upper)(lambda: stage_end(True))
         pl.when(jnp.logical_not(upper))(lambda: stage_end(False))
     else:
@@ -130,7 +132,7 @@
     group = 8
     size = group * 8
     reach = (group + 2 * GHALF) * span
-    for n in range(count):
+    for n in range(tile_count):
         for start in range(0, outer, group):
             at = (start + trim) * span
             high, low = raw_high[n, at : at + reach, :], raw_low[n, at : at + reach, :]
@@ -147,7 +149,7 @@
     for f, (w_high, w_low) in enumerate(
         ((wd_high, wd_low), (wg_high, wg_low), (wg_high, wg_low))
     ):
-        for n in range(count):
+        for n in range(tile_count):
             at = slice(n * outer * 8, (n + 1) * outer * 8)
             high, low = pre_high[f, at, :], pre_low[f, at, :]
             result = dot(high, w_high[...]) + (dot(high, w_low[...]) + dot(low, w_high[...]))
@@ -185,7 +187,7 @@
                     ]
             return carry
 
-        lax.fori_loop(0, count, average_rows, 0)
+        lax.fori_loop(0, tile_count, average_rows, 0)
 
     for f in range(6):
         held = jnp.concatenate([ty[h, f] for h in range(width // 128)], axis=1)
@@ -287,11 +289,14 @@
     last_far = cross(jnp.where(turn, near_far, away_far))
     pieces = [own, *ordered(near_own, away_own), other, *ordered(near_far, away_far)]
     pieces += [*ordered(near_other, away_other), last_far]
-    last_planes = jnp.concatenate([x[:, planes - halo :] for x in pieces], axis=0)
-    first_planes = jnp.concatenate([x[:, :halo] for x in pieces], axis=0)
+    def end_planes(blocks, first):
+        upper = jnp.concatenate([x[:, :halo] for x in blocks], axis=0)
+        lower = jnp.concatenate([x[:, planes - halo :] for x in blocks], axis=0)
+        return jnp.where(first, upper, lower)
+
     even = depth == 0
-    swap_away = depth_away(jnp.where(even, first_planes, last_planes))
-    swap_near = depth_near(jnp.where(even, last_planes, first_planes))
+    swap_away = [depth_away(end_planes(x, even)) for x in (pieces[:4], pieces[4:])]
+    swap_near = [depth_near(end_planes(pieces, jnp.logical_not(even)))]
 
     weights = []
     for matrix in (
@@ -332,9 +337,9 @@
     middle = tensors([8, 16], [], None, "tensor_middle")
     middle_away = depth_away(middle)
     middle_near = depth_near(middle)
-    end_away = tensors([0], [swap_away], "away", "tensor_away")
+    end_away = tensors([0], swap_away, (2, "away"), "tensor_away")
     from_away = depth_away(end_away)
-    end_near = tensors([0], [swap_near], "near", "tensor_near")
+    end_near = tensors([0], swap_near, (1, "near"), "tensor_near")
     from_near = depth_near(end_near)
     arrays = [middle, end_near, end_away, from_near, middle_near, from_away, middle_away]
     starts = [-HALF, -halo, 0, halo, planes - halo, planes, planes + halo]

time: 67.8 us -> 67 us (0.988)
  starting transfers between devices: 36.1 us -> 34.9 us
    ppermute x14 -> x15, starting transfers between devices: 36.1 us -> 34.9 us  [send(): return lax.ppermute(x, axis, pairs)]
    ppermute x14 -> x15, waiting for transfers between devices: 16.4 us -> 16.5 us  [send(): return lax.ppermute(x, axis, pairs)]
  transfers between devices with their start and end apart: 14 -> 15, of which waited for: 9 -> 5; matrix products, arithmetic and copies ran while one was open for 0% -> 1% of each run, Pallas kernels for 16% -> 16%
where the time goes in v5:
time: 67 us; the launch traced here: 66.7 us
  starting transfers between devices  34.9 us (52%)
  waiting for transfers between devices  16.5 us (25%)
  Pallas kernels  12.7 us (19%)
  local copies, waits for them, and re-layouts  1.26 us (2%)
  between operations  0.99 us (1%)
    ppermute x15, starting transfers between devices, send(): return lax.ppermute(x, axis, pairs)  34.9 us
    ppermute x15, waiting for transfers between devices, send(): return lax.ppermute(x, axis, pairs)  16.5 us
    pallas_call x3, Pallas kernels, tensors(): pl.pallas_call(functools.partial(tensor_kernel, rows, rows * groups, tile...  10.9 us
    pallas_call x1, Pallas kernels, local(): pl.pallas_call(functools.partial(attribute_kernel, planes, width, starts)...  1.77 us
  transfers between devices with their start and end apart: 15, of which 5 were waited for; matrix products, arithmetic and copies ran while one was open for 1% of the time, Pallas kernels for 16%

profile of v5, /device:TPU:25, one launch (start us, length us, event | category | flops | bytes accessed | tf_op | source)
XLA Modules:
  0.0 66.7 jit_solution(11600049681573173634)
XLA Ops:
  0.6 1.0 %copy.13 = f32[32,8,256]{2,0,1:T(8,128)S(1)} copy(f32[32,8,256]{2,1,0:T(8,128)} %param.8) | data formatting | bytes 524288 | tf_op args[0]
  1.7 7.7 %collective-permute-start = (f32[8,32,256]{2,1,0:T(8,128)S(1)}, f32[8,32,256]{2,1,0:T(8,128)S(1)}, u32[]{:S(2)}, u32[]{:S(2)}) collective-permute-start(f32[8,32,256]{2,1,0:T(8,128)S(1)} %bitcast.3), channel_id=1, source_target_pairs={{8,16},{12,20},{16,8},{20,12},{24,32},{28,36},{32,24},{36,28},{40,... | collective-permute-start | bytes 786440 | tf_op jit(solution)/shard_map/ppermute | solution.py:255
  9.3 0.1 collective-permute-start.1
  9.4 2.8 %collective-permute-start.2 = (f32[8,32,256]{2,1,0:T(8,128)S(1)}, f32[8,32,256]{2,1,0:T(8,128)S(1)}, u32[]{:S(2)}, u32[]{:S(2)}) collective-permute-start(f32[8,32,256]{2,1,0:T(8,128)S(1)} %bitcast.5), channel_id=1, source_target_pairs={{0,4},{4,0},{8,12},{12,8},{16,20},{20,16},{24,28},{28,24},{32,36},... | collective-permute-start | bytes 786440 | tf_op jit(solution)/shard_map/ppermute | solution.py:255
  12.3 3.1 %collective-permute-done = f32[8,32,256]{2,1,0:T(8,128)S(1)} collective-permute-done((f32[8,32,256]{2,1,0:T(8,128)S(1)}, f32[8,32,256]{2,1,0:T(8,128)S(1)}, u32[]{:S(2)}, u32[]{:S(2)}) %collective-permute-start) | collective-permute-done | bytes 262176 | tf_op jit(solution)/shard_map/ppermute | solution.py:255
  15.4 0.9 %collective-permute-done.1 = f32[8,32,256]{2,1,0:T(8,128)S(1)} collective-permute-done((f32[8,32,256]{2,1,0:T(8,128)S(1)}, f32[8,32,256]{2,1,0:T(8,128)S(1)}, u32[]{:S(2)}, u32[]{:S(2)}) %collective-permute-start.1) | collective-permute-done | bytes 262176 | tf_op jit(solution)/shard_map/ppermute | solution.py:255
  16.4 4.2 %collective-permute-start.3 = (f32[8,32,256]{2,1,0:T(8,128)S(1)}, f32[8,32,256]{2,1,0:T(8,128)S(1)}, u32[]{:S(2)}, u32[]{:S(2)}) collective-permute-start(f32[8,32,256]{2,1,0:T(8,128)S(1)} %collective-permute-done.1), channel_id=1, source_target_pairs={{8,16},{12,20},{16,8},{20,12},{24,32},{28,36},{32,24},{36,28},{40,... | collective-permute-start | bytes 786440 | tf_op jit(solution)/shard_map/ppermute | solution.py:255
  20.6 0.1 collective-permute-start.4
  20.7 0.0 collective-permute-done.2.refs_3_
  20.8 4.8 %collective-permute-start.9 = (f32[32,8,256]{2,1,0:T(8,128)S(1)}, f32[32,8,256]{2,1,0:T(8,128)S(1)}, u32[]{:S(2)}, u32[]{:S(2)}) collective-permute-start(f32[32,8,256]{2,1,0:T(8,128)S(1)} %maximum_select_fusion), channel_id=1, source_target_pairs={{1,2},{2,1},{5,6},{6,5},{9,10},{10,9},{13,14},{14,13},{17,18},{18,... | collective-permute-start | bytes 786440 | tf_op jit(solution)/shard_map/ppermute | solution.py:255
  25.7 3.5 %collective-permute-start.5 = (f32[8,32,256]{2,1,0:T(8,128)S(1)}, f32[8,32,256]{2,1,0:T(8,128)S(1)}, u32[]{:S(2)}, u32[]{:S(2)}) collective-permute-start(f32[8,32,256]{2,1,0:T(8,128)S(1)} %collective-permute-done.2.refs_3_), channel_id=1, source_target_pairs={{8,16},{12,20},{16,8},{20,12},{24,32},{28,36},{32,24},{36,28},{40,... | collective-permute-start | bytes 786440 | tf_op jit(solution)/shard_map/ppermute | solution.py:255
  29.1 0.3 collective-permute-start.6
  29.4 0.0 collective-permute-done.3
  29.4 0.0 collective-permute-done.4
  29.4 0.1 broadcast_select_fusion.2
  29.5 2.5 %collective-permute-start.7 = (f32[8,32,256]{2,1,0:T(8,128)S(1)}, f32[8,32,256]{2,1,0:T(8,128)S(1)}, u32[]{:S(2)}, u32[]{:S(2)}) collective-permute-start(f32[8,32,256]{2,1,0:T(8,128)S(1)} %get-tuple-element.3), channel_id=1, source_target_pairs={{0,4},{4,0},{8,12},{12,8},{16,20},{20,16},{24,28},{28,24},{32,36},... | collective-permute-start | bytes 786440 | tf_op jit(solution)/shard_map/ppermute | solution.py:255
  32.1 4.0 %collective-permute-done.5 = f32[8,32,256]{2,1,0:T(8,128)S(1)} collective-permute-done((f32[8,32,256]{2,1,0:T(8,128)S(1)}, f32[8,32,256]{2,1,0:T(8,128)S(1)}, u32[]{:S(2)}, u32[]{:S(2)}) %collective-permute-start.5) | collective-permute-done | bytes 262176 | tf_op jit(solution)/shard_map/ppermute | solution.py:255
  36.1 0.0 collective-permute-done.6
  36.2 2.8 %collective-permute-done.7.refs_8_ = f32[8,32,256]{2,1,0:T(8,128)S(1)} collective-permute-done((f32[8,32,256]{2,1,0:T(8,128)S(1)}, f32[8,32,256]{2,1,0:T(8,128)S(1)}, u32[]{:S(2)}, u32[]{:S(2)}) %collective-permute-start.7) | collective-permute-done | bytes 262176 | tf_op jit(solution)/shard_map/ppermute | solution.py:255
  39.0 0.0 copy-start
  39.1 0.0 copy-start.1
  39.1 0.0 copy-start.2
  39.1 0.0 copy-start.3
  39.1 0.0 copy-start.4
  39.2 3.1 %collective-permute-start.10 = (f32[40,8,256]{2,1,0:T(8,128)S(1)}, f32[40,8,256]{2,1,0:T(8,128)S(1)}, u32[]{:S(2)}, u32[]{:S(2)}) collective-permute-start(f32[40,8,256]{2,1,0:T(8,128)S(1)} %broadcast_select_fusion.1), channel_id=1, source_target_pairs={{1,2},{2,1},{5,6},{6,5},{9,10},{10,9},{13,14},{14,13},{17,18},{18,... | collective-permute-start | bytes 983048 | tf_op jit(solution)/shard_map/ppermute | solution.py:255
  42.2 0.0 copy-done.5
  42.2 0.0 copy-done.6
  42.2 0.0 copy-done
  42.3 0.0 copy-done.1
  42.3 0.0 copy-done.2
  42.3 0.0 copy-done.3
  42.3 5.0 %tensor_middle.1.refs_0_ = f32[16,6,8,256]{3,2,1,0:T(8,128)S(1)} custom-call(f32[8,32,256]{2,1,0:T(8,128)S(1)} %bitcast.7, f32[8,32,256]{2,1,0:T(8,128)S(1)} %get-tuple-element.9.refs_1_, f32[8,32,256]{2,1,0:T(8,128)S(1)} %get-tuple-element.8.refs_2_, f32[8,32,256]{2,1,0:T(8,128)S(1)} %collective-permute-done.2.refs_3_, ...), custom_call_target="tpu_custom_call" | custom-call | flops 8000000000 | bytes 4194304 | tf_op jit(solution)/shard_map/tensor_middle/pallas_call | solution.py:313
  47.3 0.1 collective-permute-start.12
  47.4 2.6 %collective-permute-start.14 = (f32[16,6,8,256]{3,2,1,0:T(8,128)S(1)}, f32[16,6,8,256]{3,2,1,0:T(8,128)S(1)}, u32[]{:S(2)}, u32[]{:S(2)}) collective-permute-start(f32[16,6,8,256]{3,2,1,0:T(8,128)S(1)} %tensor_middle.1.refs_0_), channel_id=1, source_target_pairs={{1,2},{2,1},{5,6},{6,5},{9,10},{10,9},{13,14},{14,13},{17,18},{18,... | collective-permute-start | bytes 2359304 | tf_op jit(solution)/shard_map/ppermute | solution.py:255
  50.0 0.1 broadcast_select_fusion
  50.1 0.1 collective-permute-start.8
  50.2 0.0 collective-permute-done.9.refs_9_
  50.2 0.0 collective-permute-done.10.refs_10_
  50.2 2.9 %tensor_away.1.refs_2_ = f32[8,6,8,256]{3,2,1,0:T(8,128)S(1)} custom-call(f32[8,32,256]{2,1,0:T(8,128)S(1)} %bitcast.8, f32[8,32,256]{2,1,0:T(8,128)S(1)} %get-tuple-element.9.refs_1_, f32[8,32,256]{2,1,0:T(8,128)S(1)} %get-tuple-element.8.refs_2_, f32[8,32,256]{2,1,0:T(8,128)S(1)} %collective-permute-done.2.refs_3_, ...), custom_call_target="tpu_custom_call" | custom-call | flops 8000000000 | bytes 4194304 | tf_op jit(solution)/shard_map/tensor_away/pallas_call | solution.py:313
  53.1 2.9 %collective-permute-start.13 = (f32[8,6,8,256]{3,2,1,0:T(8,128)S(1)}, f32[8,6,8,256]{3,2,1,0:T(8,128)S(1)}, u32[]{:S(2)}, u32[]{:S(2)}) collective-permute-start(f32[8,6,8,256]{3,2,1,0:T(8,128)S(1)} %tensor_away.1.refs_2_), channel_id=1, source_target_pairs={{1,2},{2,1},{5,6},{6,5},{9,10},{10,9},{13,14},{14,13},{17,18},{18,... | collective-permute-start | bytes 1179656 | tf_op jit(solution)/shard_map/ppermute | solution.py:255
  56.1 0.0 collective-permute-done.8.refs_9_
  56.1 3.1 %tensor_near.1.refs_1_ = f32[8,6,8,256]{3,2,1,0:T(8,128)S(1)} custom-call(f32[8,32,256]{2,1,0:T(8,128)S(1)} %bitcast.9, f32[8,32,256]{2,1,0:T(8,128)S(1)} %get-tuple-element.9.refs_1_, f32[8,32,256]{2,1,0:T(8,128)S(1)} %get-tuple-element.8.refs_2_, f32[8,32,256]{2,1,0:T(8,128)S(1)} %collective-permute-done.2.refs_3_, ...), custom_call_target="tpu_custom_call" | custom-call | flops 8000000000 | bytes 4194304 | tf_op jit(solution)/shard_map/tensor_near/pallas_call | solution.py:313
  59.1 0.1 collective-permute-start.11
  59.2 5.7 %collective-permute-done.13.refs_5_ = f32[8,6,8,256]{3,2,1,0:T(8,128)S(1)} collective-permute-done((f32[8,6,8,256]{3,2,1,0:T(8,128)S(1)}, f32[8,6,8,256]{3,2,1,0:T(8,128)S(1)}, u32[]{:S(2)}, u32[]{:S(2)}) %collective-permute-start.13) | collective-permute-done | bytes 393248 | tf_op jit(solution)/shard_map/ppermute | solution.py:255
  64.9 0.0 collective-permute-done.12.refs_4_
  64.9 0.0 collective-permute-done.14.refs_6_
  64.9 0.0 collective-permute-done.11.refs_3_
  64.9 1.8 %attributes.1 = (f32[32,8,256]{2,1,0:T(8,128)}, f32[32,8,256]{2,1,0:T(8,128)}, f32[32,8,256]{2,1,0:T(8,128)}) custom-call(f32[16,6,8,256]{3,2,1,0:T(8,128)S(1)} %tensor_middle.1.refs_0_, f32[8,6,8,256]{3,2,1,0:T(8,128)S(1)} %tensor_near.1.refs_1_, f32[8,6,8,256]{3,2,1,0:T(8,128)S(1)} %tensor_away.1.refs_2_, ...), custom_call_target="tpu_custom_call" | custom-call | tf_op jit(solution)/shard_map/attributes/pallas_call | solution.py:348
  (16 shorter events, 0.3 us)
Async XLA Ops:
  1.7 13.7 %collective-permute-start = (f32[8,32,256]{2,1,0:T(8,128)S(1)}, f32[8,32,256]{2,1,0:T(8,128)S(1)}, u32[]{:S(2)}, u32[]{:S(2)}) collective-permute-start(f32[8,32,256]{2,1,0:T(8,128)S(1)} %bitcast.3), channel_id=1, source_target_pairs={{8,16},{12,20},{16,8},{20,12},{24,32},{28,36},{32,24},{36,28},{40,... | collective-permute-start | bytes 786440 | tf_op jit(solution)/shard_map/ppermute | solution.py:255
  9.3 6.9 %collective-permute-start.1 = (f32[8,32,256]{2,1,0:T(8,128)S(1)}, f32[8,32,256]{2,1,0:T(8,128)S(1)}, u32[]{:S(2)}, u32[]{:S(2)}) collective-permute-start(f32[8,32,256]{2,1,0:T(8,128)S(1)} %bitcast.4), channel_id=1, source_target_pairs={{0,8},{4,12},{8,0},{12,4},{16,24},{20,28},{24,16},{28,20},{32,40},... | collective-permute-start | bytes 786440 | tf_op jit(solution)/shard_map/ppermute | solution.py:255
  9.4 11.3 %collective-permute-start.2 = (f32[8,32,256]{2,1,0:T(8,128)S(1)}, f32[8,32,256]{2,1,0:T(8,128)S(1)}, u32[]{:S(2)}, u32[]{:S(2)}) collective-permute-start(f32[8,32,256]{2,1,0:T(8,128)S(1)} %bitcast.5), channel_id=1, source_target_pairs={{0,4},{4,0},{8,12},{12,8},{16,20},{20,16},{24,28},{28,24},{32,36},... | collective-permute-start | bytes 786440 | tf_op jit(solution)/shard_map/ppermute | solution.py:255
  16.4 13.0 %collective-permute-start.3 = (f32[8,32,256]{2,1,0:T(8,128)S(1)}, f32[8,32,256]{2,1,0:T(8,128)S(1)}, u32[]{:S(2)}, u32[]{:S(2)}) collective-permute-start(f32[8,32,256]{2,1,0:T(8,128)S(1)} %collective-permute-done.1), channel_id=1, source_target_pairs={{8,16},{12,20},{16,8},{20,12},{24,32},{28,36},{32,24},{36,28},{40,... | collective-permute-start | bytes 786440 | tf_op jit(solution)/shard_map/ppermute | solution.py:255
  20.6 8.8 %collective-permute-start.4 = (f32[8,32,256]{2,1,0:T(8,128)S(1)}, f32[8,32,256]{2,1,0:T(8,128)S(1)}, u32[]{:S(2)}, u32[]{:S(2)}) collective-permute-start(f32[8,32,256]{2,1,0:T(8,128)S(1)} %collective-permute-done), channel_id=1, source_target_pairs={{0,8},{4,12},{8,0},{12,4},{16,24},{20,28},{24,16},{28,20},{32,40},... | collective-permute-start | bytes 786440 | tf_op jit(solution)/shard_map/ppermute | solution.py:255
  20.8 29.4 %collective-permute-start.9 = (f32[32,8,256]{2,1,0:T(8,128)S(1)}, f32[32,8,256]{2,1,0:T(8,128)S(1)}, u32[]{:S(2)}, u32[]{:S(2)}) collective-permute-start(f32[32,8,256]{2,1,0:T(8,128)S(1)} %maximum_select_fusion), channel_id=1, source_target_pairs={{1,2},{2,1},{5,6},{6,5},{9,10},{10,9},{13,14},{14,13},{17,18},{18,... | collective-permute-start | bytes 786440 | tf_op jit(solution)/shard_map/ppermute | solution.py:255
  25.7 10.5 %collective-permute-start.5 = (f32[8,32,256]{2,1,0:T(8,128)S(1)}, f32[8,32,256]{2,1,0:T(8,128)S(1)}, u32[]{:S(2)}, u32[]{:S(2)}) collective-permute-start(f32[8,32,256]{2,1,0:T(8,128)S(1)} %collective-permute-done.2.refs_3_), channel_id=1, source_target_pairs={{8,16},{12,20},{16,8},{20,12},{24,32},{28,36},{32,24},{36,28},{40,... | collective-permute-start | bytes 786440 | tf_op jit(solution)/shard_map/ppermute | solution.py:255
  29.1 7.0 %collective-permute-start.6 = (f32[8,32,256]{2,1,0:T(8,128)S(1)}, f32[8,32,256]{2,1,0:T(8,128)S(1)}, u32[]{:S(2)}, u32[]{:S(2)}) collective-permute-start(f32[8,32,256]{2,1,0:T(8,128)S(1)} %collective-permute-done.2.refs_3_), channel_id=1, source_target_pairs={{0,8},{4,12},{8,0},{12,4},{16,24},{20,28},{24,16},{28,20},{32,40},... | collective-permute-start | bytes 786440 | tf_op jit(solution)/shard_map/ppermute | solution.py:255
  29.5 9.5 %collective-permute-start.7 = (f32[8,32,256]{2,1,0:T(8,128)S(1)}, f32[8,32,256]{2,1,0:T(8,128)S(1)}, u32[]{:S(2)}, u32[]{:S(2)}) collective-permute-start(f32[8,32,256]{2,1,0:T(8,128)S(1)} %get-tuple-element.3), channel_id=1, source_target_pairs={{0,4},{4,0},{8,12},{12,8},{16,20},{20,16},{24,28},{28,24},{32,36},... | collective-permute-start | bytes 786440 | tf_op jit(solution)/shard_map/ppermute | solution.py:255
  39.0 3.2 %copy-start.5 = (bf16[256,256]{1,0:T(8,128)(2,1)S(1)}, bf16[256,256]{1,0:T(8,128)(2,1)}, u32[]{:S(2)}) copy-start(bf16[256,256]{1,0:T(8,128)(2,1)} %constant.48.clone.refs_14_.refs_15_.refs_16_) | copy-start | bytes 393220
  39.0 3.2 %copy-start.6 = (bf16[256,256]{1,0:T(8,128)(2,1)S(1)}, bf16[256,256]{1,0:T(8,128)(2,1)}, u32[]{:S(2)}) copy-start(bf16[256,256]{1,0:T(8,128)(2,1)} %constant.49.clone.refs_15_.refs_16_.refs_17_) | copy-start | bytes 393220
  39.0 3.2 %copy-start = (bf16[384,480]{1,0:T(8,128)(2,1)S(1)}, bf16[384,480]{1,0:T(8,128)(2,1)}, u32[]{:S(2)}) copy-start(bf16[384,480]{1,0:T(8,128)(2,1)} %constant.50.clone.refs_9_.refs_10_.refs_11_) | copy-start | bytes 1105924
  39.1 3.2 %copy-start.1 = (bf16[256,256]{1,0:T(8,128)(2,1)S(1)}, bf16[256,256]{1,0:T(8,128)(2,1)}, u32[]{:S(2)}) copy-start(bf16[256,256]{1,0:T(8,128)(2,1)} %constant.44.clone.refs_10_.refs_11_.refs_12_) | copy-start | bytes 393220
  39.1 3.2 %copy-start.2 = (bf16[256,256]{1,0:T(8,128)(2,1)S(1)}, bf16[256,256]{1,0:T(8,128)(2,1)}, u32[]{:S(2)}) copy-start(bf16[256,256]{1,0:T(8,128)(2,1)} %constant.45.clone.refs_11_.refs_12_.refs_13_) | copy-start | bytes 393220
  39.1 3.2 %copy-start.3 = (bf16[256,256]{1,0:T(8,128)(2,1)S(1)}, bf16[256,256]{1,0:T(8,128)(2,1)}, u32[]{:S(2)}) copy-start(bf16[256,256]{1,0:T(8,128)(2,1)} %constant.46.clone.refs_12_.refs_13_.refs_14_) | copy-start | bytes 393220
  39.1 3.2 %copy-start.4 = (bf16[256,256]{1,0:T(8,128)(2,1)S(1)}, bf16[256,256]{1,0:T(8,128)(2,1)}, u32[]{:S(2)}) copy-start(bf16[256,256]{1,0:T(8,128)(2,1)} %constant.47.clone.refs_13_.refs_14_.refs_15_) | copy-start | bytes 393220
  39.2 11.1 %collective-permute-start.10 = (f32[40,8,256]{2,1,0:T(8,128)S(1)}, f32[40,8,256]{2,1,0:T(8,128)S(1)}, u32[]{:S(2)}, u32[]{:S(2)}) collective-permute-start(f32[40,8,256]{2,1,0:T(8,128)S(1)} %broadcast_select_fusion.1), channel_id=1, source_target_pairs={{1,2},{2,1},{5,6},{6,5},{9,10},{10,9},{13,14},{14,13},{17,18},{18,... | collective-permute-start | bytes 983048 | tf_op jit(solution)/shard_map/ppermute | solution.py:255
  47.3 17.6 %collective-permute-start.12 = (f32[16,6,8,256]{3,2,1,0:T(8,128)S(1)}, f32[16,6,8,256]{3,2,1,0:T(8,128)S(1)}, u32[]{:S(2)}, u32[]{:S(2)}) collective-permute-start(f32[16,6,8,256]{3,2,1,0:T(8,128)S(1)} %tensor_middle.1.refs_0_), channel_id=1, source_target_pairs={{0,1},{1,0},{2,3},{3,2},{4,5},{5,4},{6,7},{7,6},{8,9},{9,8},{10,11... | collective-permute-start | bytes 2359304 | tf_op jit(solution)/shard_map/ppermute | solution.py:255
  47.4 17.5 %collective-permute-start.14 = (f32[16,6,8,256]{3,2,1,0:T(8,128)S(1)}, f32[16,6,8,256]{3,2,1,0:T(8,128)S(1)}, u32[]{:S(2)}, u32[]{:S(2)}) collective-permute-start(f32[16,6,8,256]{3,2,1,0:T(8,128)S(1)} %tensor_middle.1.refs_0_), channel_id=1, source_target_pairs={{1,2},{2,1},{5,6},{6,5},{9,10},{10,9},{13,14},{14,13},{17,18},{18,... | collective-permute-start | bytes 2359304 | tf_op jit(solution)/shard_map/ppermute | solution.py:255
  50.1 5.9 %collective-permute-start.8 = (f32[72,8,256]{2,1,0:T(8,128)S(1)}, f32[72,8,256]{2,1,0:T(8,128)S(1)}, u32[]{:S(2)}, u32[]{:S(2)}) collective-permute-start(f32[72,8,256]{2,1,0:T(8,128)S(1)} %broadcast_select_fusion), channel_id=1, source_target_pairs={{0,1},{1,0},{2,3},{3,2},{4,5},{5,4},{6,7},{7,6},{8,9},{9,8},{10,11... | collective-permute-start | bytes 1769480 | tf_op jit(solution)/shard_map/ppermute | solution.py:255
  53.1 11.8 %collective-permute-start.13 = (f32[8,6,8,256]{3,2,1,0:T(8,128)S(1)}, f32[8,6,8,256]{3,2,1,0:T(8,128)S(1)}, u32[]{:S(2)}, u32[]{:S(2)}) collective-permute-start(f32[8,6,8,256]{3,2,1,0:T(8,128)S(1)} %tensor_away.1.refs_2_), channel_id=1, source_target_pairs={{1,2},{2,1},{5,6},{6,5},{9,10},{10,9},{13,14},{14,13},{17,18},{18,... | collective-permute-start | bytes 1179656 | tf_op jit(solution)/shard_map/ppermute | solution.py:255
  59.1 5.8 %collective-permute-start.11 = (f32[8,6,8,256]{3,2,1,0:T(8,128)S(1)}, f32[8,6,8,256]{3,2,1,0:T(8,128)S(1)}, u32[]{:S(2)}, u32[]{:S(2)}) collective-permute-start(f32[8,6,8,256]{3,2,1,0:T(8,128)S(1)} %tensor_near.1.refs_1_), channel_id=1, source_target_pairs={{0,1},{1,0},{2,3},{3,2},{4,5},{5,4},{6,7},{7,6},{8,9},{9,8},{10,11... | collective-permute-start | bytes 1179656 | tf_op jit(solution)/shard_map/ppermute | solution.py:255

commit v6 on v5

--- a/solution.py
+++ b/solution.py
@@ -89,59 +89,21 @@
     return dot(high, w_high) + (dot(high, w_low) + dot(low, w_high))
 
 
-def tensor_kernel(rows, total_rows, tiles, width, halos, *refs):
-    blocks, refs = refs[:9], refs[9:]
-    if halos:
-        count, upper_side = halos
-        halo, refs = refs[:count], refs[count:]
-    taps, wd_high, wd_low, wg_high, wg_low, ws_high, ws_low = refs[:7]
-    out = refs[7]
-    raw_high, raw_low, pre_high, pre_low, grads, part, ty = refs[-7:]
-    tile_count = len(tiles)
-    planes = 8 * tile_count
-    device = lax.axis_index("pa")
-    side = 1 - 2 * lax.rem(device, 2)
-    even_depth = lax.rem(lax.axis_index("gz"), 2) == 0
-    outer = rows + 2 * HALF
-    trim = 4 * rows - REACH
-    places = [0, -2, 2, side, -4, 4, side - 2, side + 2, -3 * side]
-    span = 3 * 8
-
-    def stage(n, place, x):
-        high, low = split(x.reshape(rows * span, width))
-        at = pl.ds(pl.multiple_of((place + 4) * (rows * span), 16), rows * span)
-        raw_high[n, at, :] = high
-        raw_low[n, at, :] = low
-
-    def stage_end(first):
-        for i, (block, place) in enumerate(zip(blocks, places)):
-            part, at = (halo[0], i) if i < 4 or count == 1 else (halo[1], i - 4)
-            beyond = part[at * rows : (at + 1) * rows]
-            parts = [beyond, block[:, :16]] if first else [block[:, -16:], beyond]
-            stage(0, place, jnp.concatenate(parts, axis=1))
-
-    if halos:
-        upper = even_depth if upper_side == "away" else jnp.logical_not(even_depth)
-        pl.when(upper)(lambda: stage_end(True))
-        pl.when(jnp.logical_not(upper))(lambda: stage_end(False))
-    else:
-        for n, plane in enumerate(tiles):
-            for block, place in zip(blocks, places):
-                stage(n, place, block[:, plane - 8 : plane + 16])
-
-    group = 8
+def gradient_rows(tile_count, groups, first_row, total_rows, trim, weights, raw, pre, write):
+    taps, wd_high, wd_low, wg_high, wg_low = weights
+    (raw_high, raw_low), (pre_high, pre_low) = raw, pre
+    group, width = 8, raw_high.shape[2]
     size = group * 8
-    reach = (group + 2 * GHALF) * span
+    reach = (group + 2 * GHALF) * 24
     for n in range(tile_count):
-        for start in range(0, outer, group):
-            at = (start + trim) * span
+        for g in range(groups):
+            at = (g * group + trim) * 24
             high, low = raw_high[n, at : at + reach, :], raw_low[n, at : at + reach, :]
             both = dot(taps[...], high)
             result = both[: 3 * size] + (both[3 * size :] + dot(taps[: 3 * size, :], low))
-            first = device * rows + (start - HALF)
-            row = first + lax.broadcasted_iota(jnp.int32, (size, width), 0) // 8
+            row = first_row + g * group + lax.broadcasted_iota(jnp.int32, (size, width), 0) // 8
             inside = jnp.logical_and(row >= 0, row < total_rows).astype(F32)
-            to = n * outer * 8 + start * 8
+            to = (n * groups + g) * size
             for f in range(3):
                 high, low = split(result[f * size : (f + 1) * size] * inside)
                 pre_high[f, to : to + size, :] = high
@@ -150,10 +112,94 @@
         ((wd_high, wd_low), (wg_high, wg_low), (wg_high, wg_low))
     ):
         for n in range(tile_count):
-            at = slice(n * outer * 8, (n + 1) * outer * 8)
+            at = slice(n * groups * size, (n + 1) * groups * size)
             high, low = pre_high[f, at, :], pre_low[f, at, :]
-            result = dot(high, w_high[...]) + (dot(high, w_low[...]) + dot(low, w_high[...]))
-            grads[f, at, :] = result
+            write(f, n, dot(high, w_high[...]) + (dot(high, w_low[...]) + dot(low, w_high[...])))
+
+
+def stage_rows(raw, n, place, x):
+    rows, width = x.shape[0] * x.shape[1], x.shape[2]
+    high, low = split(x.reshape(rows, width))
+    at = pl.ds(pl.multiple_of(place * rows, 16), rows)
+    raw[0][n, at, :] = high
+    raw[1][n, at, :] = low
+
+
+def stage_window(raw, tiles, blocks, even_order, odd_order):
+    def stage(order):
+        for n, plane in enumerate(tiles):
+            for place, index in enumerate(order):
+                stage_rows(raw, n, place, blocks[index][:, plane - 8 : plane + 16])
+
+    odd = lax.rem(lax.axis_index("pa"), 2) == 1
+    pl.when(odd)(lambda: stage(odd_order))
+    pl.when(jnp.logical_not(odd))(lambda: stage(even_order))
+
+
+def early_kernel(rows, total_rows, tiles, *refs):
+    blocks, weights, out = refs[:8], refs[8:13], refs[13]
+    raw, pre = refs[14:16], refs[16:18]
+    device = lax.axis_index("pa")
+    even = 1 - lax.rem(device, 2)
+    stage_window(raw, tiles, blocks, (1, 6, 0, 3, 2, 7, 5), (4, 6, 1, 3, 0, 7, 2))
+
+    def write(f, n, result):
+        out[f, n] = result
+
+    gradient_rows(
+        len(tiles), 5, device * rows - HALF + 16 * even, total_rows, 4 * rows - REACH,
+        weights, raw, pre, write,
+    )
+
+
+def tensor_kernel(rows, total_rows, tiles, width, halos, *refs):
+    blocks, refs = refs[:9], refs[9:]
+    count, upper_side = halos
+    halo, refs = refs[:count], refs[count:]
+    weights, ws_high, ws_low, out = refs[:5], refs[5], refs[6], refs[7]
+    raw_high, raw_low, pre_high, pre_low, grads, part, ty = refs[-7:]
+    raw, pre = (raw_high, raw_low), (pre_high, pre_low)
+    tile_count = len(tiles)
+    planes = 8 * tile_count
+    device = lax.axis_index("pa")
+    odd = lax.rem(device, 2)
+    side = 1 - 2 * odd
+    even_depth = lax.rem(lax.axis_index("gz"), 2) == 0
+    outer = rows + 2 * HALF
+    trim = 4 * rows - REACH
+    places = [0, -2, 2, side, -4, 4, side - 2, side + 2, -3 * side]
+
+    def stage_end(first):
+        for i, (block, place) in enumerate(zip(blocks, places)):
+            part, at = (halo[0], i) if i < 4 or count == 1 else (halo[1], i - 4)
+            beyond = part[at * rows : (at + 1) * rows]
+            parts = [beyond, block[:, :16]] if first else [block[:, -16:], beyond]
+            stage_rows(raw, 0, place + 4, jnp.concatenate(parts, axis=1))
+
+    first_row = device * rows - HALF
+    if upper_side == "middle":
+        early = halo[0]
+        stage_window(raw, tiles, blocks, (4, 8, 1, 6), (7, 2, 8, 5))
+        for f in range(3):
+            for n in range(tile_count):
+                at = pl.multiple_of(n * outer * 8 + (1 - odd) * 128, 8)
+                grads[f, pl.ds(at, 320), :] = early[f, n]
+
+        def write(f, n, result):
+            grads[f, pl.ds(pl.multiple_of(n * outer * 8 + odd * 320, 8), 128), :] = result
+
+        gradient_rows(
+            tile_count, 2, first_row + 40 * odd, total_rows, trim, weights, raw, pre, write
+        )
+    else:
+        upper = even_depth if upper_side == "away" else jnp.logical_not(even_depth)
+        pl.when(upper)(lambda: stage_end(True))
+        pl.when(jnp.logical_not(upper))(lambda: stage_end(False))
+
+        def write(f, n, result):
+            grads[f, n * outer * 8 : (n + 1) * outer * 8, :] = result
+
+        gradient_rows(tile_count, 7, first_row, total_rows, trim, weights, raw, pre, write)
 
     def products(j, at, lanes):
         x, y, z = (grads[f, pl.ds(at + 8 * j, 8), lanes] for f in range(3))
@@ -334,7 +380,22 @@
         )(*operands)
 
     whole = pl.BlockSpec(memory_space=pltpu.VMEM)
-    middle = tensors([8, 16], [], None, "tensor_middle")
+    tiles = [8, 16]
+    early_shape = (len(tiles), 7 * rows * 24, width)
+    early_pre = (3, len(tiles) * 320, width)
+    early = pl.pallas_call(
+        functools.partial(early_kernel, rows, rows * groups, tiles),
+        out_shape=jax.ShapeDtypeStruct((3, len(tiles), 320, width), F32),
+        in_specs=[whole] * 13,
+        out_specs=whole,
+        scratch_shapes=[pltpu.VMEM(early_shape, BF16)] * 2 + [pltpu.VMEM(early_pre, BF16)] * 2,
+        compiler_params=pltpu.CompilerParams(vmem_limit_bytes=28 * 2**20),
+        cost_estimate=pl.CostEstimate(
+            flops=4 * 10**9, bytes_accessed=4 * 2**20, transcendentals=0
+        ),
+        name="early",
+    )(*pieces[:8], *weights[:5])
+    middle = tensors(tiles, [early], (1, "middle"), "tensor_middle")
     middle_away = depth_away(middle)
     middle_near = depth_near(middle)
     end_away = tensors([0], swap_away, (2, "away"), "tensor_away")

time: 67 us -> 66.6 us (level)
  waiting for transfers between devices: 16.5 us -> 14.1 us
  starting transfers between devices: 34.9 us -> 36.3 us
    pallas_call x0 -> x1, Pallas kernels: none -> 2.84 us  [local(): pl.pallas_call(functools.partial(early_kernel, rows, rows * groups, tiles...]
    ppermute x15, waiting for transfers between devices: 16.5 us -> 14.1 us  [send(): return lax.ppermute(x, axis, pairs)]
    pallas_call x3, Pallas kernels: 10.9 us -> 8.62 us  [tensors(): pl.pallas_call(functools.partial(tensor_kernel, rows, rows * groups, tile...]
    ppermute x15, starting transfers between devices: 34.9 us -> 36.3 us  [send(): return lax.ppermute(x, axis, pairs)]
  transfers between devices with their start and end apart: 15 -> 15, of which waited for: 5 -> 4; matrix products, arithmetic and copies ran while one was open for 1% -> 1% of each run, Pallas kernels for 16% -> 17%
where the time goes in v6:
time: 66.6 us; the launch traced here: 66.3 us
  starting transfers between devices  36.3 us (55%)
  waiting for transfers between devices  14.1 us (21%)
  Pallas kernels  13.2 us (20%)
  local copies, waits for them, and re-layouts  1.27 us (2%)
  between operations  1.01 us (2%)
    ppermute x15, starting transfers between devices, send(): return lax.ppermute(x, axis, pairs)  36.3 us
    ppermute x15, waiting for transfers between devices, send(): return lax.ppermute(x, axis, pairs)  14.1 us
    pallas_call x3, Pallas kernels, tensors(): pl.pallas_call(functools.partial(tensor_kernel, rows, rows * groups, tile...  8.62 us
    pallas_call x1, Pallas kernels, local(): pl.pallas_call(functools.partial(early_kernel, rows, rows * groups, tiles...  2.84 us
    pallas_call x1, Pallas kernels, local(): pl.pallas_call(functools.partial(attribute_kernel, planes, width, starts)...  1.77 us
  transfers between devices with their start and end apart: 15, of which 4 were waited for; matrix products, arithmetic and copies ran while one was open for 1% of the time, Pallas kernels for 17%

profile of v6, /device:TPU:25, one launch (start us, length us, event | category | flops | bytes accessed | tf_op | source)
XLA Modules:
  0.0 66.3 jit_solution(946327042411057080)
XLA Ops:
  0.6 1.0 %copy.13 = f32[32,8,256]{2,0,1:T(8,128)S(1)} copy(f32[32,8,256]{2,1,0:T(8,128)} %param.8) | data formatting | bytes 524288 | tf_op args[0]
  1.7 1.7 %collective-permute-start.1 = (f32[8,32,256]{2,1,0:T(8,128)S(1)}, f32[8,32,256]{2,1,0:T(8,128)S(1)}, u32[]{:S(2)}, u32[]{:S(2)}) collective-permute-start(f32[8,32,256]{2,1,0:T(8,128)S(1)} %bitcast.3), channel_id=1, source_target_pairs={{0,8},{4,12},{8,0},{12,4},{16,24},{20,28},{24,16},{28,20},{32,40},... | collective-permute-start | bytes 786440 | tf_op jit(solution)/shard_map/ppermute | solution.py:301
  3.4 6.7 %collective-permute-start = (f32[8,32,256]{2,1,0:T(8,128)S(1)}, f32[8,32,256]{2,1,0:T(8,128)S(1)}, u32[]{:S(2)}, u32[]{:S(2)}) collective-permute-start(f32[8,32,256]{2,1,0:T(8,128)S(1)} %bitcast.4), channel_id=1, source_target_pairs={{8,16},{12,20},{16,8},{20,12},{24,32},{28,36},{32,24},{36,28},{40,... | collective-permute-start | bytes 786440 | tf_op jit(solution)/shard_map/ppermute | solution.py:301
  10.1 2.8 %collective-permute-start.2 = (f32[8,32,256]{2,1,0:T(8,128)S(1)}, f32[8,32,256]{2,1,0:T(8,128)S(1)}, u32[]{:S(2)}, u32[]{:S(2)}) collective-permute-start(f32[8,32,256]{2,1,0:T(8,128)S(1)} %bitcast.5), channel_id=1, source_target_pairs={{0,4},{4,0},{8,12},{12,8},{16,20},{20,16},{24,28},{28,24},{32,36},... | collective-permute-start | bytes 786440 | tf_op jit(solution)/shard_map/ppermute | solution.py:301
  13.0 0.0 collective-permute-done.1
  13.0 2.8 %collective-permute-done = f32[8,32,256]{2,1,0:T(8,128)S(1)} collective-permute-done((f32[8,32,256]{2,1,0:T(8,128)S(1)}, f32[8,32,256]{2,1,0:T(8,128)S(1)}, u32[]{:S(2)}, u32[]{:S(2)}) %collective-permute-start) | collective-permute-done | bytes 262176 | tf_op jit(solution)/shard_map/ppermute | solution.py:301
  15.9 5.2 %collective-permute-start.3 = (f32[8,32,256]{2,1,0:T(8,128)S(1)}, f32[8,32,256]{2,1,0:T(8,128)S(1)}, u32[]{:S(2)}, u32[]{:S(2)}) collective-permute-start(f32[8,32,256]{2,1,0:T(8,128)S(1)} %collective-permute-done.1), channel_id=1, source_target_pairs={{8,16},{12,20},{16,8},{20,12},{24,32},{28,36},{32,24},{36,28},{40,... | collective-permute-start | bytes 786440 | tf_op jit(solution)/shard_map/ppermute | solution.py:301
  21.1 0.1 collective-permute-start.4
  21.2 0.0 collective-permute-done.2.refs_3_
  21.2 0.0 copy-start
  21.3 0.0 copy-start.1
  21.3 0.0 copy-start.2
  21.3 0.0 copy-start.3
  21.3 0.0 copy-start.4
  21.4 5.3 %collective-permute-start.9 = (f32[32,8,256]{2,1,0:T(8,128)S(1)}, f32[32,8,256]{2,1,0:T(8,128)S(1)}, u32[]{:S(2)}, u32[]{:S(2)}) collective-permute-start(f32[32,8,256]{2,1,0:T(8,128)S(1)} %maximum_select_fusion), channel_id=1, source_target_pairs={{1,2},{2,1},{5,6},{6,5},{9,10},{10,9},{13,14},{14,13},{17,18},{18,... | collective-permute-start | bytes 786440 | tf_op jit(solution)/shard_map/ppermute | solution.py:301
  26.6 1.8 %collective-permute-start.6 = (f32[8,32,256]{2,1,0:T(8,128)S(1)}, f32[8,32,256]{2,1,0:T(8,128)S(1)}, u32[]{:S(2)}, u32[]{:S(2)}) collective-permute-start(f32[8,32,256]{2,1,0:T(8,128)S(1)} %collective-permute-done.2.refs_3_), channel_id=1, source_target_pairs={{0,8},{4,12},{8,0},{12,4},{16,24},{20,28},{24,16},{28,20},{32,40},... | collective-permute-start | bytes 786440 | tf_op jit(solution)/shard_map/ppermute | solution.py:301
  28.5 1.9 %collective-permute-start.5 = (f32[8,32,256]{2,1,0:T(8,128)S(1)}, f32[8,32,256]{2,1,0:T(8,128)S(1)}, u32[]{:S(2)}, u32[]{:S(2)}) collective-permute-start(f32[8,32,256]{2,1,0:T(8,128)S(1)} %collective-permute-done.2.refs_3_), channel_id=1, source_target_pairs={{8,16},{12,20},{16,8},{20,12},{24,32},{28,36},{32,24},{36,28},{40,... | collective-permute-start | bytes 786440 | tf_op jit(solution)/shard_map/ppermute | solution.py:301
  30.4 0.0 collective-permute-done.3
  30.4 0.0 collective-permute-done.4
  30.4 0.1 broadcast_select_fusion.2
  30.5 2.5 %collective-permute-start.7 = (f32[8,32,256]{2,1,0:T(8,128)S(1)}, f32[8,32,256]{2,1,0:T(8,128)S(1)}, u32[]{:S(2)}, u32[]{:S(2)}) collective-permute-start(f32[8,32,256]{2,1,0:T(8,128)S(1)} %get-tuple-element.3), channel_id=1, source_target_pairs={{0,4},{4,0},{8,12},{12,8},{16,20},{20,16},{24,28},{28,24},{32,36},... | collective-permute-start | bytes 786440 | tf_op jit(solution)/shard_map/ppermute | solution.py:301
  33.1 2.0 %collective-permute-done.6 = f32[8,32,256]{2,1,0:T(8,128)S(1)} collective-permute-done((f32[8,32,256]{2,1,0:T(8,128)S(1)}, f32[8,32,256]{2,1,0:T(8,128)S(1)}, u32[]{:S(2)}, u32[]{:S(2)}) %collective-permute-start.6) | collective-permute-done | bytes 262176 | tf_op jit(solution)/shard_map/ppermute | solution.py:301
  35.1 4.1 %collective-permute-done.5 = f32[8,32,256]{2,1,0:T(8,128)S(1)} collective-permute-done((f32[8,32,256]{2,1,0:T(8,128)S(1)}, f32[8,32,256]{2,1,0:T(8,128)S(1)}, u32[]{:S(2)}, u32[]{:S(2)}) %collective-permute-start.5) | collective-permute-done | bytes 262176 | tf_op jit(solution)/shard_map/ppermute | solution.py:301
  39.2 0.0 copy-done
  39.2 0.0 copy-done.1
  39.3 0.0 copy-done.2
  39.3 2.8 %early.1.refs_9_ = f32[3,2,320,256]{3,2,1,0:T(8,128)S(1)} custom-call(f32[8,32,256]{2,1,0:T(8,128)S(1)} %bitcast.7, f32[8,32,256]{2,1,0:T(8,128)S(1)} %get-tuple-element.9.refs_1_, f32[8,32,256]{2,1,0:T(8,128)S(1)} %get-tuple-element.8.refs_2_, f32[8,32,256]{2,1,0:T(8,128)S(1)} %collective-permute-done.2.refs_3_, ...), custom_call_target="tpu_custom_call" | custom-call | flops 4000000000 | bytes 4194304 | tf_op jit(solution)/shard_map/early/pallas_call | solution.py:386
  42.1 0.0 copy-start.5
  42.1 0.0 copy-start.6
  42.2 0.0 collective-permute-done.7.refs_8_
  42.3 1.9 %collective-permute-start.10 = (f32[40,8,256]{2,1,0:T(8,128)S(1)}, f32[40,8,256]{2,1,0:T(8,128)S(1)}, u32[]{:S(2)}, u32[]{:S(2)}) collective-permute-start(f32[40,8,256]{2,1,0:T(8,128)S(1)} %broadcast_select_fusion.1), channel_id=1, source_target_pairs={{1,2},{2,1},{5,6},{6,5},{9,10},{10,9},{13,14},{14,13},{17,18},{18,... | collective-permute-start | bytes 983048 | tf_op jit(solution)/shard_map/ppermute | solution.py:301
  44.3 2.7 %tensor_middle.1.refs_0_ = f32[16,6,8,256]{3,2,1,0:T(8,128)S(1)} custom-call(f32[8,32,256]{2,1,0:T(8,128)S(1)} %bitcast.8, f32[8,32,256]{2,1,0:T(8,128)S(1)} %get-tuple-element.9.refs_1_, f32[8,32,256]{2,1,0:T(8,128)S(1)} %get-tuple-element.8.refs_2_, f32[8,32,256]{2,1,0:T(8,128)S(1)} %collective-permute-done.2.refs_3_, ...), custom_call_target="tpu_custom_call" | custom-call | flops 8000000000 | bytes 4194304 | tf_op jit(solution)/shard_map/tensor_middle/pallas_call | solution.py:359
  47.0 3.6 %collective-permute-start.14 = (f32[16,6,8,256]{3,2,1,0:T(8,128)S(1)}, f32[16,6,8,256]{3,2,1,0:T(8,128)S(1)}, u32[]{:S(2)}, u32[]{:S(2)}) collective-permute-start(f32[16,6,8,256]{3,2,1,0:T(8,128)S(1)} %tensor_middle.1.refs_0_), channel_id=1, source_target_pairs={{1,2},{2,1},{5,6},{6,5},{9,10},{10,9},{13,14},{14,13},{17,18},{18,... | collective-permute-start | bytes 2359304 | tf_op jit(solution)/shard_map/ppermute | solution.py:301
  50.6 0.1 collective-permute-start.12
  50.7 0.1 broadcast_select_fusion
  50.8 0.6 collective-permute-start.8
  51.4 0.0 collective-permute-done.9.refs_9_
  51.4 0.0 collective-permute-done.10.refs_10_
  51.4 3.0 %tensor_away.1.refs_2_ = f32[8,6,8,256]{3,2,1,0:T(8,128)S(1)} custom-call(f32[8,32,256]{2,1,0:T(8,128)S(1)} %bitcast.9, f32[8,32,256]{2,1,0:T(8,128)S(1)} %get-tuple-element.9.refs_1_, f32[8,32,256]{2,1,0:T(8,128)S(1)} %get-tuple-element.8.refs_2_, f32[8,32,256]{2,1,0:T(8,128)S(1)} %collective-permute-done.2.refs_3_, ...), custom_call_target="tpu_custom_call" | custom-call | flops 8000000000 | bytes 4194304 | tf_op jit(solution)/shard_map/tensor_away/pallas_call | solution.py:359
  54.4 1.9 %collective-permute-start.13 = (f32[8,6,8,256]{3,2,1,0:T(8,128)S(1)}, f32[8,6,8,256]{3,2,1,0:T(8,128)S(1)}, u32[]{:S(2)}, u32[]{:S(2)}) collective-permute-start(f32[8,6,8,256]{3,2,1,0:T(8,128)S(1)} %tensor_away.1.refs_2_), channel_id=1, source_target_pairs={{1,2},{2,1},{5,6},{6,5},{9,10},{10,9},{13,14},{14,13},{17,18},{18,... | collective-permute-start | bytes 1179656 | tf_op jit(solution)/shard_map/ppermute | solution.py:301
  56.4 0.0 collective-permute-done.8.refs_9_
  56.4 2.9 %tensor_near.1.refs_1_ = f32[8,6,8,256]{3,2,1,0:T(8,128)S(1)} custom-call(f32[8,32,256]{2,1,0:T(8,128)S(1)} %bitcast.10, f32[8,32,256]{2,1,0:T(8,128)S(1)} %get-tuple-element.9.refs_1_, f32[8,32,256]{2,1,0:T(8,128)S(1)} %get-tuple-element.8.refs_2_, f32[8,32,256]{2,1,0:T(8,128)S(1)} %collective-permute-done.2.refs_3_, ...), custom_call_target="tpu_custom_call" | custom-call | flops 8000000000 | bytes 4194304 | tf_op jit(solution)/shard_map/tensor_near/pallas_call | solution.py:359
  59.3 0.1 collective-permute-start.11
  59.4 5.1 %collective-permute-done.13.refs_5_ = f32[8,6,8,256]{3,2,1,0:T(8,128)S(1)} collective-permute-done((f32[8,6,8,256]{3,2,1,0:T(8,128)S(1)}, f32[8,6,8,256]{3,2,1,0:T(8,128)S(1)}, u32[]{:S(2)}, u32[]{:S(2)}) %collective-permute-start.13) | collective-permute-done | bytes 393248 | tf_op jit(solution)/shard_map/ppermute | solution.py:301
  64.5 0.0 collective-permute-done.14.refs_6_
  64.5 0.0 collective-permute-done.12.refs_4_
  64.5 0.0 collective-permute-done.11.refs_3_
  64.5 1.8 %attributes.1 = (f32[32,8,256]{2,1,0:T(8,128)}, f32[32,8,256]{2,1,0:T(8,128)}, f32[32,8,256]{2,1,0:T(8,128)}) custom-call(f32[16,6,8,256]{3,2,1,0:T(8,128)S(1)} %tensor_middle.1.refs_0_, f32[8,6,8,256]{3,2,1,0:T(8,128)S(1)} %tensor_near.1.refs_1_, f32[8,6,8,256]{3,2,1,0:T(8,128)S(1)} %tensor_away.1.refs_2_, ...), custom_call_target="tpu_custom_call" | custom-call | tf_op jit(solution)/shard_map/attributes/pallas_call | solution.py:409
  (17 shorter events, 0.4 us)
Async XLA Ops:
  1.7 11.3 %collective-permute-start.1 = (f32[8,32,256]{2,1,0:T(8,128)S(1)}, f32[8,32,256]{2,1,0:T(8,128)S(1)}, u32[]{:S(2)}, u32[]{:S(2)}) collective-permute-start(f32[8,32,256]{2,1,0:T(8,128)S(1)} %bitcast.3), channel_id=1, source_target_pairs={{0,8},{4,12},{8,0},{12,4},{16,24},{20,28},{24,16},{28,20},{32,40},... | collective-permute-start | bytes 786440 | tf_op jit(solution)/shard_map/ppermute | solution.py:301
  3.4 12.4 %collective-permute-start = (f32[8,32,256]{2,1,0:T(8,128)S(1)}, f32[8,32,256]{2,1,0:T(8,128)S(1)}, u32[]{:S(2)}, u32[]{:S(2)}) collective-permute-start(f32[8,32,256]{2,1,0:T(8,128)S(1)} %bitcast.4), channel_id=1, source_target_pairs={{8,16},{12,20},{16,8},{20,12},{24,32},{28,36},{32,24},{36,28},{40,... | collective-permute-start | bytes 786440 | tf_op jit(solution)/shard_map/ppermute | solution.py:301
  10.1 11.1 %collective-permute-start.2 = (f32[8,32,256]{2,1,0:T(8,128)S(1)}, f32[8,32,256]{2,1,0:T(8,128)S(1)}, u32[]{:S(2)}, u32[]{:S(2)}) collective-permute-start(f32[8,32,256]{2,1,0:T(8,128)S(1)} %bitcast.5), channel_id=1, source_target_pairs={{0,4},{4,0},{8,12},{12,8},{16,20},{20,16},{24,28},{28,24},{32,36},... | collective-permute-start | bytes 786440 | tf_op jit(solution)/shard_map/ppermute | solution.py:301
  15.9 14.5 %collective-permute-start.3 = (f32[8,32,256]{2,1,0:T(8,128)S(1)}, f32[8,32,256]{2,1,0:T(8,128)S(1)}, u32[]{:S(2)}, u32[]{:S(2)}) collective-permute-start(f32[8,32,256]{2,1,0:T(8,128)S(1)} %collective-permute-done.1), channel_id=1, source_target_pairs={{8,16},{12,20},{16,8},{20,12},{24,32},{28,36},{32,24},{36,28},{40,... | collective-permute-start | bytes 786440 | tf_op jit(solution)/shard_map/ppermute | solution.py:301
  21.1 9.3 %collective-permute-start.4 = (f32[8,32,256]{2,1,0:T(8,128)S(1)}, f32[8,32,256]{2,1,0:T(8,128)S(1)}, u32[]{:S(2)}, u32[]{:S(2)}) collective-permute-start(f32[8,32,256]{2,1,0:T(8,128)S(1)} %collective-permute-done), channel_id=1, source_target_pairs={{0,8},{4,12},{8,0},{12,4},{16,24},{20,28},{24,16},{28,20},{32,40},... | collective-permute-start | bytes 786440 | tf_op jit(solution)/shard_map/ppermute | solution.py:301
  21.2 18.0 %copy-start = (bf16[384,480]{1,0:T(8,128)(2,1)S(1)}, bf16[384,480]{1,0:T(8,128)(2,1)}, u32[]{:S(2)}) copy-start(bf16[384,480]{1,0:T(8,128)(2,1)} %constant.50.clone.refs_8_.refs_10_.refs_11_) | copy-start | bytes 1105924
  21.3 18.0 %copy-start.1 = (bf16[256,256]{1,0:T(8,128)(2,1)S(1)}, bf16[256,256]{1,0:T(8,128)(2,1)}, u32[]{:S(2)}) copy-start(bf16[256,256]{1,0:T(8,128)(2,1)} %constant.47.clone.refs_12_.refs_14_.refs_15_) | copy-start | bytes 393220
  21.3 18.0 %copy-start.2 = (bf16[256,256]{1,0:T(8,128)(2,1)S(1)}, bf16[256,256]{1,0:T(8,128)(2,1)}, u32[]{:S(2)}) copy-start(bf16[256,256]{1,0:T(8,128)(2,1)} %constant.46.clone.refs_11_.refs_13_.refs_14_) | copy-start | bytes 393220
  21.3 18.0 %copy-start.3 = (bf16[256,256]{1,0:T(8,128)(2,1)S(1)}, bf16[256,256]{1,0:T(8,128)(2,1)}, u32[]{:S(2)}) copy-start(bf16[256,256]{1,0:T(8,128)(2,1)} %constant.45.clone.refs_10_.refs_12_.refs_13_) | copy-start | bytes 393220
  21.3 18.0 %copy-start.4 = (bf16[256,256]{1,0:T(8,128)(2,1)S(1)}, bf16[256,256]{1,0:T(8,128)(2,1)}, u32[]{:S(2)}) copy-start(bf16[256,256]{1,0:T(8,128)(2,1)} %constant.44.clone.refs_9_.refs_11_.refs_12_) | copy-start | bytes 393220
  21.4 30.0 %collective-permute-start.9 = (f32[32,8,256]{2,1,0:T(8,128)S(1)}, f32[32,8,256]{2,1,0:T(8,128)S(1)}, u32[]{:S(2)}, u32[]{:S(2)}) collective-permute-start(f32[32,8,256]{2,1,0:T(8,128)S(1)} %maximum_select_fusion), channel_id=1, source_target_pairs={{1,2},{2,1},{5,6},{6,5},{9,10},{10,9},{13,14},{14,13},{17,18},{18,... | collective-permute-start | bytes 786440 | tf_op jit(solution)/shard_map/ppermute | solution.py:301
  26.6 8.5 %collective-permute-start.6 = (f32[8,32,256]{2,1,0:T(8,128)S(1)}, f32[8,32,256]{2,1,0:T(8,128)S(1)}, u32[]{:S(2)}, u32[]{:S(2)}) collective-permute-start(f32[8,32,256]{2,1,0:T(8,128)S(1)} %collective-permute-done.2.refs_3_), channel_id=1, source_target_pairs={{0,8},{4,12},{8,0},{12,4},{16,24},{20,28},{24,16},{28,20},{32,40},... | collective-permute-start | bytes 786440 | tf_op jit(solution)/shard_map/ppermute | solution.py:301
  28.5 10.7 %collective-permute-start.5 = (f32[8,32,256]{2,1,0:T(8,128)S(1)}, f32[8,32,256]{2,1,0:T(8,128)S(1)}, u32[]{:S(2)}, u32[]{:S(2)}) collective-permute-start(f32[8,32,256]{2,1,0:T(8,128)S(1)} %collective-permute-done.2.refs_3_), channel_id=1, source_target_pairs={{8,16},{12,20},{16,8},{20,12},{24,32},{28,36},{32,24},{36,28},{40,... | collective-permute-start | bytes 786440 | tf_op jit(solution)/shard_map/ppermute | solution.py:301
  30.5 11.7 %collective-permute-start.7 = (f32[8,32,256]{2,1,0:T(8,128)S(1)}, f32[8,32,256]{2,1,0:T(8,128)S(1)}, u32[]{:S(2)}, u32[]{:S(2)}) collective-permute-start(f32[8,32,256]{2,1,0:T(8,128)S(1)} %get-tuple-element.3), channel_id=1, source_target_pairs={{0,4},{4,0},{8,12},{12,8},{16,20},{20,16},{24,28},{28,24},{32,36},... | collective-permute-start | bytes 786440 | tf_op jit(solution)/shard_map/ppermute | solution.py:301
  42.1 2.1 %copy-start.5 = (bf16[256,256]{1,0:T(8,128)(2,1)S(1)}, bf16[256,256]{1,0:T(8,128)(2,1)}, u32[]{:S(2)}) copy-start(bf16[256,256]{1,0:T(8,128)(2,1)} %constant.49.clone.refs_16_.refs_17_) | copy-start | bytes 393220
  42.1 2.1 %copy-start.6 = (bf16[256,256]{1,0:T(8,128)(2,1)S(1)}, bf16[256,256]{1,0:T(8,128)(2,1)}, u32[]{:S(2)}) copy-start(bf16[256,256]{1,0:T(8,128)(2,1)} %constant.48.clone.refs_15_.refs_16_) | copy-start | bytes 393220
  42.3 9.1 %collective-permute-start.10 = (f32[40,8,256]{2,1,0:T(8,128)S(1)}, f32[40,8,256]{2,1,0:T(8,128)S(1)}, u32[]{:S(2)}, u32[]{:S(2)}) collective-permute-start(f32[40,8,256]{2,1,0:T(8,128)S(1)} %broadcast_select_fusion.1), channel_id=1, source_target_pairs={{1,2},{2,1},{5,6},{6,5},{9,10},{10,9},{13,14},{14,13},{17,18},{18,... | collective-permute-start | bytes 983048 | tf_op jit(solution)/shard_map/ppermute | solution.py:301
  47.0 17.5 %collective-permute-start.14 = (f32[16,6,8,256]{3,2,1,0:T(8,128)S(1)}, f32[16,6,8,256]{3,2,1,0:T(8,128)S(1)}, u32[]{:S(2)}, u32[]{:S(2)}) collective-permute-start(f32[16,6,8,256]{3,2,1,0:T(8,128)S(1)} %tensor_middle.1.refs_0_), channel_id=1, source_target_pairs={{1,2},{2,1},{5,6},{6,5},{9,10},{10,9},{13,14},{14,13},{17,18},{18,... | collective-permute-start | bytes 2359304 | tf_op jit(solution)/shard_map/ppermute | solution.py:301
  50.6 13.9 %collective-permute-start.12 = (f32[16,6,8,256]{3,2,1,0:T(8,128)S(1)}, f32[16,6,8,256]{3,2,1,0:T(8,128)S(1)}, u32[]{:S(2)}, u32[]{:S(2)}) collective-permute-start(f32[16,6,8,256]{3,2,1,0:T(8,128)S(1)} %tensor_middle.1.refs_0_), channel_id=1, source_target_pairs={{0,1},{1,0},{2,3},{3,2},{4,5},{5,4},{6,7},{7,6},{8,9},{9,8},{10,11... | collective-permute-start | bytes 2359304 | tf_op jit(solution)/shard_map/ppermute | solution.py:301
  50.8 5.6 %collective-permute-start.8 = (f32[72,8,256]{2,1,0:T(8,128)S(1)}, f32[72,8,256]{2,1,0:T(8,128)S(1)}, u32[]{:S(2)}, u32[]{:S(2)}) collective-permute-start(f32[72,8,256]{2,1,0:T(8,128)S(1)} %broadcast_select_fusion), channel_id=1, source_target_pairs={{0,1},{1,0},{2,3},{3,2},{4,5},{5,4},{6,7},{7,6},{8,9},{9,8},{10,11... | collective-permute-start | bytes 1769480 | tf_op jit(solution)/shard_map/ppermute | solution.py:301
  54.4 10.1 %collective-permute-start.13 = (f32[8,6,8,256]{3,2,1,0:T(8,128)S(1)}, f32[8,6,8,256]{3,2,1,0:T(8,128)S(1)}, u32[]{:S(2)}, u32[]{:S(2)}) collective-permute-start(f32[8,6,8,256]{3,2,1,0:T(8,128)S(1)} %tensor_away.1.refs_2_), channel_id=1, source_target_pairs={{1,2},{2,1},{5,6},{6,5},{9,10},{10,9},{13,14},{14,13},{17,18},{18,... | collective-permute-start | bytes 1179656 | tf_op jit(solution)/shard_map/ppermute | solution.py:301
  59.3 5.3 %collective-permute-start.11 = (f32[8,6,8,256]{3,2,1,0:T(8,128)S(1)}, f32[8,6,8,256]{3,2,1,0:T(8,128)S(1)}, u32[]{:S(2)}, u32[]{:S(2)}) collective-permute-start(f32[8,6,8,256]{3,2,1,0:T(8,128)S(1)} %tensor_near.1.refs_1_), channel_id=1, source_target_pairs={{0,1},{1,0},{2,3},{3,2},{4,5},{5,4},{6,7},{7,6},{8,9},{9,8},{10,11... | collective-permute-start | bytes 1179656 | tf_op jit(solution)/shard_map/ppermute | solution.py:301
